TPU v7x, 256 devices: a whole 4x4x8 slice. The times are simulated.
256 devices in a mesh: box: 64 (over z, x, y_hi), grp: 4 (over y_lo, core).
Axes of the slice: x: 4, y: 4 (y_hi: 2, y_lo: 2; y = y_hi * 2 + y_lo), z: 8, core: 2. Of those that a mesh axis runs over, the one named last changes fastest.
Arguments:
- old_fields: float32 [3, 4, 256, 32, 1024], P(None, 'grp', 'box'), may hold values from -6 to 6, as said below
- old_count: int32 [4, 64], P('grp'), may hold values from 0 to 4, as said below
- neighbours: int32 [4, 128, 6], P('grp', 'box'), may hold values from -1 to 127, as said below
- parents: int32 [4, 128, 3], P('grp', 'box'), may hold values from 0 to 7, as said below
- coarse_source: float32 [4, 128, 8, 16, 256], P('grp', 'box'), may hold values from -6 to 6
Outputs:
- smoothed: float32 [4, 128, 32, 1024], P('grp', 'box')
- residual: float32 [4, 128, 32, 1024], P('grp', 'box')
- coarse_rhs: float32 [4, 128, 8, 16, 256], P('grp', 'box')
Inputs may be any that keep to these rules, and one draw needn't show every extreme that they name: `old_fields`: components 0, 1, 2 are the solution, the right side and the cell coefficient; the coefficient lies in [0.25, 4]. `old_count`: in each owner group the counts sum to 128, and the sum of the first j counts differs from j * 2 by at most 1 for every j; some device holds 4 boxes and some none. Neighbourhood is symmetric; the x- neighbour of a box lies in the previous run of 2 boxes along the curve, the x+ neighbour in the next run, the y and z neighbours in the box's own run. `parents`: the named coarse box belongs to the owner on the same curve position as the fine box; no two fine boxes name the same octant of the same coarse box.
All inputs are finite; a program needn't handle non-finite values.
Results may differ from a plain program's by a relative error of at most 0.0001.
Values sent between devices are 32-bit elements; how exact they have to be, the bound alone decides.
No kernel may reach another device: no remote copies, remote signals or barrier semaphores. Data moves between devices by JAX's collectives and lax.ppermute only.
A program may use at most 64 MiB of HBM per device.

v0:
```python
import jax
import jax.numpy as jnp
from jax import lax
from jax.sharding import PartitionSpec as P

MASS_TERM = 0.25


def with_halo(cells, sides, width):
    for axis, dim in sides:
        count = lax.axis_size(axis)
        ends = count - 1
        head = lax.slice_in_dim(cells, 0, width, axis=dim)
        tail = lax.slice_in_dim(cells, cells.shape[dim] - width, cells.shape[dim], axis=dim)
        cells = jnp.concatenate(
            [
                lax.ppermute(tail, axis, [(i, (i + 1) % count) for i in range(ends)]),
                cells,
                lax.ppermute(head, axis, [((i + 1) % count, i) for i in range(ends)]),
            ],
            axis=dim,
        )
    return cells


def box_planes(box_field, box_edge):
    plane_cells = box_edge * box_edge
    return (
        box_field[:, 0, :],
        box_field[:, -1, :],
        box_field[:, :, :box_edge],
        box_field[:, :, plane_cells - box_edge :],
        box_field[:, :, 0::box_edge],
        box_field[:, :, box_edge - 1 :: box_edge],
    )


def ghost_planes(
    box_field,
    lower_table,
    upper_table,
    lower_offset,
    upper_offset,
    link_rows,
    first_box,
    keep_own,
    box_edge,
):
    planes = box_planes(box_field, box_edge)
    tables = (lower_table, upper_table, planes[3], planes[2], planes[5], planes[4])
    offsets = (lower_offset, upper_offset, first_box, first_box, first_box, first_box)
    results = []
    for face_id in range(6):
        fallback = planes[face_id] if keep_own else jnp.zeros_like(planes[face_id])
        target = link_rows[:, face_id]
        local_row = jnp.clip(target - offsets[face_id], 0, tables[face_id].shape[0] - 1)
        chosen = jnp.take(tables[face_id], local_row, axis=0)
        is_valid = (target >= 0).reshape((-1,) + (1,) * (chosen.ndim - 1))
        results.append(jnp.where(is_valid, chosen, fallback))
    return results


def beside_cells(box_field, planes, box_edge, low_mask, high_mask):
    plane_cells = box_field.shape[2]
    zero_column = jnp.zeros(box_field.shape[:2] + (1,), box_field.dtype)
    low_shift = jnp.concatenate([zero_column, box_field[:, :, :-1]], axis=2)
    high_shift = jnp.concatenate([box_field[:, :, 1:], zero_column], axis=2)
    return (
        jnp.concatenate([planes[0][:, None, :], box_field[:, :-1, :]], axis=1),
        jnp.concatenate([box_field[:, 1:, :], planes[1][:, None, :]], axis=1),
        jnp.concatenate([planes[2], box_field[:, :, : plane_cells - box_edge]], axis=2),
        jnp.concatenate([box_field[:, :, box_edge:], planes[3]], axis=2),
        jnp.where(low_mask, jnp.repeat(planes[4], box_edge, axis=2), low_shift),
        jnp.where(high_mask, jnp.repeat(planes[5], box_edge, axis=2), high_shift),
    )


def weighted_sum(weights, nearby):
    running = weights[0] * nearby[0]
    for face_id in range(1, 6):
        running = running + weights[face_id] * nearby[face_id]
    return running


def make_weights(coefficient, coef_ghosts, box_edge, low_mask, high_mask):
    weights = [
        0.5 * (coefficient + nearby_coef)
        for nearby_coef in beside_cells(coefficient, coef_ghosts, box_edge, low_mask, high_mask)
    ]
    diagonal = MASS_TERM + weights[0]
    for face_id in range(1, 6):
        diagonal = diagonal + weights[face_id]
    return (weights, diagonal)


def half_sweep(
    field, ghosts, right_side, weights, diagonal, parity_rows, colour, box_edge, low_mask, high_mask
):
    nearby = beside_cells(field, ghosts, box_edge, low_mask, high_mask)
    updated = (right_side + weighted_sum(weights, nearby)) / diagonal
    return jnp.where(parity_rows == colour, updated, field)


def fresh_faces(solution, box_count, box_edge):
    outgoing = jnp.concatenate([solution[:, 0], solution[:, box_edge - 1]], axis=0)
    arrived = with_halo(outgoing, (("box", 0),), box_count)
    return (arrived[:box_count], arrived[3 * box_count :])


def per_device(old_fields, old_count, neighbours, parents, coarse_source):
    box_edge = old_fields.shape[3]
    plane_cells = box_edge * box_edge
    slot_count = old_fields.shape[2]
    box_count = neighbours.shape[1]
    position = lax.axis_index("box")
    counts = old_count[0]
    run_ends = jnp.cumsum(counts)
    run_starts = run_ends - counts
    wanted = position * box_count + jnp.arange(box_count, dtype=jnp.int32)
    source = jnp.sum((run_ends[None, :] <= wanted[:, None]).astype(jnp.int32), axis=1)
    old_slot = wanted - jnp.take(run_starts, source)
    holdings = old_fields[:, 0]
    gathered = with_halo(holdings, (("box", 1),), slot_count)
    moved_fields = jnp.take(gathered, (source - position + 1) * slot_count + old_slot, axis=1)
    solution = moved_fields[0]
    right_side = moved_fields[1]
    coefficient = moved_fields[2]
    link_rows = neighbours[0]
    first_box = position * box_count
    lower_offset = first_box - box_count
    upper_offset = first_box + box_count
    columns = jnp.arange(plane_cells, dtype=jnp.int32)
    depth_ids = columns % box_edge
    low_mask = (depth_ids == 0)[None, None, :]
    high_mask = (depth_ids == box_edge - 1)[None, None, :]
    layer_ids = jnp.arange(box_edge, dtype=jnp.int32)
    parity = (layer_ids[:, None] + columns[None, :] // box_edge + depth_ids[None, :]) % 2
    edge_pair = jnp.stack(
        [
            jnp.concatenate([solution[:, 0], solution[:, box_edge - 1]], axis=0),
            jnp.concatenate([coefficient[:, 0], coefficient[:, box_edge - 1]], axis=0),
        ]
    )
    beside_all = with_halo(edge_pair, (("box", 1),), box_count)
    coef_ghosts = ghost_planes(
        coefficient,
        beside_all[1, :box_count],
        beside_all[1, 3 * box_count :],
        lower_offset,
        upper_offset,
        link_rows,
        first_box,
        True,
        box_edge,
    )
    weights, diagonal = make_weights(coefficient, coef_ghosts, box_edge, low_mask, high_mask)
    lower_faces = beside_all[0, :box_count]
    upper_faces = beside_all[0, 3 * box_count :]
    for sweep_step in range(4):
        if sweep_step > 0:
            lower_faces, upper_faces = fresh_faces(solution, box_count, box_edge)
        ghosts = ghost_planes(
            solution,
            lower_faces,
            upper_faces,
            lower_offset,
            upper_offset,
            link_rows,
            first_box,
            False,
            box_edge,
        )
        solution = half_sweep(
            solution,
            ghosts,
            right_side,
            weights,
            diagonal,
            parity,
            sweep_step % 2,
            box_edge,
            low_mask,
            high_mask,
        )
    lower_faces, upper_faces = fresh_faces(solution, box_count, box_edge)
    final_ghosts = ghost_planes(
        solution,
        lower_faces,
        upper_faces,
        lower_offset,
        upper_offset,
        link_rows,
        first_box,
        False,
        box_edge,
    )
    nearby = beside_cells(solution, final_ghosts, box_edge, low_mask, high_mask)
    residual = right_side - (diagonal * solution - weighted_sum(weights, nearby))
    half_edge = box_edge // 2
    octant_cells = half_edge * half_edge
    paired = residual.reshape(box_count, half_edge, 2, plane_cells).sum(axis=2)
    merge_target = columns // box_edge // 2 * half_edge + depth_ids // 2
    merge_map = (
        merge_target[:, None] == jnp.arange(octant_cells, dtype=jnp.int32)[None, :]
    ).astype(jnp.float32)
    restricted = (
        jnp.einsum("bxm,mq->bxq", paired, merge_map, precision=lax.Precision.HIGHEST) * 0.125
    )
    groups = lax.axis_size("grp")
    owner_group = parents[0, :, 0]
    target_cell = parents[0, :, 1] * 8 + parents[0, :, 2]
    box_ids = jnp.arange(box_count, dtype=jnp.int32)
    earlier = (owner_group[:, None] == owner_group[None, :]) & (box_ids[None, :] < box_ids[:, None])
    send_slot = owner_group * box_count + jnp.sum(earlier.astype(jnp.int32), axis=1)
    placing = (
        send_slot[None, :] == jnp.arange(groups * box_count, dtype=jnp.int32)[:, None]
    ).astype(jnp.float32)
    packed = jnp.dot(placing, restricted.reshape(box_count, -1), precision=lax.Precision.HIGHEST)
    labels = (
        jnp.dot(placing, (target_cell + 1).astype(jnp.float32), precision=lax.Precision.HIGHEST)
        - 1.0
    )
    got_cells, got_labels = (
        lax.all_to_all(
            packed.reshape(groups, box_count, -1), "grp", split_axis=0, concat_axis=0, tiled=True
        ),
        lax.all_to_all(
            labels.reshape(groups, box_count), "grp", split_axis=0, concat_axis=0, tiled=True
        ),
    )
    coarse_slots = coarse_source.shape[1] * 8
    picking = (
        got_labels.reshape(1, -1) == jnp.arange(coarse_slots, dtype=jnp.float32)[:, None]
    ).astype(jnp.float32)
    filled = jnp.dot(
        picking, got_cells.reshape(groups * box_count, -1), precision=lax.Precision.HIGHEST
    )
    covered = jnp.sum(picking, axis=1) > 0.5
    coarse_rhs = jnp.where(
        covered[:, None], filled, coarse_source[0].reshape(coarse_slots, -1)
    ).reshape(coarse_source.shape)
    return (solution[None], residual[None], coarse_rhs)


def solution(mesh):
    in_specs = (
        P(None, "grp", "box", None, None),
        P("grp", None),
        P("grp", "box", None),
        P("grp", "box", None),
        P("grp", "box", None, None, None),
    )
    out_specs = (
        P("grp", "box", None, None),
        P("grp", "box", None, None),
        P("grp", "box", None, None, None),
    )
    return jax.shard_map(
        per_device, mesh=mesh, in_specs=in_specs, out_specs=out_specs, check_vma=False
    )
```

profile of v0, /device:TPU:128, one launch (start us, length us, event | category | flops | bytes accessed | tf_op | source)
XLA Modules:
  0.0 250.1 jit_solution(16667523893371066858)
XLA Ops:
  0.6 6.8 %collective-permute-start.1 = (f32[3,4,32,1024]{3,2,1,0:T(8,128)}, f32[3,4,32,1024]{3,2,1,0:T(8,128)S(1)}, u32[]{:S(2)}, u32[]{:S(2)}) collective-permute-start(f32[3,4,32,1024]{3,2,1,0:T(8,128)} %bitcast.222), channel_id=1, source_target_pairs={{4,0},{8,4},{12,8},{16,12},{20,16},{24,20},{28,24},{32,28},{36,32}... | collective-permute-start | bytes 4718600 | tf_op jit(solution)/shard_map/ppermute | solution.py:19
  7.5 1.9 collective-permute-start
  10.2 0.9 convert_reduce_fusion.1
  12.1 3.2 %all-to-all-start = ((f32[4,1,2]{2,1,0:T(1,128)}), f32[4,1,2]{2,1,0:T(1,128)S(1)}, u32[]{:S(2)}, u32[]{:S(2)}) async-start(f32[4,1,2]{2,1,0:T(1,128)} %bitcast.48), calls=%async_computation | async-start | bytes 4096 | tf_op jit(solution)/shard_map/all_to_all | solution.py:227
  18.5 1.0 fusion.120
  23.2 1.8 copy.120
  26.4 48.9 %all-to-all-done = f32[4,1,2]{2,1,0:T(1,128)S(1)} async-done(((f32[4,1,2]{2,1,0:T(1,128)}), f32[4,1,2]{2,1,0:T(1,128)S(1)}, u32[]{:S(2)}, u32[]{:S(2)}) %all-to-all-start) | async-done | bytes 64 | tf_op jit(solution)/shard_map/all_to_all | solution.py:227
  77.2 4.1 %pad_maximum_fusion = f32[3,12,32,1024]{3,2,1,0:T(8,128)} fusion(f32[3,4,32,1024]{3,2,1,0:T(8,128)S(1)} %collective-permute-done.1, f32[3,4,32,1024]{3,2,1,0:T(8,128)} %bitcast.224, f32[3,4,32,1024]{3,2,1,0:T(8,128)S(1)} %collective-permute-done), kind=kLoop, calls=%fused_computation.38 | loop fusion | flops 2359296 | bytes 9437184 | tf_op jit(solution)/shard_map/concatenate | solution.py:15
  81.3 2.9 %gather_fusion.1 = f32[2,3,32,1024]{3,2,1,0:T(8,128)S(1)} fusion(f32[3,12,32,1024]{3,2,1,0:T(8,128)} %pad_maximum_fusion, s32[1024]{0:T(1024)S(1)} %pad_clamp_fusion.6), kind=kCustom, calls=%fused_computation.37 | custom fusion | bytes 1572872 | tf_op jit(solution)/shard_map/jit(_take)/gather | solution.py:124
  84.5 1.0 fusion.111
  85.5 1.1 fusion.112
  87.8 1.1 fusion.113
  89.4 2.9 %collective-permute-start.2 = (f32[2,2,1024]{2,1,0:T(2,128)S(1)}, f32[2,2,1024]{2,1,0:T(2,128)S(1)}, u32[]{:S(2)}, u32[]{:S(2)}) collective-permute-start(f32[2,2,1024]{2,1,0:T(2,128)S(1)} %get-tuple-element.99), channel_id=1, source_target_pairs={{0,4},{4,8},{8,12},{12,16},{16,20},{20,24},{24,28},{28,32},{32,36}... | collective-permute-start | bytes 49160 | tf_op jit(solution)/shard_map/ppermute | solution.py:17
  92.3 8.7 %collective-permute-start.3 = (f32[2,2,1024]{2,1,0:T(2,128)S(1)}, f32[2,2,1024]{2,1,0:T(2,128)S(1)}, u32[]{:S(2)}, u32[]{:S(2)}) collective-permute-start(f32[2,2,1024]{2,1,0:T(2,128)S(1)} %get-tuple-element.98), channel_id=1, source_target_pairs={{4,0},{8,4},{12,8},{16,12},{20,16},{24,20},{28,24},{32,28},{36,32}... | collective-permute-start | bytes 49160 | tf_op jit(solution)/shard_map/ppermute | solution.py:19
  109.3 1.2 reshape.420
  113.6 2.6 %fusion.12 = (f32[2,32,1024]{2,1,0:T(8,128)S(1)}, f32[2,32,1024]{2,1,0:T(8,128)S(1)}, f32[2,32,1024]{2,1,0:T(8,128)S(1)}, f32[2,32,1024]{2,1,0:T(8,128)S(1)}, f3...) fusion(f32[2,31,1024]{2,1,0:T(8,128)} %get-tuple-element.127, ...), kind=kLoop, calls=%fused_computation.60 | loop fusion | flops 2883584 | bytes 6849536 | tf_op jit(solution)/shard_map/jit(_where)/select_n | solution.py:101
  119.6 1.9 collective-permute-start.4
  121.5 9.8 %collective-permute-start.5 = (f32[2,1024]{1,0:T(2,128)S(1)}, f32[2,1024]{1,0:T(2,128)S(1)}, u32[]{:S(2)}, u32[]{:S(2)}) collective-permute-start(f32[2,1024]{1,0:T(2,128)S(1)} %bitcast.236), channel_id=1, source_target_pairs={{4,0},{8,4},{12,8},{16,12},{20,16},{24,20},{28,24},{32,28},{36,32}... | collective-permute-start | bytes 24584 | tf_op jit(solution)/shard_map/ppermute | solution.py:19
  137.0 1.3 broadcast_in_dim.362
  138.3 1.7 reshape.423
  140.0 1.3 broadcast_in_dim.361
  141.4 1.7 reshape.422
  144.7 1.8 fusion.23
  149.9 1.9 collective-permute-start.6
  151.9 9.6 %collective-permute-start.7 = (f32[2,1024]{1,0:T(2,128)S(1)}, f32[2,1024]{1,0:T(2,128)S(1)}, u32[]{:S(2)}, u32[]{:S(2)}) collective-permute-start(f32[2,1024]{1,0:T(2,128)S(1)} %bitcast.237), channel_id=1, source_target_pairs={{4,0},{8,4},{12,8},{16,12},{20,16},{24,20},{28,24},{32,28},{36,32}... | collective-permute-start | bytes 24584 | tf_op jit(solution)/shard_map/ppermute | solution.py:19
  167.2 1.3 broadcast_in_dim.366
  168.5 1.7 reshape.425
  170.2 1.3 broadcast_in_dim.365
  171.6 1.7 reshape.424
  174.9 1.8 fusion.31
  180.1 1.9 collective-permute-start.8
  182.0 9.6 %collective-permute-start.9 = (f32[2,1024]{1,0:T(2,128)S(1)}, f32[2,1024]{1,0:T(2,128)S(1)}, u32[]{:S(2)}, u32[]{:S(2)}) collective-permute-start(f32[2,1024]{1,0:T(2,128)S(1)} %bitcast.238), channel_id=1, source_target_pairs={{4,0},{8,4},{12,8},{16,12},{20,16},{24,20},{28,24},{32,28},{36,32}... | collective-permute-start | bytes 24584 | tf_op jit(solution)/shard_map/ppermute | solution.py:19
  197.4 1.3 broadcast_in_dim.370
  198.7 1.7 reshape.427
  200.4 1.3 broadcast_in_dim.369
  201.8 1.7 reshape.426
  205.1 1.8 fusion.39
  210.3 1.9 collective-permute-start.10
  212.3 9.9 %collective-permute-start.11 = (f32[2,1024]{1,0:T(2,128)S(1)}, f32[2,1024]{1,0:T(2,128)S(1)}, u32[]{:S(2)}, u32[]{:S(2)}) collective-permute-start(f32[2,1024]{1,0:T(2,128)S(1)} %bitcast.234), channel_id=1, source_target_pairs={{4,0},{8,4},{12,8},{16,12},{20,16},{24,20},{28,24},{32,28},{36,32}... | collective-permute-start | bytes 24584 | tf_op jit(solution)/shard_map/ppermute | solution.py:19
  227.7 1.3 broadcast_in_dim.375
  229.0 1.7 reshape.429
  230.8 1.3 broadcast_in_dim.374
  232.1 1.7 reshape.428
  235.4 2.5 %fusion.46 = f32[2,32,1024]{2,1,0:T(8,128)} fusion(f32[2,32,1024]{2,1,0:T(8,128)S(1)} %get-tuple-element.23, f32[2,31,1024]{2,1,0:T(8,128)} %get-tuple-element.45, f32[2,1,1024]{2,1,0:T(1,128)S(1)} %copy.94, f32[2,32,1024]{2,1,0:T(8,128)S(1)} %get-tuple-element.22, f32[2,1,1024]{2,1,0:T(1,128)S(1)} %broadcast_in_dim.373, ...), kind=kLoop, calls=%fused_computation.113 | loop fusion | flops 1703936 | bytes 4457984 | tf_op jit(solution)/shard_map/sub | solution.py:198
  238.0 1.1 reshape.430
  239.9 0.9 fusion.121
  240.9 3.3 %all-to-all-start.1 = ((f32[4,2,4096]{2,1,0:T(2,128)}), f32[4,2,4096]{2,1,0:T(2,128)S(1)}, u32[]{:S(2)}, u32[]{:S(2)}) async-start(f32[4,2,4096]{2,1,0:T(2,128)} %fusion.121), calls=%async_computation.1 | async-start | bytes 262144 | tf_op jit(solution)/shard_map/all_to_all | solution.py:224
  244.2 4.6 %all-to-all-done.1 = f32[4,2,4096]{2,1,0:T(2,128)S(1)} async-done(((f32[4,2,4096]{2,1,0:T(2,128)}), f32[4,2,4096]{2,1,0:T(2,128)S(1)}, u32[]{:S(2)}, u32[]{:S(2)}) %all-to-all-start.1) | async-done | bytes 131104 | tf_op jit(solution)/shard_map/all_to_all | solution.py:224
  (294 shorter events, 68.8 us)
Async XLA Ops:
  0.6 76.6 %collective-permute-start.1 = (f32[3,4,32,1024]{3,2,1,0:T(8,128)}, f32[3,4,32,1024]{3,2,1,0:T(8,128)S(1)}, u32[]{:S(2)}, u32[]{:S(2)}) collective-permute-start(f32[3,4,32,1024]{3,2,1,0:T(8,128)} %bitcast.222), channel_id=1, source_target_pairs={{4,0},{8,4},{12,8},{16,12},{20,16},{24,20},{28,24},{32,28},{36,32}... | collective-permute-start | bytes 4718600 | tf_op jit(solution)/shard_map/ppermute | solution.py:19
  7.5 69.7 %collective-permute-start = (f32[3,4,32,1024]{3,2,1,0:T(8,128)}, f32[3,4,32,1024]{3,2,1,0:T(8,128)S(1)}, u32[]{:S(2)}, u32[]{:S(2)}) collective-permute-start(f32[3,4,32,1024]{3,2,1,0:T(8,128)} %bitcast.223), channel_id=1, source_target_pairs={{0,4},{4,8},{8,12},{12,16},{16,20},{20,24},{24,28},{28,32},{32,36}... | collective-permute-start | bytes 4718600 | tf_op jit(solution)/shard_map/ppermute | solution.py:17
  12.1 63.2 %all-to-all-start = ((f32[4,1,2]{2,1,0:T(1,128)}), f32[4,1,2]{2,1,0:T(1,128)S(1)}, u32[]{:S(2)}, u32[]{:S(2)}) async-start(f32[4,1,2]{2,1,0:T(1,128)} %bitcast.48), calls=%async_computation | async-start | bytes 4096 | tf_op jit(solution)/shard_map/all_to_all | solution.py:227
  20.2 91.8 %copy-start.15 = (pred[2]{0:T(512)(128)(4,1)}, pred[2]{0:T(512)(128)(4,1)S(1)}, u32[]{:S(2)}) copy-start(pred[2]{0:T(512)(128)(4,1)S(1)} %get-tuple-element.34) | copy-start | bytes 10
  22.8 79.3 %copy-start.8 = (pred[2]{0:T(512)(128)(4,1)}, pred[2]{0:T(512)(128)(4,1)S(1)}, u32[]{:S(2)}) copy-start(pred[2]{0:T(512)(128)(4,1)S(1)} %get-tuple-element.125) | copy-start | bytes 10
  22.8 83.4 %copy-start.2 = (pred[2]{0:T(512)(128)(4,1)}, pred[2]{0:T(512)(128)(4,1)S(1)}, u32[]{:S(2)}) copy-start(pred[2]{0:T(512)(128)(4,1)S(1)} %get-tuple-element.28) | copy-start | bytes 10
  22.8 78.7 %copy-start.37 = (s32[1024]{0:T(1024)}, s32[1024]{0:T(1024)S(1)}, u32[]{:S(2)}) copy-start(s32[1024]{0:T(1024)S(1)} %pad_clamp_fusion.3) | copy-start | bytes 12292
  22.8 80.6 %copy-start.34 = (s32[1024]{0:T(1024)}, s32[1024]{0:T(1024)S(1)}, u32[]{:S(2)}) copy-start(s32[1024]{0:T(1024)S(1)} %pad_clamp_fusion.2) | copy-start | bytes 12292
  23.0 83.3 %copy-start.6 = (pred[2]{0:T(512)(128)(4,1)}, pred[2]{0:T(512)(128)(4,1)S(1)}, u32[]{:S(2)}) copy-start(pred[2]{0:T(512)(128)(4,1)S(1)} %get-tuple-element.26) | copy-start | bytes 10
  23.1 83.4 %copy-start.4 = (pred[2]{0:T(512)(128)(4,1)}, pred[2]{0:T(512)(128)(4,1)S(1)}, u32[]{:S(2)}) copy-start(pred[2]{0:T(512)(128)(4,1)S(1)} %get-tuple-element.123) | copy-start | bytes 10
  23.1 81.4 %copy-start.36 = (s32[1024]{0:T(1024)}, s32[1024]{0:T(1024)S(1)}, u32[]{:S(2)}) copy-start(s32[1024]{0:T(1024)S(1)} %pad_clamp_fusion) | copy-start | bytes 12292
  23.1 82.5 %copy-start.35 = (s32[1024]{0:T(1024)}, s32[1024]{0:T(1024)S(1)}, u32[]{:S(2)}) copy-start(s32[1024]{0:T(1024)S(1)} %pad_clamp_fusion.1) | copy-start | bytes 12292
  25.7 76.4 %copy-start.23 = (pred[2]{0:T(512)(128)(4,1)}, pred[2]{0:T(512)(128)(4,1)S(1)}, u32[]{:S(2)}) copy-start(pred[2]{0:T(512)(128)(4,1)S(1)} %compare_bitcast_fusion.3) | copy-start | bytes 10
  25.7 80.5 %copy-start.22 = (pred[2]{0:T(512)(128)(4,1)}, pred[2]{0:T(512)(128)(4,1)S(1)}, u32[]{:S(2)}) copy-start(pred[2]{0:T(512)(128)(4,1)S(1)} %compare_bitcast_fusion.2) | copy-start | bytes 10
  25.8 80.6 %copy-start.21 = (pred[2]{0:T(512)(128)(4,1)}, pred[2]{0:T(512)(128)(4,1)S(1)}, u32[]{:S(2)}) copy-start(pred[2]{0:T(512)(128)(4,1)S(1)} %compare_bitcast_fusion) | copy-start | bytes 10
  84.4 22.0 %copy-start.20 = (pred[2]{0:T(512)(128)(4,1)S(1)}, pred[2]{0:T(512)(128)(4,1)}, u32[]{:S(2)}) copy-start(pred[2]{0:T(512)(128)(4,1)} %compare_bitcast_fusion.1) | copy-start | bytes 10
  89.4 21.1 %collective-permute-start.2 = (f32[2,2,1024]{2,1,0:T(2,128)S(1)}, f32[2,2,1024]{2,1,0:T(2,128)S(1)}, u32[]{:S(2)}, u32[]{:S(2)}) collective-permute-start(f32[2,2,1024]{2,1,0:T(2,128)S(1)} %get-tuple-element.99), channel_id=1, source_target_pairs={{0,4},{4,8},{8,12},{12,16},{16,20},{20,24},{24,28},{28,32},{32,36}... | collective-permute-start | bytes 49160 | tf_op jit(solution)/shard_map/ppermute | solution.py:17
  92.3 19.7 %collective-permute-start.3 = (f32[2,2,1024]{2,1,0:T(2,128)S(1)}, f32[2,2,1024]{2,1,0:T(2,128)S(1)}, u32[]{:S(2)}, u32[]{:S(2)}) collective-permute-start(f32[2,2,1024]{2,1,0:T(2,128)S(1)} %get-tuple-element.98), channel_id=1, source_target_pairs={{4,0},{8,4},{12,8},{16,12},{20,16},{24,20},{28,24},{32,28},{36,32}... | collective-permute-start | bytes 49160 | tf_op jit(solution)/shard_map/ppermute | solution.py:19
  116.2 27.6 %copy-start.16 = (pred[2]{0:T(512)(128)(4,1)S(1)}, pred[2]{0:T(512)(128)(4,1)}, u32[]{:S(2)}) copy-start(pred[2]{0:T(512)(128)(4,1)} %copy-done.15) | copy-start | bytes 10
  116.2 27.6 %copy-start.30 = (pred[2]{0:T(512)(128)(4,1)S(1)}, pred[2]{0:T(512)(128)(4,1)}, u32[]{:S(2)}) copy-start(pred[2]{0:T(512)(128)(4,1)} %compare_bitcast_fusion.5) | copy-start | bytes 10
  116.2 28.4 %copy-start.11 = (pred[2]{0:T(512)(128)(4,1)S(1)}, pred[2]{0:T(512)(128)(4,1)}, u32[]{:S(2)}) copy-start(pred[2]{0:T(512)(128)(4,1)} %get-tuple-element.32) | copy-start | bytes 10
  116.2 28.4 %copy-start.25 = (pred[2]{0:T(512)(128)(4,1)S(1)}, pred[2]{0:T(512)(128)(4,1)}, u32[]{:S(2)}) copy-start(pred[2]{0:T(512)(128)(4,1)} %compare_bitcast_fusion.4) | copy-start | bytes 10
  119.6 23.5 %collective-permute-start.4 = (f32[2,1024]{1,0:T(2,128)S(1)}, f32[2,1024]{1,0:T(2,128)S(1)}, u32[]{:S(2)}, u32[]{:S(2)}) collective-permute-start(f32[2,1024]{1,0:T(2,128)S(1)} %bitcast.239), channel_id=1, source_target_pairs={{0,4},{4,8},{8,12},{12,16},{16,20},{20,24},{24,28},{28,32},{32,36}... | collective-permute-start | bytes 24584 | tf_op jit(solution)/shard_map/ppermute | solution.py:17
  121.5 22.4 %collective-permute-start.5 = (f32[2,1024]{1,0:T(2,128)S(1)}, f32[2,1024]{1,0:T(2,128)S(1)}, u32[]{:S(2)}, u32[]{:S(2)}) collective-permute-start(f32[2,1024]{1,0:T(2,128)S(1)} %bitcast.236), channel_id=1, source_target_pairs={{4,0},{8,4},{12,8},{16,12},{20,16},{24,20},{28,24},{32,28},{36,32}... | collective-permute-start | bytes 24584 | tf_op jit(solution)/shard_map/ppermute | solution.py:19
  146.5 27.4 %copy-start.17 = (pred[2]{0:T(512)(128)(4,1)S(1)}, pred[2]{0:T(512)(128)(4,1)}, u32[]{:S(2)}) copy-start(pred[2]{0:T(512)(128)(4,1)} %copy-done.15) | copy-start | bytes 10
  146.5 27.4 %copy-start.31 = (pred[2]{0:T(512)(128)(4,1)S(1)}, pred[2]{0:T(512)(128)(4,1)}, u32[]{:S(2)}) copy-start(pred[2]{0:T(512)(128)(4,1)} %compare_bitcast_fusion.5) | copy-start | bytes 10
  146.5 28.2 %copy-start.12 = (pred[2]{0:T(512)(128)(4,1)S(1)}, pred[2]{0:T(512)(128)(4,1)}, u32[]{:S(2)}) copy-start(pred[2]{0:T(512)(128)(4,1)} %get-tuple-element.32) | copy-start | bytes 10
  146.6 28.2 %copy-start.26 = (pred[2]{0:T(512)(128)(4,1)S(1)}, pred[2]{0:T(512)(128)(4,1)}, u32[]{:S(2)}) copy-start(pred[2]{0:T(512)(128)(4,1)} %compare_bitcast_fusion.4) | copy-start | bytes 10
  149.9 23.4 %collective-permute-start.6 = (f32[2,1024]{1,0:T(2,128)S(1)}, f32[2,1024]{1,0:T(2,128)S(1)}, u32[]{:S(2)}, u32[]{:S(2)}) collective-permute-start(f32[2,1024]{1,0:T(2,128)S(1)} %bitcast.240), channel_id=1, source_target_pairs={{0,4},{4,8},{8,12},{12,16},{16,20},{20,24},{24,28},{28,32},{32,36}... | collective-permute-start | bytes 24584 | tf_op jit(solution)/shard_map/ppermute | solution.py:17
  151.9 22.2 %collective-permute-start.7 = (f32[2,1024]{1,0:T(2,128)S(1)}, f32[2,1024]{1,0:T(2,128)S(1)}, u32[]{:S(2)}, u32[]{:S(2)}) collective-permute-start(f32[2,1024]{1,0:T(2,128)S(1)} %bitcast.237), channel_id=1, source_target_pairs={{4,0},{8,4},{12,8},{16,12},{20,16},{24,20},{28,24},{32,28},{36,32}... | collective-permute-start | bytes 24584 | tf_op jit(solution)/shard_map/ppermute | solution.py:19
  176.7 27.5 %copy-start.18 = (pred[2]{0:T(512)(128)(4,1)S(1)}, pred[2]{0:T(512)(128)(4,1)}, u32[]{:S(2)}) copy-start(pred[2]{0:T(512)(128)(4,1)} %copy-done.15) | copy-start | bytes 10
  176.7 27.5 %copy-start.32 = (pred[2]{0:T(512)(128)(4,1)S(1)}, pred[2]{0:T(512)(128)(4,1)}, u32[]{:S(2)}) copy-start(pred[2]{0:T(512)(128)(4,1)} %compare_bitcast_fusion.5) | copy-start | bytes 10
  176.7 28.2 %copy-start.13 = (pred[2]{0:T(512)(128)(4,1)S(1)}, pred[2]{0:T(512)(128)(4,1)}, u32[]{:S(2)}) copy-start(pred[2]{0:T(512)(128)(4,1)} %get-tuple-element.32) | copy-start | bytes 10
  176.7 28.2 %copy-start.27 = (pred[2]{0:T(512)(128)(4,1)S(1)}, pred[2]{0:T(512)(128)(4,1)}, u32[]{:S(2)}) copy-start(pred[2]{0:T(512)(128)(4,1)} %compare_bitcast_fusion.4) | copy-start | bytes 10
  180.1 23.4 %collective-permute-start.8 = (f32[2,1024]{1,0:T(2,128)S(1)}, f32[2,1024]{1,0:T(2,128)S(1)}, u32[]{:S(2)}, u32[]{:S(2)}) collective-permute-start(f32[2,1024]{1,0:T(2,128)S(1)} %bitcast.241), channel_id=1, source_target_pairs={{0,4},{4,8},{8,12},{12,16},{16,20},{20,24},{24,28},{28,32},{32,36}... | collective-permute-start | bytes 24584 | tf_op jit(solution)/shard_map/ppermute | solution.py:17
  182.0 22.2 %collective-permute-start.9 = (f32[2,1024]{1,0:T(2,128)S(1)}, f32[2,1024]{1,0:T(2,128)S(1)}, u32[]{:S(2)}, u32[]{:S(2)}) collective-permute-start(f32[2,1024]{1,0:T(2,128)S(1)} %bitcast.238), channel_id=1, source_target_pairs={{4,0},{8,4},{12,8},{16,12},{20,16},{24,20},{28,24},{32,28},{36,32}... | collective-permute-start | bytes 24584 | tf_op jit(solution)/shard_map/ppermute | solution.py:19
  201.7 21.1 %copy-start.9 = (pred[2]{0:T(512)(128)(4,1)S(1)}, pred[2]{0:T(512)(128)(4,1)}, u32[]{:S(2)}) copy-start(pred[2]{0:T(512)(128)(4,1)} %copy-done.8) | copy-start | bytes 10
  201.7 22.5 %copy-start.3 = (pred[2]{0:T(512)(128)(4,1)S(1)}, pred[2]{0:T(512)(128)(4,1)}, u32[]{:S(2)}) copy-start(pred[2]{0:T(512)(128)(4,1)} %copy-done.2) | copy-start | bytes 10
  201.8 23.9 %copy-start.7 = (pred[2]{0:T(512)(128)(4,1)S(1)}, pred[2]{0:T(512)(128)(4,1)}, u32[]{:S(2)}) copy-start(pred[2]{0:T(512)(128)(4,1)} %copy-done.6) | copy-start | bytes 10
  201.8 25.3 %copy-start.5 = (pred[2]{0:T(512)(128)(4,1)S(1)}, pred[2]{0:T(512)(128)(4,1)}, u32[]{:S(2)}) copy-start(pred[2]{0:T(512)(128)(4,1)} %copy-done.4) | copy-start | bytes 10
  206.9 31.1 %copy-start = (f32[2,32,1024]{2,1,0:T(8,128)}, f32[2,32,1024]{2,1,0:T(8,128)S(1)}, u32[]{:S(2)}) copy-start(f32[2,32,1024]{2,1,0:T(8,128)S(1)} %fusion.39) | copy-start | bytes 786436
  206.9 27.6 %copy-start.19 = (pred[2]{0:T(512)(128)(4,1)S(1)}, pred[2]{0:T(512)(128)(4,1)}, u32[]{:S(2)}) copy-start(pred[2]{0:T(512)(128)(4,1)} %copy-done.15) | copy-start | bytes 10
  206.9 27.6 %copy-start.33 = (pred[2]{0:T(512)(128)(4,1)S(1)}, pred[2]{0:T(512)(128)(4,1)}, u32[]{:S(2)}) copy-start(pred[2]{0:T(512)(128)(4,1)} %compare_bitcast_fusion.5) | copy-start | bytes 10
  206.9 28.4 %copy-start.14 = (pred[2]{0:T(512)(128)(4,1)S(1)}, pred[2]{0:T(512)(128)(4,1)}, u32[]{:S(2)}) copy-start(pred[2]{0:T(512)(128)(4,1)} %get-tuple-element.32) | copy-start | bytes 10
  206.9 28.4 %copy-start.28 = (pred[2]{0:T(512)(128)(4,1)S(1)}, pred[2]{0:T(512)(128)(4,1)}, u32[]{:S(2)}) copy-start(pred[2]{0:T(512)(128)(4,1)} %compare_bitcast_fusion.4) | copy-start | bytes 10
  210.3 23.5 %collective-permute-start.10 = (f32[2,1024]{1,0:T(2,128)S(1)}, f32[2,1024]{1,0:T(2,128)S(1)}, u32[]{:S(2)}, u32[]{:S(2)}) collective-permute-start(f32[2,1024]{1,0:T(2,128)S(1)} %bitcast.235), channel_id=1, source_target_pairs={{0,4},{4,8},{8,12},{12,16},{16,20},{20,24},{24,28},{28,32},{32,36}... | collective-permute-start | bytes 24584 | tf_op jit(solution)/shard_map/ppermute | solution.py:17
  212.3 22.4 %collective-permute-start.11 = (f32[2,1024]{1,0:T(2,128)S(1)}, f32[2,1024]{1,0:T(2,128)S(1)}, u32[]{:S(2)}, u32[]{:S(2)}) collective-permute-start(f32[2,1024]{1,0:T(2,128)S(1)} %bitcast.234), channel_id=1, source_target_pairs={{4,0},{8,4},{12,8},{16,12},{20,16},{24,20},{28,24},{32,28},{36,32}... | collective-permute-start | bytes 24584 | tf_op jit(solution)/shard_map/ppermute | solution.py:19
  240.9 7.9 %all-to-all-start.1 = ((f32[4,2,4096]{2,1,0:T(2,128)}), f32[4,2,4096]{2,1,0:T(2,128)S(1)}, u32[]{:S(2)}, u32[]{:S(2)}) async-start(f32[4,2,4096]{2,1,0:T(2,128)} %fusion.121), calls=%async_computation.1 | async-start | bytes 262144 | tf_op jit(solution)/shard_map/all_to_all | solution.py:224
  (9 other events, 94.2 us)
where the time goes:
time: 252 us; the launch traced here: 250 us
  local copies, waits for them, and re-layouts  82.9 us (33%)
  starting transfers between devices  73.5 us (29%)
  waiting for transfers between devices  53.5 us (21%)
  other arithmetic  36.2 us (14%)
    ppermute x6, starting transfers between devices, with_halo(): lax.ppermute(head, axis, [((i + 1) % count, i) for i in range(ends)])  54.5 us
    all_to_all x1, waiting for transfers between devices, per_device(): lax.all_to_all(labels.reshape(groups, box_count), 'grp', split_axis=0, co...  48.9 us
    gather x36, local copies, waits for them, and re-layouts, ghost_planes(): chosen = jnp.take(tables[face_id], local_row, axis=0)  23.4 us
    select_n x21, other arithmetic, ghost_planes(): results.append(jnp.where(is_valid, chosen, fallback))  12.6 us
    ppermute x6, starting transfers between devices, with_halo(): lax.ppermute(tail, axis, [(i, (i + 1) % count) for i in range(ends)])  12.5 us
    reshape x6, local copies, waits for them, and re-layouts, beside_cells(): jnp.repeat(planes[5], box_edge, axis=2)  8.55 us
    select_n x4, other arithmetic, half_sweep(): return jnp.where(parity_rows == colour, updated, field)  8.05 us
    reshape x6, local copies, waits for them, and re-layouts, beside_cells(): jnp.repeat(planes[4], box_edge, axis=2)  7.84 us
  transfers between devices with their start and end apart: 14, of which 2 were waited for; matrix products, arithmetic and copies ran while one was open for 30% of the time, Pallas kernels for 0%

commit v1 on v0

v1 whole, which is shorter than its diff:
```python
import jax
import jax.numpy as jnp
from jax import lax
from jax.experimental import pallas as pl
from jax.experimental.pallas import tpu as pltpu
from jax.sharding import PartitionSpec as P

MASS_TERM = 0.25
LANES = 128
SOL, RHS, COEF, ENDS = 0, 16, 48, 80
END_ROWS = 12
PAD, PAIR_PAD = 8, 4
OWN, PAIRS, FIRST = 32, 24, 8

VMEM = pl.BlockSpec(memory_space=pltpu.VMEM)
SMEM = pl.BlockSpec(memory_space=pltpu.SMEM)


def lane_ids(rows):
    return lax.broadcasted_iota(jnp.int32, (rows, LANES), 1)


def row_ids(rows):
    return lax.broadcasted_iota(jnp.int32, (rows, LANES), 0)


def odd_lanes(rows):
    lane = lane_ids(rows)
    return ((lane >> 5) + lane) & 1


def offsets(counts, position):
    count = counts.shape[1]
    start = jnp.int32(0)
    for j in range(count):
        start = start + jnp.where(j < position, counts[0, j], 0)
    here = start - 2 * position
    after = here + counts[0, position] - 2
    before = here - counts[0, jnp.maximum(position - 1, 0)] + 2
    beyond = after + counts[0, jnp.minimum(position + 1, count - 1)] - 2
    return before, here, after, beyond


def link_code(links, box, face, first_box):
    target = links[0, box, face]
    return jnp.where(target < 0, 0, jnp.where(target - first_box == box, 1, 2))


def end_pieces(fields, row, tile, upper):
    lanes = slice(tile * LANES, (tile + 1) * LANES)
    rows = slice(24, 32) if upper else slice(0, 8)
    sol = fields[0, 0, row, rows, lanes]
    rhs = fields[1, 0, row, rows, lanes]
    coef = fields[2, 0, row, rows, lanes]
    mixed = (row_ids(8) + odd_lanes(8)) & 1
    if upper:
        packed = jnp.where(mixed == 0, pltpu.roll(sol, 5, 0), pltpu.roll(sol, 2, 0))
        return packed[:3], rhs[4:], coef[3:]
    packed = jnp.where(mixed == 1, sol, pltpu.roll(sol, 5, 0))
    return packed[:3], rhs[:4], coef[:5]


def store_ends(out, tile, base, pieces):
    out[tile, base : base + 3, :] = pieces[0]
    out[tile, base + 3 : base + 7, :] = pieces[1]
    out[tile, base + 7 : base + 12, :] = pieces[2]


def load_ends(ref, tile, base):
    return (
        ref[tile, base : base + 3, :],
        ref[tile, base + 3 : base + 7, :],
        ref[tile, base + 7 : base + 12, :],
    )


def pack_kernel(counts, links, fields, near_a, near_b, far_a, far_b):
    position = lax.axis_index("box")
    _, here, after, _ = offsets(counts, position)
    tiles = fields.shape[4] // LANES
    first_box = 2 * position
    held = (jnp.maximum(-here, 0), 1 - here)
    move_up = jnp.minimum(2 - here, 3)

    def message(out, upper):
        row = move_up if upper else 0
        mixed = (row_ids(16) + odd_lanes(16)) & 1
        for tile in range(tiles):
            lanes = slice(tile * LANES, (tile + 1) * LANES)
            low = fields[0, 0, row, 0:16, lanes]
            high = pltpu.roll(fields[0, 0, row, 16:32, lanes], 15, 0)
            out[tile, SOL : SOL + 16, :] = jnp.where(mixed == 1, low, high)
            out[tile, RHS : RHS + 32, :] = fields[1, 0, row, :, lanes]
            out[tile, COEF : COEF + 32, :] = fields[2, 0, row, :, lanes]
            for box in range(2):
                packed, rhs, coef = end_pieces(fields, held[box], tile, upper)
                if tile == 0:
                    lane = lane_ids(3)
                    for face in range(2, 6):
                        code = link_code(links, box, face, first_box).astype(jnp.float32)
                        mine = (lane == 2 * (face - 2) + int(upper)) & (row_ids(3) == 2)
                        packed = jnp.where(mine, code, packed)
                store_ends(out, tile, ENDS + END_ROWS * box, (packed, rhs, coef))

    def far_message(out, upper):
        row = move_up if upper else 0
        for tile in range(tiles):
            store_ends(out, tile, 0, end_pieces(fields, row, tile, upper))

    even = position % 2 == 0
    lower = position % 4 < 2

    @pl.when(even)
    def _():
        message(near_a, True)
        message(near_b, False)

    @pl.when(jnp.logical_not(even))
    def _():
        message(near_a, False)
        message(near_b, True)

    @pl.when(lower)
    def _():
        far_message(far_a, True)
        far_message(far_b, False)

    @pl.when(jnp.logical_not(lower))
    def _():
        far_message(far_a, False)
        far_message(far_b, True)


def choose(flag, one, other):
    return tuple(jnp.where(flag, a, b) for a, b in zip(one, other, strict=True))


def smooth_kernel(
    counts,
    links,
    parents,
    fields,
    near_a,
    near_b,
    far_a,
    far_b,
    smoothed,
    residual,
    coarse,
    raw,
    value,
    coef,
    weight,
    source,
    diagonal,
    defect,
    code,
    stage,
):
    position = lax.axis_index("box")
    before, here, after, beyond = offsets(counts, position)
    tiles = fields.shape[4] // LANES
    first_box = 2 * position
    even = position % 2 == 0
    lower = position % 4 < 2

    def place_local(box, row):
        for tile in range(tiles):
            lanes = slice(tile * LANES, (tile + 1) * LANES)
            for field in range(3):
                raw[field, box, tile, PAD : PAD + OWN, :] = fields[field, 0, row, :, lanes]

    def place_moved(box, ref):
        for tile in range(tiles):
            packed = ref[tile, SOL : SOL + 16, :]
            raw[0, box, tile, PAD : PAD + 16, :] = packed
            raw[0, box, tile, PAD + 16 : PAD + 32, :] = pltpu.roll(packed, 1, 0)
            raw[1, box, tile, PAD : PAD + OWN, :] = ref[tile, RHS : RHS + 32, :]
            raw[2, box, tile, PAD : PAD + OWN, :] = ref[tile, COEF : COEF + 32, :]

    from_below = here == 1
    from_above = after == -1

    @pl.when(jnp.logical_not(from_below))
    def _():
        place_local(0, jnp.maximum(-here, 0))

    @pl.when(from_below & even)
    def _():
        place_moved(0, near_b)

    @pl.when(from_below & jnp.logical_not(even))
    def _():
        place_moved(0, near_a)

    @pl.when(jnp.logical_not(from_above))
    def _():
        place_local(1, 1 - here)

    @pl.when(from_above & even)
    def _():
        place_moved(1, near_a)

    @pl.when(from_above & jnp.logical_not(even))
    def _():
        place_moved(1, near_b)

    def crossing(face, run_first):
        ids = [links[0, box, face] for box in range(2)]
        linked = [one >= 0 for one in ids]
        swap = jnp.where(
            linked[0],
            ids[0] - run_first == 1,
            linked[1] & (ids[1] - run_first == 0),
        )
        return linked, swap

    low_linked, low_swap = crossing(0, first_box - 2)
    high_linked, high_swap = crossing(1, first_box + 2)
    zeros = jnp.zeros((8, LANES), jnp.float32)
    for tile in range(tiles):
        ends = [
            choose(even, load_ends(near_b, tile, ENDS + END_ROWS * i), load_ends(near_a, tile, ENDS + END_ROWS * i))
            for i in range(2)
        ]
        far = choose(lower, load_ends(far_b, tile, 0), load_ends(far_a, tile, 0))
        low = (
            choose(before == 1, far, ends[0]),
            choose(here == -1, end_pieces(fields, 0, tile, True), ends[1]),
        )
        ends = [
            choose(even, load_ends(near_a, tile, ENDS + END_ROWS * i), load_ends(near_b, tile, ENDS + END_ROWS * i))
            for i in range(2)
        ]
        far = choose(lower, load_ends(far_a, tile, 0), load_ends(far_b, tile, 0))
        high = (
            choose(after == 1, end_pieces(fields, jnp.minimum(2 - here, 3), tile, False), ends[0]),
            choose(beyond == -1, far, ends[1]),
        )
        for box in range(2):
            sol, rhs, cof = choose(low_swap, low[1 - box], low[box])
            for field in range(3):
                raw[field, box, tile, 0:8, :] = zeros
                raw[field, box, tile, PAD + OWN : PAD + OWN + 8, :] = zeros
            raw[0, box, tile, 3:6, :] = sol
            raw[0, box, tile, 6:8, :] = sol[:2]
            raw[1, box, tile, 4:8, :] = rhs
            raw[2, box, tile, 3:8, :] = cof
            sol, rhs, cof = choose(high_swap, high[1 - box], high[box])
            raw[0, box, tile, 40:43, :] = sol
            raw[0, box, tile, 43:45, :] = sol[:2]
            raw[1, box, tile, 40:44, :] = rhs
            raw[2, box, tile, 40:45, :] = cof

    pair = row_ids(PAIRS)
    for face in range(2, 6):
        slot = 2 * (face - 2)
        ends = []
        for i in range(2):
            at = ENDS + END_ROWS * i + 2
            below = jnp.where(even, near_b[0, at : at + 1, :], near_a[0, at : at + 1, :])[:, slot + 1 : slot + 2]
            above = jnp.where(even, near_a[0, at : at + 1, :], near_b[0, at : at + 1, :])[:, slot : slot + 1]
            ends.append([jnp.broadcast_to(one, (PAIRS, LANES)) for one in (below, above)])
        for box in range(2):
            below = jnp.where(low_swap, ends[1 - box][0], ends[box][0])
            above = jnp.where(high_swap, ends[1 - box][1], ends[box][1])
            own = link_code(links, box, face, first_box).astype(jnp.float32)
            code[box, face - 2] = jnp.where(
                pair < PAIR_PAD, below, jnp.where(pair < PAIR_PAD + 16, own, above)
            )

    odd = odd_lanes(PAIRS)
    for box in range(2):
        for tile in range(tiles):
            for field, out in ((0, value), (2, coef)):
                lo = raw[field, box, tile, pl.ds(0, PAIRS, 2), :]
                hi = raw[field, box, tile, pl.ds(1, PAIRS, 2), :]
                out[0, box, tile, FIRST : FIRST + PAIRS, :] = jnp.where(odd == 1, hi, lo)
                out[1, box, tile, FIRST : FIRST + PAIRS, :] = jnp.where(odd == 1, lo, hi)
            lo = raw[1, box, tile, pl.ds(0, PAIRS, 2), :]
            hi = raw[1, box, tile, pl.ds(1, PAIRS, 2), :]
            source[0, box, tile] = jnp.where(odd == 1, hi, lo)
            source[1, box, tile] = jnp.where(odd == 1, lo, hi)

    lane = lane_ids(PAIRS)
    depth = lane & 31
    mid = slice(FIRST, FIRST + PAIRS)

    def nearby(ref, colour, box, tile):
        other = 1 - colour
        here_ = ref[other, box, tile, mid, :]
        there = ref[other, 1 - box, tile, mid, :]
        across = jnp.where(
            odd == colour,
            ref[other, box, tile, FIRST - 1 : FIRST - 1 + PAIRS, :],
            ref[other, box, tile, FIRST + 1 : FIRST + 1 + PAIRS, :],
        )
        y_low = ref[other, box, (tile - 1) % tiles, mid, :]
        if tile == 0:
            y_low = jnp.where(code[box, 0] == 2, ref[other, 1 - box, tiles - 1, mid, :], y_low)
        y_high = ref[other, box, (tile + 1) % tiles, mid, :]
        if tile == tiles - 1:
            y_high = jnp.where(code[box, 1] == 2, ref[other, 1 - box, 0, mid, :], y_high)
        z_low = jnp.where(code[box, 2] == 2, there, here_)
        z_high = jnp.where(code[box, 3] == 2, there, here_)
        return (
            across,
            here_,
            pltpu.roll(jnp.where(lane >= 96, y_low, here_), 32, 1),
            pltpu.roll(jnp.where(lane < 32, y_high, here_), 96, 1),
            jnp.where(depth == 0, pltpu.roll(z_low, 97, 1), pltpu.roll(here_, 1, 1)),
            jnp.where(depth == 31, pltpu.roll(z_high, 31, 1), pltpu.roll(here_, 127, 1)),
        )

    def weigh(colour, carry):
        for box in range(2):
            cut_low = jnp.logical_not(low_linked[box])
            cut_high = jnp.logical_not(high_linked[box])
            low_rows = ((pair == PAIR_PAD) & cut_low) | ((pair == PAIR_PAD + 16) & cut_high)
            high_rows = ((pair == PAIR_PAD + 15) & cut_high) | ((pair == PAIR_PAD - 1) & cut_low)
            end = jnp.where(odd == colour, low_rows.astype(jnp.int32), high_rows.astype(jnp.int32)) == 1
            none = [code[box, k] == 0 for k in range(4)]
            for tile in range(tiles):
                own = coef[colour, box, tile, mid, :]
                near = nearby(coef, colour, box, tile)
                lost = (
                    end,
                    None,
                    (lane < 32) & none[0] if tile == 0 else None,
                    (lane >= 96) & none[1] if tile == tiles - 1 else None,
                    (depth == 0) & none[2],
                    (depth == 31) & none[3],
                )
                total = jnp.full((PAIRS, LANES), MASS_TERM, jnp.float32)
                kept = []
                for one, gone in zip(near, lost, strict=True):
                    if gone is None:
                        w = 0.5 * (own + one)
                        kept.append(w)
                    else:
                        w = 0.5 * (own + jnp.where(gone, own, one))
                        kept.append(jnp.where(gone, 0.0, w))
                    total = total + w
                inverse = 1.0 / total
                diagonal[colour, box, tile] = total
                source[colour, box, tile] = source[colour, box, tile] * inverse
                for d in range(6):
                    weight[colour, d, box, tile] = kept[d] * inverse
        return carry

    lax.fori_loop(0, 2, weigh, 0)

    def update(colour, box, tile):
        total = source[colour, box, tile]
        for d, one in enumerate(nearby(value, colour, box, tile)):
            total = total + weight[colour, d, box, tile] * one
        return total

    def sweep(step, carry):
        colour = step & 1
        for box in range(2):
            for tile in range(tiles):
                value[colour, box, tile, mid, :] = update(colour, box, tile)
        return carry

    lax.fori_loop(0, 4, sweep, 0)

    def remain(colour, carry):
        for box in range(2):
            for tile in range(tiles):
                defect[colour, box, tile] = diagonal[colour, box, tile] * (
                    update(colour, box, tile) - value[colour, box, tile, mid, :]
                )
        return carry

    lax.fori_loop(0, 2, remain, 0)

    own_pairs = slice(PAIR_PAD, PAIR_PAD + 16)
    own_rows = slice(FIRST + PAIR_PAD, FIRST + PAIR_PAD + 16)
    odd = odd_lanes(16)
    halves = tiles // 2
    gathered = []
    for half in range(2):
        for box in range(2):
            sums = []
            for tile in range(half * halves, (half + 1) * halves):
                lanes = slice(tile * LANES, (tile + 1) * LANES)
                for k, out, red, black in (
                    (0, smoothed, value[0, box, tile, own_rows, :], value[1, box, tile, own_rows, :]),
                    (1, residual, defect[0, box, tile, own_pairs, :], defect[1, box, tile, own_pairs, :]),
                ):
                    stage[k, box, tile, pl.ds(0, 16, 2), :] = jnp.where(odd == 1, black, red)
                    stage[k, box, tile, pl.ds(1, 16, 2), :] = jnp.where(odd == 1, red, black)
                    out[0, box, :, lanes] = stage[k, box, tile]
                sums.append(red + black)
            gathered.append(jnp.concatenate(sums, axis=1))
    whole = jnp.concatenate(gathered, axis=0)
    first = whole.astype(jnp.bfloat16)
    rest = whole - first.astype(jnp.float32)
    second = rest.astype(jnp.bfloat16)
    third = (rest - second.astype(jnp.float32)).astype(jnp.bfloat16)
    width = halves * LANES
    cell = lax.broadcasted_iota(jnp.int32, (width, LANES), 0)
    block = lax.broadcasted_iota(jnp.int32, (width, LANES), 1)
    merge = jnp.where((cell >> 6) * 16 + ((cell & 31) >> 1) == block, 1.0, 0.0).astype(jnp.bfloat16)
    split = jnp.dot(
        jnp.concatenate([first, second, third], axis=0), merge, preferred_element_type=jnp.float32
    )
    mean = (split[:64] + split[64:128] + split[128:]) * 0.125
    for half in range(2):
        coarse[0:32, half * LANES : (half + 1) * LANES] = mean[32 * half : 32 * half + 32]
    for box in range(2):
        label = parents[0, box, 0] * 16 + parents[0, box, 1] * 8 + parents[0, box, 2]
        coarse[32 + 8 * box : 40 + 8 * box, :] = jnp.full((8, 2 * LANES), label.astype(jnp.float32))


def place_kernel(got, source, out):
    group = lax.axis_index("grp")
    base = (group * 16).astype(jnp.float32)
    for octant in range(16):
        kept = source[0, octant // 8, octant % 8]
        for sender in range(got.shape[0]):
            for box in range(2):
                label = got[sender, 32 + 8 * box : 40 + 8 * box, :]
                mine = jnp.concatenate([label, label], axis=0) == base + float(octant)
                kept = jnp.where(mine, got[sender, 16 * box : 16 * box + 16, :], kept)
        out[0, octant // 8, octant % 8] = kept


def per_device(old_fields, old_count, neighbours, parents, coarse_source):
    f32 = jnp.float32
    curve = lax.axis_size("box")
    box_edge, plane_cells = old_fields.shape[3:]
    tiles = plane_cells // LANES
    near = jax.ShapeDtypeStruct((tiles, ENDS + 2 * END_ROWS, LANES), f32)
    far = jax.ShapeDtypeStruct((tiles, END_ROWS, LANES), f32)
    params = pltpu.CompilerParams(vmem_limit_bytes=40 << 20)
    messages = pl.pallas_call(
        pack_kernel,
        out_shape=(near, near, far, far),
        in_specs=[SMEM, SMEM, VMEM],
        out_specs=(VMEM,) * 4,
        compiler_params=params,
        cost_estimate=pl.CostEstimate(flops=10**6, bytes_accessed=3 << 20, transcendentals=0),
        name="pack",
    )(old_count, neighbours, old_fields)

    def pairs(distance, shift):
        ids = [i for i in range(curve) if (i - shift) % (2 * distance) < distance and 0 <= i and i + distance < curve]
        return [(i, i + distance) for i in ids] + [(i + distance, i) for i in ids]

    moved = [
        lax.ppermute(message, "box", pairs(distance, shift))
        for message, distance, shift in zip(messages, (1, 1, 2, 2), (0, 1, 0, 2), strict=True)
    ]
    boxes = neighbours.shape[1]
    fine = jax.ShapeDtypeStruct((1, boxes, box_edge, plane_cells), f32)
    packed = (2, boxes, tiles, PAIRS, LANES)
    smoothed, residual, coarse = pl.pallas_call(
        smooth_kernel,
        out_shape=(fine, fine, jax.ShapeDtypeStruct((48, 2 * LANES), f32)),
        in_specs=[SMEM, SMEM, SMEM] + [VMEM] * 5,
        out_specs=(VMEM,) * 3,
        scratch_shapes=[
            pltpu.VMEM((3, boxes, tiles, OWN + 2 * PAD, LANES), f32),
            pltpu.VMEM((2, boxes, tiles, PAIRS + 2 * FIRST, LANES), f32),
            pltpu.VMEM((2, boxes, tiles, PAIRS + 2 * FIRST, LANES), f32),
            pltpu.VMEM((2, 6, boxes, tiles, PAIRS, LANES), f32),
            pltpu.VMEM(packed, f32),
            pltpu.VMEM(packed, f32),
            pltpu.VMEM(packed, f32),
            pltpu.VMEM((boxes, 4, PAIRS, LANES), f32),
            pltpu.VMEM((2, boxes, tiles, OWN, LANES), f32),
        ],
        compiler_params=params,
        cost_estimate=pl.CostEstimate(flops=10**7, bytes_accessed=6 << 20, transcendentals=0),
        name="smooth",
    )(old_count, neighbours, parents, old_fields, *moved)
    got = lax.all_gather(coarse, "grp")
    coarse_rhs = pl.pallas_call(
        place_kernel,
        out_shape=jax.ShapeDtypeStruct(coarse_source.shape, f32),
        in_specs=[VMEM, VMEM],
        out_specs=VMEM,
        compiler_params=params,
        name="place",
    )(got, coarse_source)
    return smoothed, residual, coarse_rhs


def solution(mesh):
    in_specs = (
        P(None, "grp", "box", None, None),
        P("grp", None),
        P("grp", "box", None),
        P("grp", "box", None),
        P("grp", "box", None, None, None),
    )
    out_specs = (
        P("grp", "box", None, None),
        P("grp", "box", None, None),
        P("grp", "box", None, None, None),
    )
    return jax.shard_map(
        per_device, mesh=mesh, in_specs=in_specs, out_specs=out_specs, check_vma=False
    )
```

time: 252 us -> 42.8 us (0.17)
  local copies, waits for them, and re-layouts: 82.9 us -> 2.74 us
  starting transfers between devices: 73.5 us -> 10.6 us
  waiting for transfers between devices: 53.5 us -> 12.3 us
  other arithmetic: 36.2 us -> 0 us
  Pallas kernels: 0 us -> 10.2 us
  blocking collectives: 0 us -> 5.59 us
    ppermute x12 -> x4, starting transfers between devices: 67 us -> 10.6 us  [per_device(): lax.ppermute(message, 'box', pairs(distance, shift))]
    all_to_all x2 -> x0, waiting for transfers between devices: 53.5 us -> none  [the longest x1 48.9 us: per_device(): lax.all_to_all(labels.reshape(groups, box_count), 'grp', split_axis=0, co...]
    gather x38 -> x0, local copies, waits for them, and re-layouts: 26.9 us -> none  [the longest x36 23.4 us: ghost_planes(): chosen = jnp.take(tables[face_id], local_row, axis=0)]
    select_n x29 -> x0, other arithmetic: 20.8 us -> none  [the longest x21 12.6 us: ghost_planes(): results.append(jnp.where(is_valid, chosen, fallback))]
    slice x40 -> x0, local copies, waits for them, and re-layouts: 20 us -> none  [the longest x4 3.54 us: beside_cells(): low_shift = jnp.concatenate([zero_column, box_field[:, :, :-1]], axis=2)]
    reshape x15 -> x0, local copies, waits for them, and re-layouts: 17.6 us -> none  [the longest x6 8.55 us: beside_cells(): jnp.repeat(planes[5], box_edge, axis=2)]
    ppermute x12 -> x4, waiting for transfers between devices: 0.03 us -> 12.3 us  [per_device(): lax.ppermute(message, 'box', pairs(distance, shift))]
    broadcast_in_dim x24 -> x0, local copies, waits for them, and re-layouts: 12.2 us -> none  [the longest x6 6.03 us: beside_cells(): jnp.repeat(planes[5], box_edge, axis=2)]
  transfers between devices with their start and end apart: 14 -> 4, of which waited for: 2 -> 3; matrix products, arithmetic and copies ran while one was open for 30% -> 0% of each run, Pallas kernels for 0% -> 0%
where the time goes in v1:
time: 42.8 us; the launch traced here: 42.1 us
  waiting for transfers between devices  12.3 us (29%)
  starting transfers between devices  10.6 us (25%)
  Pallas kernels  10.2 us (24%)
  blocking collectives  5.59 us (13%)
  local copies, waits for them, and re-layouts  2.74 us (6%)
  between operations  0.69 us (2%)
    ppermute x4, waiting for transfers between devices, per_device(): lax.ppermute(message, 'box', pairs(distance, shift))  12.3 us
    ppermute x4, starting transfers between devices, per_device(): lax.ppermute(message, 'box', pairs(distance, shift))  10.6 us
    pallas_call x1, Pallas kernels, per_device(): pl.pallas_call(smooth_kernel, out_shape=(fine, fine, jax.ShapeDtypeStruct...  8.62 us
    all_gather x1, blocking collectives, per_device(): got = lax.all_gather(coarse, 'grp')  5.59 us
    unnamed x10, local copies, waits for them, and re-layouts  2.74 us
  transfers between devices with their start and end apart: 4, of which 3 were waited for; matrix products, arithmetic and copies ran while one was open for 0% of the time, Pallas kernels for 0%

profile of v1, /device:TPU:128, one launch (start us, length us, event | category | flops | bytes accessed | tf_op | source)
XLA Modules:
  0.0 42.1 jit_solution(12307293970819498989)
XLA Ops:
  0.6 0.0 copy-start
  0.6 1.4 %copy-done = f32[3,1,4,32,1024]{4,3,2,1,0:T(8,128)S(1)} copy-done((f32[3,1,4,32,1024]{4,3,2,1,0:T(8,128)S(1)}, f32[3,1,4,32,1024]{4,3,2,1,0:T(8,128)}, u32[]{:S(2)}) %copy-start) | copy-done | bytes 1572888
  2.0 0.0 copy-start.2
  2.0 0.7 %copy-done.2 = s32[1,2,6]{2,1,0:T(2,128)S(1)} copy-done((s32[1,2,6]{2,1,0:T(2,128)S(1)}, s32[1,2,6]{2,1,0:T(2,128)}, u32[]{:S(2)}) %copy-start.2) | copy-done | bytes 72
  2.7 0.0 copy-start.3
  2.7 0.7 %copy-done.3 = s32[1,64]{1,0:T(1,128)S(1)} copy-done((s32[1,64]{1,0:T(1,128)S(1)}, s32[1,64]{1,0:T(1,128)}, u32[]{:S(2)}) %copy-start.3) | copy-done | bytes 280
  3.4 0.0 copy-start.4
  3.4 0.7 %pack.1 = (f32[8,104,128]{2,1,0:T(8,128)S(1)}, f32[8,104,128]{2,1,0:T(8,128)S(1)}, f32[8,12,128]{2,1,0:T(8,128)S(1)}, f32[8,12,128]{2,1,0:T(8,128)S(1)}) custom-call(s32[1,64]{1,0:T(1,128)S(1)} %copy-done.3, s32[1,2,6]{2,1,0:T(2,128)S(1)} %copy-done.2, f32[3,1,4,32,1024]{4,3,2,1,0:T(8,128)S(1)} %copy-done), custom_call_target="tpu_custom_call" | custom-call | flops 1000000 | bytes 3145728 | tf_op jit(solution)/shard_map/pack/pallas_call | solution.py:438
  4.1 0.0 copy-start.1
  4.1 3.3 %collective-permute-start = (f32[8,104,128]{2,1,0:T(8,128)S(1)}, f32[8,104,128]{2,1,0:T(8,128)S(1)}, u32[]{:S(2)}, u32[]{:S(2)}) collective-permute-start(f32[8,104,128]{2,1,0:T(8,128)S(1)} %get-tuple-element.10), channel_id=1, source_target_pairs={{0,4},{8,12},{16,20},{24,28},{32,36},{40,44},{48,52},{56,60},{64,6... | collective-permute-start | bytes 1277960 | tf_op jit(solution)/shard_map/ppermute | solution.py:453
  7.4 4.0 %collective-permute-start.1 = (f32[8,104,128]{2,1,0:T(8,128)S(1)}, f32[8,104,128]{2,1,0:T(8,128)S(1)}, u32[]{:S(2)}, u32[]{:S(2)}) collective-permute-start(f32[8,104,128]{2,1,0:T(8,128)S(1)} %get-tuple-element.11), channel_id=1, source_target_pairs={{4,8},{12,16},{20,24},{28,32},{36,40},{44,48},{52,56},{60,64},{68,... | collective-permute-start | bytes 1277960 | tf_op jit(solution)/shard_map/ppermute | solution.py:453
  11.4 0.1 collective-permute-start.2
  11.5 3.2 %collective-permute-start.3 = (f32[8,12,128]{2,1,0:T(8,128)S(1)}, f32[8,12,128]{2,1,0:T(8,128)S(1)}, u32[]{:S(2)}, u32[]{:S(2)}) collective-permute-start(f32[8,12,128]{2,1,0:T(8,128)S(1)} %get-tuple-element.13), channel_id=1, source_target_pairs={{8,16},{12,20},{24,32},{28,36},{40,48},{44,52},{56,64},{60,68},{72... | collective-permute-start | bytes 147464 | tf_op jit(solution)/shard_map/ppermute | solution.py:453
  14.8 7.0 %collective-permute-done.2.far_a = f32[8,12,128]{2,1,0:T(8,128)S(1)} collective-permute-done((f32[8,12,128]{2,1,0:T(8,128)S(1)}, f32[8,12,128]{2,1,0:T(8,128)S(1)}, u32[]{:S(2)}, u32[]{:S(2)}) %collective-permute-start.2) | collective-permute-done | bytes 49184 | tf_op jit(solution)/shard_map/ppermute | solution.py:453
  21.8 0.0 collective-permute-done.3.far_b
  21.8 3.8 %collective-permute-done.near_a = f32[8,104,128]{2,1,0:T(8,128)S(1)} collective-permute-done((f32[8,104,128]{2,1,0:T(8,128)S(1)}, f32[8,104,128]{2,1,0:T(8,128)S(1)}, u32[]{:S(2)}, u32[]{:S(2)}) %collective-permute-start) | collective-permute-done | bytes 426016 | tf_op jit(solution)/shard_map/ppermute | solution.py:453
  25.6 1.4 %collective-permute-done.1.near_b = f32[8,104,128]{2,1,0:T(8,128)S(1)} collective-permute-done((f32[8,104,128]{2,1,0:T(8,128)S(1)}, f32[8,104,128]{2,1,0:T(8,128)S(1)}, u32[]{:S(2)}, u32[]{:S(2)}) %collective-permute-start.1) | collective-permute-done | bytes 426016 | tf_op jit(solution)/shard_map/ppermute | solution.py:453
  27.0 0.0 copy-done.4
  27.0 8.6 %smooth.1 = (f32[1,2,32,1024]{3,2,1,0:T(8,128)}, f32[1,2,32,1024]{3,2,1,0:T(8,128)}, f32[48,256]{1,0:T(8,128)S(1)}) custom-call(s32[1,64]{1,0:T(1,128)S(1)} %copy-done.3, s32[1,2,6]{2,1,0:T(2,128)S(1)} %copy-done.2, s32[1,2,3]{2,1,0:T(2,128)S(1)} %copy-done.4, f32[3,1,4,32,1024]{4,3,2,1,0:T(8,128)S(1)} %copy-done, ...), custom_call_target="tpu_custom_call" | custom-call | flops 10000000 | bytes 6291456 | tf_op jit(solution)/shard_map/smooth/pallas_call | solution.py:459
  35.7 5.6 %all-gather = f32[192,256]{1,0:T(8,128)S(1)} all-gather(f32[48,256]{1,0:T(8,128)S(1)} %get-tuple-element.16), channel_id=2, replica_groups=mesh['box'=64,'grp'=4] {'grp'}, dimensions={0}, use_global_device_ids=true | all-gather | bytes 245760 | tf_op jit(solution)/shard_map/all_gather | solution.py:479
  41.3 0.0 copy-done.1
  41.3 0.8 %place.1 = f32[1,2,8,16,256]{4,3,2,1,0:T(8,128)} custom-call(f32[4,48,256]{2,1,0:T(8,128)S(1)} %bitcast.1, f32[1,2,8,16,256]{4,3,2,1,0:T(8,128)S(1)} %copy-done.1), custom_call_target="tpu_custom_call" | custom-call | tf_op jit(solution)/shard_map/place/pallas_call | solution.py:480
Async XLA Ops:
  0.6 1.4 %copy-start = (f32[3,1,4,32,1024]{4,3,2,1,0:T(8,128)S(1)}, f32[3,1,4,32,1024]{4,3,2,1,0:T(8,128)}, u32[]{:S(2)}) copy-start(f32[3,1,4,32,1024]{4,3,2,1,0:T(8,128)} %fields.3) | copy-start | bytes 4718596
  2.0 0.7 %copy-start.2 = (s32[1,2,6]{2,1,0:T(2,128)S(1)}, s32[1,2,6]{2,1,0:T(2,128)}, u32[]{:S(2)}) copy-start(s32[1,2,6]{2,1,0:T(2,128)} %links.3) | copy-start | bytes 148
  2.7 0.7 %copy-start.3 = (s32[1,64]{1,0:T(1,128)S(1)}, s32[1,64]{1,0:T(1,128)}, u32[]{:S(2)}) copy-start(s32[1,64]{1,0:T(1,128)} %counts.3) | copy-start | bytes 772
  3.4 23.7 %copy-start.4 = (s32[1,2,3]{2,1,0:T(2,128)S(1)}, s32[1,2,3]{2,1,0:T(2,128)}, u32[]{:S(2)}) copy-start(s32[1,2,3]{2,1,0:T(2,128)} %parents.1) | copy-start | bytes 76
  4.1 37.1 %copy-start.1 = (f32[1,2,8,16,256]{4,3,2,1,0:T(8,128)S(1)}, f32[1,2,8,16,256]{4,3,2,1,0:T(8,128)}, u32[]{:S(2)}) copy-start(f32[1,2,8,16,256]{4,3,2,1,0:T(8,128)} %source.1) | copy-start | bytes 786436
  4.1 21.5 %collective-permute-start = (f32[8,104,128]{2,1,0:T(8,128)S(1)}, f32[8,104,128]{2,1,0:T(8,128)S(1)}, u32[]{:S(2)}, u32[]{:S(2)}) collective-permute-start(f32[8,104,128]{2,1,0:T(8,128)S(1)} %get-tuple-element.10), channel_id=1, source_target_pairs={{0,4},{8,12},{16,20},{24,28},{32,36},{40,44},{48,52},{56,60},{64,6... | collective-permute-start | bytes 1277960 | tf_op jit(solution)/shard_map/ppermute | solution.py:453
  7.4 19.6 %collective-permute-start.1 = (f32[8,104,128]{2,1,0:T(8,128)S(1)}, f32[8,104,128]{2,1,0:T(8,128)S(1)}, u32[]{:S(2)}, u32[]{:S(2)}) collective-permute-start(f32[8,104,128]{2,1,0:T(8,128)S(1)} %get-tuple-element.11), channel_id=1, source_target_pairs={{4,8},{12,16},{20,24},{28,32},{36,40},{44,48},{52,56},{60,64},{68,... | collective-permute-start | bytes 1277960 | tf_op jit(solution)/shard_map/ppermute | solution.py:453
  11.4 10.4 %collective-permute-start.2 = (f32[8,12,128]{2,1,0:T(8,128)S(1)}, f32[8,12,128]{2,1,0:T(8,128)S(1)}, u32[]{:S(2)}, u32[]{:S(2)}) collective-permute-start(f32[8,12,128]{2,1,0:T(8,128)S(1)} %get-tuple-element.12), channel_id=1, source_target_pairs={{0,8},{4,12},{16,24},{20,28},{32,40},{36,44},{48,56},{52,60},{64,7... | collective-permute-start | bytes 147464 | tf_op jit(solution)/shard_map/ppermute | solution.py:453
  11.5 10.3 %collective-permute-start.3 = (f32[8,12,128]{2,1,0:T(8,128)S(1)}, f32[8,12,128]{2,1,0:T(8,128)S(1)}, u32[]{:S(2)}, u32[]{:S(2)}) collective-permute-start(f32[8,12,128]{2,1,0:T(8,128)S(1)} %get-tuple-element.13), channel_id=1, source_target_pairs={{8,16},{12,20},{24,32},{28,36},{40,48},{44,52},{56,64},{60,68},{72... | collective-permute-start | bytes 147464 | tf_op jit(solution)/shard_map/ppermute | solution.py:453

commit v2 on v1

--- a/solution.py
+++ b/solution.py
@@ -14,6 +14,7 @@
 
 VMEM = pl.BlockSpec(memory_space=pltpu.VMEM)
 SMEM = pl.BlockSpec(memory_space=pltpu.SMEM)
+HBM = pl.BlockSpec(memory_space=pltpu.HBM)
 
 
 def lane_ids(rows):
@@ -74,7 +75,22 @@
     )
 
 
-def pack_kernel(counts, links, fields, near_a, near_b, far_a, far_b):
+def pack_kernel(counts_hbm, links_hbm, fields_hbm, near_a, near_b, far_a, far_b, counts, links, fields, sems):
+    copies = [
+        pltpu.make_async_copy(counts_hbm, counts, sems.at[0]),
+        pltpu.make_async_copy(links_hbm, links, sems.at[1]),
+    ]
+    for field in range(3):
+        for row in range(fields.shape[2]):
+            copies.append(
+                pltpu.make_async_copy(
+                    fields_hbm.at[field, 0, row], fields.at[field, 0, row], sems.at[len(copies)]
+                )
+            )
+    for copy in copies:
+        copy.start()
+    for copy in copies:
+        copy.wait()
     position = lax.axis_index("box")
     _, here, after, _ = offsets(counts, position)
     tiles = fields.shape[4] // LANES
@@ -144,19 +160,22 @@
     near_b,
     far_a,
     far_b,
-    smoothed,
-    residual,
+    red_out,
+    black_out,
+    red_left,
+    black_left,
     coarse,
     raw,
-    value,
-    coef,
+    red,
+    black,
+    red_coef,
+    black_coef,
     weight,
     source,
     diagonal,
-    defect,
     code,
-    stage,
 ):
+    value, coef = (red, black), (red_coef, black_coef)
     position = lax.axis_index("box")
     before, here, after, beyond = offsets(counts, position)
     tiles = fields.shape[4] // LANES
@@ -275,8 +294,8 @@
             for field, out in ((0, value), (2, coef)):
                 lo = raw[field, box, tile, pl.ds(0, PAIRS, 2), :]
                 hi = raw[field, box, tile, pl.ds(1, PAIRS, 2), :]
-                out[0, box, tile, FIRST : FIRST + PAIRS, :] = jnp.where(odd == 1, hi, lo)
-                out[1, box, tile, FIRST : FIRST + PAIRS, :] = jnp.where(odd == 1, lo, hi)
+                out[0][box, tile, FIRST : FIRST + PAIRS, :] = jnp.where(odd == 1, hi, lo)
+                out[1][box, tile, FIRST : FIRST + PAIRS, :] = jnp.where(odd == 1, lo, hi)
             lo = raw[1, box, tile, pl.ds(0, PAIRS, 2), :]
             hi = raw[1, box, tile, pl.ds(1, PAIRS, 2), :]
             source[0, box, tile] = jnp.where(odd == 1, hi, lo)
@@ -287,20 +306,20 @@
     mid = slice(FIRST, FIRST + PAIRS)
 
     def nearby(ref, colour, box, tile):
-        other = 1 - colour
-        here_ = ref[other, box, tile, mid, :]
-        there = ref[other, 1 - box, tile, mid, :]
+        ref = ref[1 - colour]
+        here_ = ref[box, tile, mid, :]
+        there = ref[1 - box, tile, mid, :]
         across = jnp.where(
             odd == colour,
-            ref[other, box, tile, FIRST - 1 : FIRST - 1 + PAIRS, :],
-            ref[other, box, tile, FIRST + 1 : FIRST + 1 + PAIRS, :],
+            ref[box, tile, FIRST - 1 : FIRST - 1 + PAIRS, :],
+            ref[box, tile, FIRST + 1 : FIRST + 1 + PAIRS, :],
         )
-        y_low = ref[other, box, (tile - 1) % tiles, mid, :]
+        y_low = ref[box, (tile - 1) % tiles, mid, :]
         if tile == 0:
-            y_low = jnp.where(code[box, 0] == 2, ref[other, 1 - box, tiles - 1, mid, :], y_low)
-        y_high = ref[other, box, (tile + 1) % tiles, mid, :]
+            y_low = jnp.where(code[box, 0] == 2, ref[1 - box, tiles - 1, mid, :], y_low)
+        y_high = ref[box, (tile + 1) % tiles, mid, :]
         if tile == tiles - 1:
-            y_high = jnp.where(code[box, 1] == 2, ref[other, 1 - box, 0, mid, :], y_high)
+            y_high = jnp.where(code[box, 1] == 2, ref[1 - box, 0, mid, :], y_high)
         z_low = jnp.where(code[box, 2] == 2, there, here_)
         z_high = jnp.where(code[box, 3] == 2, there, here_)
         return (
@@ -312,7 +331,7 @@
             jnp.where(depth == 31, pltpu.roll(z_high, 31, 1), pltpu.roll(here_, 127, 1)),
         )
 
-    def weigh(colour, carry):
+    for colour in range(2):
         for box in range(2):
             cut_low = jnp.logical_not(low_linked[box])
             cut_high = jnp.logical_not(high_linked[box])
@@ -321,7 +340,7 @@
             end = jnp.where(odd == colour, low_rows.astype(jnp.int32), high_rows.astype(jnp.int32)) == 1
             none = [code[box, k] == 0 for k in range(4)]
             for tile in range(tiles):
-                own = coef[colour, box, tile, mid, :]
+                own = coef[colour][box, tile, mid, :]
                 near = nearby(coef, colour, box, tile)
                 lost = (
                     end,
@@ -346,9 +365,6 @@
                 source[colour, box, tile] = source[colour, box, tile] * inverse
                 for d in range(6):
                     weight[colour, d, box, tile] = kept[d] * inverse
-        return carry
-
-    lax.fori_loop(0, 2, weigh, 0)
 
     def update(colour, box, tile):
         total = source[colour, box, tile]
@@ -357,42 +373,32 @@
         return total
 
     def sweep(step, carry):
-        colour = step & 1
-        for box in range(2):
-            for tile in range(tiles):
-                value[colour, box, tile, mid, :] = update(colour, box, tile)
+        for colour in range(2):
+            for box in range(2):
+                for tile in range(tiles):
+                    value[colour][box, tile, mid, :] = update(colour, box, tile)
         return carry
 
-    lax.fori_loop(0, 4, sweep, 0)
-
-    def remain(colour, carry):
-        for box in range(2):
-            for tile in range(tiles):
-                defect[colour, box, tile] = diagonal[colour, box, tile] * (
-                    update(colour, box, tile) - value[colour, box, tile, mid, :]
-                )
-        return carry
-
-    lax.fori_loop(0, 2, remain, 0)
+    lax.fori_loop(0, 2, sweep, 0)
 
     own_pairs = slice(PAIR_PAD, PAIR_PAD + 16)
     own_rows = slice(FIRST + PAIR_PAD, FIRST + PAIR_PAD + 16)
-    odd = odd_lanes(16)
     halves = tiles // 2
     gathered = []
     for half in range(2):
         for box in range(2):
             sums = []
             for tile in range(half * halves, (half + 1) * halves):
-                lanes = slice(tile * LANES, (tile + 1) * LANES)
-                for k, out, red, black in (
-                    (0, smoothed, value[0, box, tile, own_rows, :], value[1, box, tile, own_rows, :]),
-                    (1, residual, defect[0, box, tile, own_pairs, :], defect[1, box, tile, own_pairs, :]),
-                ):
-                    stage[k, box, tile, pl.ds(0, 16, 2), :] = jnp.where(odd == 1, black, red)
-                    stage[k, box, tile, pl.ds(1, 16, 2), :] = jnp.where(odd == 1, red, black)
-                    out[0, box, :, lanes] = stage[k, box, tile]
-                sums.append(red + black)
+                total = None
+                for colour, out, left in ((0, red_out, red_left), (1, black_out, black_left)):
+                    kept = value[colour][box, tile, own_rows, :]
+                    out[box, tile] = kept
+                    rest = diagonal[colour, box, tile, own_pairs, :] * (
+                        update(colour, box, tile)[own_pairs] - kept
+                    )
+                    left[box, tile] = rest
+                    total = rest if total is None else total + rest
+                sums.append(total)
             gathered.append(jnp.concatenate(sums, axis=1))
     whole = jnp.concatenate(gathered, axis=0)
     first = whole.astype(jnp.bfloat16)
@@ -414,16 +420,29 @@
         coarse[32 + 8 * box : 40 + 8 * box, :] = jnp.full((8, 2 * LANES), label.astype(jnp.float32))
 
 
-def place_kernel(got, source, out):
+def unpack_kernel(red, black, red_left, black_left, smoothed, residual, stage):
+    boxes, tiles = red.shape[:2]
+    odd = odd_lanes(red.shape[2])
+    for k, one, two, out in ((0, red, black, smoothed), (1, red_left, black_left, residual)):
+        for box in range(boxes):
+            for tile in range(tiles):
+                low, high = one[box, tile], two[box, tile]
+                stage[k, box, tile, pl.ds(0, 16, 2), :] = jnp.where(odd == 1, high, low)
+                stage[k, box, tile, pl.ds(1, 16, 2), :] = jnp.where(odd == 1, low, high)
+                out[0, box, :, tile * LANES : (tile + 1) * LANES] = stage[k, box, tile]
+
+
+def place_kernel(*refs):
+    *got, source, out = refs
     group = lax.axis_index("grp")
     base = (group * 16).astype(jnp.float32)
     for octant in range(16):
         kept = source[0, octant // 8, octant % 8]
-        for sender in range(got.shape[0]):
+        for sender in got:
             for box in range(2):
-                label = got[sender, 32 + 8 * box : 40 + 8 * box, :]
+                label = sender[32 + 8 * box : 40 + 8 * box, :]
                 mine = jnp.concatenate([label, label], axis=0) == base + float(octant)
-                kept = jnp.where(mine, got[sender, 16 * box : 16 * box + 16, :], kept)
+                kept = jnp.where(mine, sender[16 * box : 16 * box + 16, :], kept)
         out[0, octant // 8, octant % 8] = kept
 
 
@@ -438,12 +457,18 @@
     messages = pl.pallas_call(
         pack_kernel,
         out_shape=(near, near, far, far),
-        in_specs=[SMEM, SMEM, VMEM],
+        in_specs=[HBM] * 3,
         out_specs=(VMEM,) * 4,
+        scratch_shapes=[
+            pltpu.SMEM(old_count.shape, old_count.dtype),
+            pltpu.SMEM(neighbours.shape, neighbours.dtype),
+            pltpu.VMEM(old_fields.shape, f32),
+            pltpu.SemaphoreType.DMA((2 + 3 * old_fields.shape[2],)),
+        ],
         compiler_params=params,
         cost_estimate=pl.CostEstimate(flops=10**6, bytes_accessed=3 << 20, transcendentals=0),
         name="pack",
-    )(old_count, neighbours, old_fields)
+    )(*[pltpu.with_memory_space_constraint(x, pltpu.HBM) for x in (old_count, neighbours, old_fields)])
 
     def pairs(distance, shift):
         ids = [i for i in range(curve) if (i - shift) % (2 * distance) < distance and 0 <= i and i + distance < curve]
@@ -456,35 +481,52 @@
     boxes = neighbours.shape[1]
     fine = jax.ShapeDtypeStruct((1, boxes, box_edge, plane_cells), f32)
     packed = (2, boxes, tiles, PAIRS, LANES)
-    smoothed, residual, coarse = pl.pallas_call(
+    column = (boxes, tiles, PAIRS + 2 * FIRST, LANES)
+    half = jax.ShapeDtypeStruct((boxes, tiles, box_edge // 2, LANES), f32)
+    *halves, coarse = pl.pallas_call(
         smooth_kernel,
-        out_shape=(fine, fine, jax.ShapeDtypeStruct((48, 2 * LANES), f32)),
+        out_shape=(half, half, half, half, jax.ShapeDtypeStruct((48, 2 * LANES), f32)),
         in_specs=[SMEM, SMEM, SMEM] + [VMEM] * 5,
-        out_specs=(VMEM,) * 3,
+        out_specs=(VMEM,) * 5,
         scratch_shapes=[
             pltpu.VMEM((3, boxes, tiles, OWN + 2 * PAD, LANES), f32),
-            pltpu.VMEM((2, boxes, tiles, PAIRS + 2 * FIRST, LANES), f32),
-            pltpu.VMEM((2, boxes, tiles, PAIRS + 2 * FIRST, LANES), f32),
+            pltpu.VMEM(column, f32),
+            pltpu.VMEM(column, f32),
+            pltpu.VMEM(column, f32),
+            pltpu.VMEM(column, f32),
             pltpu.VMEM((2, 6, boxes, tiles, PAIRS, LANES), f32),
             pltpu.VMEM(packed, f32),
             pltpu.VMEM(packed, f32),
-            pltpu.VMEM(packed, f32),
             pltpu.VMEM((boxes, 4, PAIRS, LANES), f32),
-            pltpu.VMEM((2, boxes, tiles, OWN, LANES), f32),
         ],
         compiler_params=params,
         cost_estimate=pl.CostEstimate(flops=10**7, bytes_accessed=6 << 20, transcendentals=0),
         name="smooth",
     )(old_count, neighbours, parents, old_fields, *moved)
-    got = lax.all_gather(coarse, "grp")
+    groups = lax.axis_size("grp")
+    got = [coarse] + [
+        lax.ppermute(coarse, "grp", [(i, (i + k) % groups) for i in range(groups)])
+        for k in range(1, groups)
+    ]
+    smoothed, residual = pl.pallas_call(
+        unpack_kernel,
+        out_shape=(fine, fine),
+        in_specs=[VMEM] * 4,
+        out_specs=(VMEM,) * 2,
+        scratch_shapes=[pltpu.VMEM((2, boxes, tiles, OWN, LANES), f32)],
+        compiler_params=params,
+        cost_estimate=pl.CostEstimate(flops=10**6, bytes_accessed=3 << 20, transcendentals=0),
+        name="unpack",
+    )(*halves)
     coarse_rhs = pl.pallas_call(
         place_kernel,
         out_shape=jax.ShapeDtypeStruct(coarse_source.shape, f32),
-        in_specs=[VMEM, VMEM],
+        in_specs=[VMEM] * (groups + 1),
         out_specs=VMEM,
         compiler_params=params,
+        cost_estimate=pl.CostEstimate(flops=10**6, bytes_accessed=1 << 20, transcendentals=0),
         name="place",
-    )(got, coarse_source)
+    )(*got, coarse_source)
     return smoothed, residual, coarse_rhs
 
 

time: 42.8 us -> 35.2 us (0.82); the launches traced: 42.1 us -> 35.1 us
  blocking collectives: 5.59 us -> 0 us
  local copies, waits for them, and re-layouts: 2.74 us -> 0.02 us
  Pallas kernels: 10.2 us -> 7.51 us
  waiting for transfers between devices: 12.3 us -> 14.9 us
  starting transfers between devices: 10.6 us -> 11.9 us
    all_gather x1 -> x0, blocking collectives: 5.59 us -> none  [per_device(): got = lax.all_gather(coarse, 'grp')]
    unnamed x10, local copies, waits for them, and re-layouts: 2.74 us -> 0.02 us
    pallas_call x2 -> x3, Pallas kernels: 9.36 us -> 6.68 us  [the longest x1 4.06 us: per_device(): pl.pallas_call(smooth_kernel, out_shape=(half, half, half, half, jax.Shap...]
    ppermute x0 -> x3, waiting for transfers between devices: none -> 2.65 us  [per_device(): lax.ppermute(coarse, 'grp', [(i, (i + k) % groups) for i in range(groups)])]
    ppermute x0 -> x3, starting transfers between devices: none -> 1.29 us  [per_device(): lax.ppermute(coarse, 'grp', [(i, (i + k) % groups) for i in range(groups)])]
  transfers between devices with their start and end apart: 4 -> 7, of which waited for: 3 -> 5; matrix products, arithmetic and copies ran while one was open for 0% -> 0% of each run, Pallas kernels for 0% -> 2%
where the time goes in v2:
time: 35.2 us; the launch traced here: 35.1 us
  waiting for transfers between devices  14.9 us (42%)
  starting transfers between devices  11.9 us (34%)
  Pallas kernels  7.51 us (21%)
  between operations  0.73 us (2%)
    ppermute x4, waiting for transfers between devices, per_device(): lax.ppermute(message, 'box', pairs(distance, shift))  12.3 us
    ppermute x4, starting transfers between devices, per_device(): lax.ppermute(message, 'box', pairs(distance, shift))  10.6 us
    pallas_call x1, Pallas kernels, per_device(): pl.pallas_call(smooth_kernel, out_shape=(half, half, half, half, jax.Shap...  4.06 us
    ppermute x3, waiting for transfers between devices, per_device(): lax.ppermute(coarse, 'grp', [(i, (i + k) % groups) for i in range(groups)])  2.65 us
    pallas_call x1, Pallas kernels, per_device(): pl.pallas_call(pack_kernel, out_shape=(near, near, far, far), in_specs=[H...  1.78 us
    ppermute x3, starting transfers between devices, per_device(): lax.ppermute(coarse, 'grp', [(i, (i + k) % groups) for i in range(groups)])  1.29 us
    pallas_call x1, Pallas kernels, per_device(): pl.pallas_call(unpack_kernel, out_shape=(fine, fine), in_specs=[VMEM] * 4...  0.85 us
    pallas_call x1, Pallas kernels, per_device(): pl.pallas_call(place_kernel, out_shape=jax.ShapeDtypeStruct(coarse_source...  0.83 us
  transfers between devices with their start and end apart: 7, of which 5 were waited for; matrix products, arithmetic and copies ran while one was open for 0% of the time, Pallas kernels for 2%

profile of v2, /device:TPU:128, one launch (start us, length us, event | category | flops | bytes accessed | tf_op | source)
XLA Modules:
  0.0 35.1 jit_solution(15416749541818470010)
XLA Ops:
  0.6 0.0 copy-start.2
  0.6 0.0 copy-start.3
  0.7 0.0 copy-start
  0.7 0.0 copy-start.4
  0.7 1.8 %pack.1 = (f32[8,104,128]{2,1,0:T(8,128)S(1)}, f32[8,104,128]{2,1,0:T(8,128)S(1)}, f32[8,12,128]{2,1,0:T(8,128)S(1)}, f32[8,12,128]{2,1,0:T(8,128)S(1)}) custom-call(s32[1,64]{1,0:T(1,128)} %counts.1, s32[1,2,6]{2,1,0:T(2,128)} %links.1, f32[3,1,4,32,1024]{4,3,2,1,0:T(8,128)} %fields.1), custom_call_target="tpu_custom_call" | custom-call | flops 1000000 | bytes 3145728 | tf_op jit(solution)/shard_map/pack/pallas_call | solution.py:457
  2.5 0.0 copy-start.1
  2.5 3.3 %collective-permute-start = (f32[8,104,128]{2,1,0:T(8,128)S(1)}, f32[8,104,128]{2,1,0:T(8,128)S(1)}, u32[]{:S(2)}, u32[]{:S(2)}) collective-permute-start(f32[8,104,128]{2,1,0:T(8,128)S(1)} %get-tuple-element.14), channel_id=1, source_target_pairs={{0,4},{8,12},{16,20},{24,28},{32,36},{40,44},{48,52},{56,60},{64,6... | collective-permute-start | bytes 1277960 | tf_op jit(solution)/shard_map/ppermute | solution.py:478
  5.7 4.0 %collective-permute-start.1 = (f32[8,104,128]{2,1,0:T(8,128)S(1)}, f32[8,104,128]{2,1,0:T(8,128)S(1)}, u32[]{:S(2)}, u32[]{:S(2)}) collective-permute-start(f32[8,104,128]{2,1,0:T(8,128)S(1)} %get-tuple-element.15), channel_id=1, source_target_pairs={{4,8},{12,16},{20,24},{28,32},{36,40},{44,48},{52,56},{60,64},{68,... | collective-permute-start | bytes 1277960 | tf_op jit(solution)/shard_map/ppermute | solution.py:478
  9.7 0.1 collective-permute-start.2
  9.8 3.2 %collective-permute-start.3 = (f32[8,12,128]{2,1,0:T(8,128)S(1)}, f32[8,12,128]{2,1,0:T(8,128)S(1)}, u32[]{:S(2)}, u32[]{:S(2)}) collective-permute-start(f32[8,12,128]{2,1,0:T(8,128)S(1)} %get-tuple-element.17), channel_id=1, source_target_pairs={{8,16},{12,20},{24,32},{28,36},{40,48},{44,52},{56,64},{60,68},{72... | collective-permute-start | bytes 147464 | tf_op jit(solution)/shard_map/ppermute | solution.py:478
  13.1 7.0 %collective-permute-done.2.far_a = f32[8,12,128]{2,1,0:T(8,128)S(1)} collective-permute-done((f32[8,12,128]{2,1,0:T(8,128)S(1)}, f32[8,12,128]{2,1,0:T(8,128)S(1)}, u32[]{:S(2)}, u32[]{:S(2)}) %collective-permute-start.2) | collective-permute-done | bytes 49184 | tf_op jit(solution)/shard_map/ppermute | solution.py:478
  20.1 0.0 collective-permute-done.3.far_b
  20.1 3.8 %collective-permute-done.near_a = f32[8,104,128]{2,1,0:T(8,128)S(1)} collective-permute-done((f32[8,104,128]{2,1,0:T(8,128)S(1)}, f32[8,104,128]{2,1,0:T(8,128)S(1)}, u32[]{:S(2)}, u32[]{:S(2)}) %collective-permute-start) | collective-permute-done | bytes 426016 | tf_op jit(solution)/shard_map/ppermute | solution.py:478
  23.9 1.4 %collective-permute-done.1.near_b = f32[8,104,128]{2,1,0:T(8,128)S(1)} collective-permute-done((f32[8,104,128]{2,1,0:T(8,128)S(1)}, f32[8,104,128]{2,1,0:T(8,128)S(1)}, u32[]{:S(2)}, u32[]{:S(2)}) %collective-permute-start.1) | collective-permute-done | bytes 426016 | tf_op jit(solution)/shard_map/ppermute | solution.py:478
  25.4 0.0 copy-done.2
  25.4 0.0 copy-done.3
  25.4 0.0 copy-done
  25.4 0.0 copy-done.4
  25.4 4.1 %smooth.1 = (f32[2,8,16,128]{3,2,1,0:T(8,128)S(1)}, f32[2,8,16,128]{3,2,1,0:T(8,128)S(1)}, f32[2,8,16,128]{3,2,1,0:T(8,128)S(1)}, f32[2,8,16,128]{3,2,1,0:T(8,128)S(1)}, f32[48,256]{1,0:T(8,128)S(1)}) custom-call(s32[1,64]{1,0:T(1,128)S(1)} %copy-done.3, s32[1,2,6]{2,1,0:T(2,128)S(1)} %copy-done.2, s32[1,2,3]{2,1,0:T(2,128)S(1)} %copy-done.4, ...), custom_call_target="tpu_custom_call" | custom-call | flops 10000000 | bytes 6291456 | tf_op jit(solution)/shard_map/smooth/pallas_call | solution.py:486
  29.5 0.1 collective-permute-start.6
  29.5 1.1 %collective-permute-start.5 = (f32[48,256]{1,0:T(8,128)S(1)}, f32[48,256]{1,0:T(8,128)S(1)}, u32[]{:S(2)}, u32[]{:S(2)}) collective-permute-start(f32[48,256]{1,0:T(8,128)S(1)} %get-tuple-element.24.refs_0_), channel_id=1, source_target_pairs={{0,2},{1,3},{2,0},{3,1},{4,6},{5,7},{6,4},{7,5},{8,10},{9,11},{10,... | collective-permute-start | bytes 147464 | tf_op jit(solution)/shard_map/ppermute | solution.py:508
  30.6 0.1 collective-permute-start.4
  30.8 0.8 %unpack.1 = (f32[1,2,32,1024]{3,2,1,0:T(8,128)}, f32[1,2,32,1024]{3,2,1,0:T(8,128)}) custom-call(f32[2,8,16,128]{3,2,1,0:T(8,128)S(1)} %get-tuple-element.18.red, f32[2,8,16,128]{3,2,1,0:T(8,128)S(1)} %get-tuple-element.19.black, f32[2,8,16,128]{3,2,1,0:T(8,128)S(1)} %get-tuple-element.20.red_left, f32[2,8,16,128]{3,2,1,0:T(8,128)S(1)} %get-tuple-element.21.black_left), custom_call_target="tpu_custom_call" | custom-call | flops 1000000 | bytes 3145728 | tf_op jit(solution)/shard_map/unpack/pallas_call | solution.py:511
  31.6 0.0 collective-permute-done.6.refs_3_
  31.6 2.3 %collective-permute-done.5.refs_2_ = f32[48,256]{1,0:T(8,128)S(1)} collective-permute-done((f32[48,256]{1,0:T(8,128)S(1)}, f32[48,256]{1,0:T(8,128)S(1)}, u32[]{:S(2)}, u32[]{:S(2)}) %collective-permute-start.5) | collective-permute-done | bytes 49184 | tf_op jit(solution)/shard_map/ppermute | solution.py:508
  33.9 0.3 collective-permute-done.4.refs_1_
  34.3 0.0 copy-done.1
  34.3 0.8 %place.1 = f32[1,2,8,16,256]{4,3,2,1,0:T(8,128)} custom-call(f32[48,256]{1,0:T(8,128)S(1)} %get-tuple-element.24.refs_0_, f32[48,256]{1,0:T(8,128)S(1)} %collective-permute-done.4.refs_1_, f32[48,256]{1,0:T(8,128)S(1)} %collective-permute-done.5.refs_2_, f32[48,256]{1,0:T(8,128)S(1)} %collective-permute-done.6.refs_3_, f32[1,2,8,16,256]{4,3,2,1,0:T(8,128)S(1)} %copy-done.1), custom_call_target="tpu_custom_call" | custom-call | flops 1000000 | bytes 1048576 | tf_op jit(solution)/shard_map/place/pallas_call | solution.py:521
Async XLA Ops:
  0.6 24.7 %copy-start.2 = (s32[1,2,6]{2,1,0:T(2,128)S(1)}, s32[1,2,6]{2,1,0:T(2,128)}, u32[]{:S(2)}) copy-start(s32[1,2,6]{2,1,0:T(2,128)} %links.1) | copy-start | bytes 148
  0.6 24.7 %copy-start.3 = (s32[1,64]{1,0:T(1,128)S(1)}, s32[1,64]{1,0:T(1,128)}, u32[]{:S(2)}) copy-start(s32[1,64]{1,0:T(1,128)} %counts.1) | copy-start | bytes 772
  0.7 24.7 %copy-start = (f32[3,1,4,32,1024]{4,3,2,1,0:T(8,128)S(1)}, f32[3,1,4,32,1024]{4,3,2,1,0:T(8,128)}, u32[]{:S(2)}) copy-start(f32[3,1,4,32,1024]{4,3,2,1,0:T(8,128)} %fields.1) | copy-start | bytes 4718596
  0.7 24.7 %copy-start.4 = (s32[1,2,3]{2,1,0:T(2,128)S(1)}, s32[1,2,3]{2,1,0:T(2,128)}, u32[]{:S(2)}) copy-start(s32[1,2,3]{2,1,0:T(2,128)} %parents.1) | copy-start | bytes 76
  2.5 31.8 %copy-start.1 = (f32[1,2,8,16,256]{4,3,2,1,0:T(8,128)S(1)}, f32[1,2,8,16,256]{4,3,2,1,0:T(8,128)}, u32[]{:S(2)}) copy-start(f32[1,2,8,16,256]{4,3,2,1,0:T(8,128)} %refs_4_.1) | copy-start | bytes 786436
  2.5 21.5 %collective-permute-start = (f32[8,104,128]{2,1,0:T(8,128)S(1)}, f32[8,104,128]{2,1,0:T(8,128)S(1)}, u32[]{:S(2)}, u32[]{:S(2)}) collective-permute-start(f32[8,104,128]{2,1,0:T(8,128)S(1)} %get-tuple-element.14), channel_id=1, source_target_pairs={{0,4},{8,12},{16,20},{24,28},{32,36},{40,44},{48,52},{56,60},{64,6... | collective-permute-start | bytes 1277960 | tf_op jit(solution)/shard_map/ppermute | solution.py:478
  5.7 19.6 %collective-permute-start.1 = (f32[8,104,128]{2,1,0:T(8,128)S(1)}, f32[8,104,128]{2,1,0:T(8,128)S(1)}, u32[]{:S(2)}, u32[]{:S(2)}) collective-permute-start(f32[8,104,128]{2,1,0:T(8,128)S(1)} %get-tuple-element.15), channel_id=1, source_target_pairs={{4,8},{12,16},{20,24},{28,32},{36,40},{44,48},{52,56},{60,64},{68,... | collective-permute-start | bytes 1277960 | tf_op jit(solution)/shard_map/ppermute | solution.py:478
  9.7 10.4 %collective-permute-start.2 = (f32[8,12,128]{2,1,0:T(8,128)S(1)}, f32[8,12,128]{2,1,0:T(8,128)S(1)}, u32[]{:S(2)}, u32[]{:S(2)}) collective-permute-start(f32[8,12,128]{2,1,0:T(8,128)S(1)} %get-tuple-element.16), channel_id=1, source_target_pairs={{0,8},{4,12},{16,24},{20,28},{32,40},{36,44},{48,56},{52,60},{64,7... | collective-permute-start | bytes 147464 | tf_op jit(solution)/shard_map/ppermute | solution.py:478
  9.8 10.3 %collective-permute-start.3 = (f32[8,12,128]{2,1,0:T(8,128)S(1)}, f32[8,12,128]{2,1,0:T(8,128)S(1)}, u32[]{:S(2)}, u32[]{:S(2)}) collective-permute-start(f32[8,12,128]{2,1,0:T(8,128)S(1)} %get-tuple-element.17), channel_id=1, source_target_pairs={{8,16},{12,20},{24,32},{28,36},{40,48},{44,52},{56,64},{60,68},{72... | collective-permute-start | bytes 147464 | tf_op jit(solution)/shard_map/ppermute | solution.py:478
  29.5 2.1 %collective-permute-start.6 = (f32[48,256]{1,0:T(8,128)S(1)}, f32[48,256]{1,0:T(8,128)S(1)}, u32[]{:S(2)}, u32[]{:S(2)}) collective-permute-start(f32[48,256]{1,0:T(8,128)S(1)} %get-tuple-element.24.refs_0_), channel_id=1, source_target_pairs={{0,3},{1,0},{2,1},{3,2},{4,7},{5,4},{6,5},{7,6},{8,11},{9,8},{10,9... | collective-permute-start | bytes 147464 | tf_op jit(solution)/shard_map/ppermute | solution.py:508
  29.5 4.4 %collective-permute-start.5 = (f32[48,256]{1,0:T(8,128)S(1)}, f32[48,256]{1,0:T(8,128)S(1)}, u32[]{:S(2)}, u32[]{:S(2)}) collective-permute-start(f32[48,256]{1,0:T(8,128)S(1)} %get-tuple-element.24.refs_0_), channel_id=1, source_target_pairs={{0,2},{1,3},{2,0},{3,1},{4,6},{5,7},{6,4},{7,5},{8,10},{9,11},{10,... | collective-permute-start | bytes 147464 | tf_op jit(solution)/shard_map/ppermute | solution.py:508
  30.6 3.6 %collective-permute-start.4 = (f32[48,256]{1,0:T(8,128)S(1)}, f32[48,256]{1,0:T(8,128)S(1)}, u32[]{:S(2)}, u32[]{:S(2)}) collective-permute-start(f32[48,256]{1,0:T(8,128)S(1)} %get-tuple-element.24.refs_0_), channel_id=1, source_target_pairs={{0,1},{1,2},{2,3},{3,0},{4,5},{5,6},{6,7},{7,4},{8,9},{9,10},{10,1... | collective-permute-start | bytes 147464 | tf_op jit(solution)/shard_map/ppermute | solution.py:508

commit v3 on v2

v3 whole, which is shorter than its diff:
```python
import jax
import jax.numpy as jnp
from jax import lax
from jax.experimental import pallas as pl
from jax.experimental.pallas import tpu as pltpu
from jax.sharding import PartitionSpec as P

MASS_TERM = 0.25
LANES = 128
PAD, PAIR_PAD = 8, 4
OWN, PAIRS, FIRST = 32, 24, 8
TILES = 8
SIDE_END, VALUE_END = 8, 2
SIDE = OWN * TILES
SIDE_ENDS = SIDE + OWN * TILES
LINKS = SIDE_ENDS + 2 * SIDE_END * TILES
FIRST_ROWS = LINKS + 8
VALUE_ENDS = OWN // 2 * TILES
REST_ROWS = VALUE_ENDS + 2 * VALUE_END * TILES
FAR_VALUES = SIDE_END * TILES
FAR_ROWS = FAR_VALUES + VALUE_END * TILES

VMEM = pl.BlockSpec(memory_space=pltpu.VMEM)
SMEM = pl.BlockSpec(memory_space=pltpu.SMEM)
HBM = pl.BlockSpec(memory_space=pltpu.HBM)


def lane_ids(rows):
    return lax.broadcasted_iota(jnp.int32, (rows, LANES), 1)


def row_ids(rows):
    return lax.broadcasted_iota(jnp.int32, (rows, LANES), 0)


def odd_lanes(rows):
    lane = lane_ids(rows)
    return ((lane >> 5) + lane) & 1


def offsets(counts, position):
    count = counts.shape[1]
    start = jnp.int32(0)
    for j in range(count):
        start = start + jnp.where(j < position, counts[0, j], 0)
    here = start - 2 * position
    after = here + counts[0, position] - 2
    before = here - counts[0, jnp.maximum(position - 1, 0)] + 2
    beyond = after + counts[0, jnp.minimum(position + 1, count - 1)] - 2
    return before, here, after, beyond


def link_code(links, box, face, first_box):
    target = links[0, box, face]
    return jnp.where(target < 0, 0, jnp.where(target - first_box == box, 1, 2))


def swap_depth(cells):
    odd = lane_ids(cells.shape[0]) & 1
    return jnp.where(odd == 1, pltpu.roll(cells, 1, 1), pltpu.roll(cells, LANES - 1, 1))


def end_tiles(fields, row, tile, upper):
    lanes = slice(tile * LANES, (tile + 1) * LANES)
    rows = slice(OWN - 8, OWN) if upper else slice(0, 8)
    return [fields[field, 0, row, rows, lanes] for field in range(3)]


def side_end(fields, row, tile, upper):
    sol, rhs, coef = end_tiles(fields, row, tile, upper)
    towards = 1 if upper else 7
    next_coef = pltpu.roll(coef, towards, 0)
    folded = rhs + 0.5 * (coef + next_coef) * pltpu.roll(sol, towards, 0)
    mixed = jnp.where(odd_lanes(8) == int(not upper), folded, swap_depth(next_coef))
    side = jnp.where(row_ids(8) == (4 if upper else 3), mixed, rhs)
    rows = slice(4, 8) if upper else slice(0, 4)
    return coef[rows], side[rows]


def value_end(fields, row, tile, upper):
    sol, _, _ = end_tiles(fields, row, tile, upper)
    packed = jnp.where(odd_lanes(8) == 1, sol, pltpu.roll(sol, 7, 0))
    return (packed[4:5], packed[6:7]) if upper else (packed[0:1], packed[2:3])


def store_rows(out, base, pieces):
    for piece in pieces:
        out[base : base + piece.shape[0], :] = piece
        base += piece.shape[0]


def load_rows(ref, base, sizes):
    pieces = []
    for size in sizes:
        pieces.append(ref[base : base + size, :])
        base += size
    return tuple(pieces)


SIDE_SIZES, VALUE_SIZES = (4, 4), (1, 1)


def slots(here):
    return (jnp.maximum(-here, 0), 1 - here), jnp.minimum(2 - here, 3)


def pack_first_kernel(counts_hbm, links_hbm, fields_hbm, near_a, near_b, shifts, counts, links, fields, sems):
    copies = []

    def fetch(source, target):
        copies.append(pltpu.make_async_copy(source, target, sems.at[len(copies)]))

    fetch(counts_hbm, counts)
    fetch(links_hbm, links)
    for row in range(fields.shape[2]):
        for field in (2, 1):
            fetch(fields_hbm.at[field, 0, row], fields.at[field, 0, row])
    for row in range(3):
        for rows in (pl.ds(0, 8), pl.ds(OWN - 8, 8)):
            fetch(fields_hbm.at[0, 0, row, rows], fields.at[0, 0, row, rows])
    for copy in copies:
        copy.start()
    for copy in copies:
        copy.wait()
    position = lax.axis_index("box")
    found = offsets(counts, position)
    for k in range(4):
        shifts[k] = found[k]
    here = found[1]
    held, move_up = slots(here)
    codes = jnp.zeros((8, LANES), jnp.float32)
    for box in range(2):
        for face in range(2, 6):
            mine = (row_ids(8) == box) & (lane_ids(8) == face - 2)
            codes = jnp.where(mine, link_code(links, box, face, 2 * position).astype(jnp.float32), codes)

    def message(out, upper):
        row = move_up if upper else 0
        for tile in range(TILES):
            lanes = slice(tile * LANES, (tile + 1) * LANES)
            out[OWN * tile : OWN * (tile + 1), :] = fields[2, 0, row, :, lanes]
            out[SIDE + OWN * tile : SIDE + OWN * (tile + 1), :] = fields[1, 0, row, :, lanes]
            for box in range(2):
                store_rows(
                    out, SIDE_ENDS + SIDE_END * (2 * tile + box), side_end(fields, held[box], tile, upper)
                )
        out[LINKS : LINKS + 8, :] = codes

    even = position % 2 == 0

    @pl.when(even)
    def _():
        message(near_a, True)
        message(near_b, False)

    @pl.when(jnp.logical_not(even))
    def _():
        message(near_a, False)
        message(near_b, True)


def pack_rest_kernel(shifts, fields, near_a, near_b, far_a, far_b):
    position = lax.axis_index("box")
    here = shifts[1]
    held, move_up = slots(here)

    def message(out, upper):
        row = move_up if upper else 0
        mixed = (row_ids(16) + odd_lanes(16)) & 1
        for tile in range(TILES):
            lanes = slice(tile * LANES, (tile + 1) * LANES)
            low = fields[0, 0, row, 0:16, lanes]
            high = pltpu.roll(fields[0, 0, row, 16:32, lanes], 15, 0)
            out[16 * tile : 16 * tile + 16, :] = jnp.where(mixed == 1, low, high)
            for box in range(2):
                store_rows(
                    out, VALUE_ENDS + VALUE_END * (2 * tile + box), value_end(fields, held[box], tile, upper)
                )

    def far_message(out, upper):
        row = move_up if upper else 0
        for tile in range(TILES):
            store_rows(out, SIDE_END * tile, side_end(fields, row, tile, upper))
            store_rows(out, FAR_VALUES + VALUE_END * tile, value_end(fields, row, tile, upper))

    even = position % 2 == 0
    lower = position % 4 < 2

    @pl.when(lower)
    def _():
        far_message(far_a, True)
        far_message(far_b, False)

    @pl.when(jnp.logical_not(lower))
    def _():
        far_message(far_a, False)
        far_message(far_b, True)

    @pl.when(even)
    def _():
        message(near_a, True)
        message(near_b, False)

    @pl.when(jnp.logical_not(even))
    def _():
        message(near_a, False)
        message(near_b, True)


def choose(flag, one, other):
    return tuple(jnp.where(flag, a, b) for a, b in zip(one, other, strict=True))


def crossing(links, face, run_first):
    ids = [links[0, box, face] for box in range(2)]
    linked = [one >= 0 for one in ids]
    swap = jnp.where(linked[0], ids[0] - run_first == 1, linked[1] & (ids[1] - run_first == 0))
    return linked, swap


def neighbour_ends(offset, even, lower, swaps, fields, near, far, tile, start, far_start, sizes, local):
    before, here, after, beyond = offset
    near_a, near_b = near
    far_a, far_b = far
    at = [start + sum(sizes) * (2 * tile + i) for i in range(2)]
    far_at = far_start + sum(sizes) * tile
    below = [choose(even, load_rows(near_b, at[i], sizes), load_rows(near_a, at[i], sizes)) for i in range(2)]
    above = [choose(even, load_rows(near_a, at[i], sizes), load_rows(near_b, at[i], sizes)) for i in range(2)]
    far_below = choose(lower, load_rows(far_b, far_at, sizes), load_rows(far_a, far_at, sizes))
    far_above = choose(lower, load_rows(far_a, far_at, sizes), load_rows(far_b, far_at, sizes))
    below = (choose(before == 1, far_below, below[0]), choose(here == -1, local(fields, 0, tile, True), below[1]))
    above = (
        choose(after == 1, local(fields, jnp.minimum(2 - here, 3), tile, False), above[0]),
        choose(beyond == -1, far_above, above[1]),
    )
    return [
        (choose(swaps[0], below[1 - box], below[box]), choose(swaps[1], above[1 - box], above[box]))
        for box in range(2)
    ]


def place_own(here, after, even, place_local, place_moved, near):
    from_below = here == 1
    from_above = after == -1
    held = slots(here)[0]
    for box, moved, first, second in ((0, from_below, near[1], near[0]), (1, from_above, near[0], near[1])):

        @pl.when(jnp.logical_not(moved))
        def _(box=box):
            place_local(box, held[box])

        @pl.when(moved & even)
        def _(box=box, ref=first):
            place_moved(box, ref)

        @pl.when(moved & jnp.logical_not(even))
        def _(box=box, ref=second):
            place_moved(box, ref)


def split_colours(raw, box, tile):
    odd = odd_lanes(PAIRS)
    low = raw[box, tile, pl.ds(0, PAIRS, 2), :]
    high = raw[box, tile, pl.ds(1, PAIRS, 2), :]
    return jnp.where(odd == 1, high, low), jnp.where(odd == 1, low, high)


def nearby(ref, code, colour, box, tile):
    mid = slice(FIRST, FIRST + PAIRS)
    lane = lane_ids(PAIRS)
    depth = lane & 31
    ref = ref[1 - colour]
    here_ = ref[box, tile, mid, :]
    there = ref[1 - box, tile, mid, :]
    across = jnp.where(
        odd_lanes(PAIRS) == colour,
        ref[box, tile, FIRST - 1 : FIRST - 1 + PAIRS, :],
        ref[box, tile, FIRST + 1 : FIRST + 1 + PAIRS, :],
    )
    y_low = ref[box, (tile - 1) % TILES, mid, :]
    if tile == 0:
        y_low = jnp.where(code[box, 0] == 2, ref[1 - box, TILES - 1, mid, :], y_low)
    y_high = ref[box, (tile + 1) % TILES, mid, :]
    if tile == TILES - 1:
        y_high = jnp.where(code[box, 1] == 2, ref[1 - box, 0, mid, :], y_high)
    z_low = jnp.where(code[box, 2] == 2, there, here_)
    z_high = jnp.where(code[box, 3] == 2, there, here_)
    return (
        across,
        here_,
        pltpu.roll(jnp.where(lane >= 96, y_low, here_), 32, 1),
        pltpu.roll(jnp.where(lane < 32, y_high, here_), 96, 1),
        jnp.where(depth == 0, pltpu.roll(z_low, 97, 1), pltpu.roll(here_, 1, 1)),
        jnp.where(depth == 31, pltpu.roll(z_high, 31, 1), pltpu.roll(here_, 127, 1)),
    )


def weigh_kernel(
    shifts,
    links,
    fields,
    near_a,
    near_b,
    far_a,
    far_b,
    weight,
    source,
    diagonal,
    code,
    raw,
    raw_side,
    red_coef,
    black_coef,
):
    coef = (red_coef, black_coef)
    position = lax.axis_index("box")
    offset = [shifts[k] for k in range(4)]
    _, here, after, _ = offset
    first_box = 2 * position
    even = position % 2 == 0
    lower = position % 4 < 2

    def place_local(box, row):
        for tile in range(TILES):
            lanes = slice(tile * LANES, (tile + 1) * LANES)
            raw[box, tile, PAD : PAD + OWN, :] = fields[2, 0, row, :, lanes]
            raw_side[box, tile, PAD : PAD + OWN, :] = fields[1, 0, row, :, lanes]

    def place_moved(box, ref):
        for tile in range(TILES):
            raw[box, tile, PAD : PAD + OWN, :] = ref[OWN * tile : OWN * (tile + 1), :]
            raw_side[box, tile, PAD : PAD + OWN, :] = ref[SIDE + OWN * tile : SIDE + OWN * (tile + 1), :]

    place_own(here, after, even, place_local, place_moved, (near_a, near_b))
    low_linked, low_swap = crossing(links, 0, first_box - 2)
    high_linked, high_swap = crossing(links, 1, first_box + 2)
    ones = jnp.ones((8, LANES), jnp.float32)
    odd = odd_lanes(1)
    for tile in range(TILES):
        ends = neighbour_ends(
            offset, even, lower, (low_swap, high_swap), fields, (near_a, near_b), (far_a, far_b), tile,
            SIDE_ENDS, 0, SIDE_SIZES, side_end,
        )
        for box in range(2):
            (below, side_below), (above, side_above) = ends[box]
            for one in (raw, raw_side):
                one[box, tile, 0:8, :] = ones
                one[box, tile, PAD + OWN : PAD + OWN + 8, :] = ones
            raw[box, tile, 3:4, :] = jnp.where(odd == 0, swap_depth(side_below[0:1]), below[0:1])
            raw[box, tile, 4:8, :] = below
            raw_side[box, tile, 4:8, :] = side_below
            raw[box, tile, 40:44, :] = above
            raw[box, tile, 44:45, :] = jnp.where(odd == 1, swap_depth(side_above[3:4]), above[3:4])
            raw_side[box, tile, 40:44, :] = side_above

    pair = row_ids(PAIRS)
    tile_a, tile_b = near_a[LINKS : LINKS + 8, :], near_b[LINKS : LINKS + 8, :]
    codes_below, codes_above = jnp.where(even, tile_b, tile_a), jnp.where(even, tile_a, tile_b)
    for face in range(4):
        spread = [
            [jnp.broadcast_to(one[i : i + 1, face : face + 1], (PAIRS, LANES)) for i in range(2)]
            for one in (codes_below, codes_above)
        ]
        for box in range(2):
            below = jnp.where(low_swap, spread[0][1 - box], spread[0][box])
            above = jnp.where(high_swap, spread[1][1 - box], spread[1][box])
            own = link_code(links, box, face + 2, first_box).astype(jnp.float32)
            code[box, face] = jnp.where(
                pair < PAIR_PAD, below, jnp.where(pair < PAIR_PAD + 16, own, above)
            )

    odd = odd_lanes(PAIRS)
    lane = lane_ids(PAIRS)
    depth = lane & 31
    mid = slice(FIRST, FIRST + PAIRS)
    for box in range(2):
        for tile in range(TILES):
            red_coef[box, tile, mid, :], black_coef[box, tile, mid, :] = split_colours(raw, box, tile)
            source[0, box, tile], source[1, box, tile] = split_colours(raw_side, box, tile)

    for colour in range(2):
        for box in range(2):
            cut_low = jnp.logical_not(low_linked[box])
            cut_high = jnp.logical_not(high_linked[box])
            low_rows = ((pair == PAIR_PAD) & cut_low) | ((pair == PAIR_PAD + 16) & cut_high)
            high_rows = ((pair == PAIR_PAD + 15) & cut_high) | ((pair == PAIR_PAD - 1) & cut_low)
            end = jnp.where(odd == colour, low_rows.astype(jnp.int32), high_rows.astype(jnp.int32)) == 1
            none = [code[box, k] == 0 for k in range(4)]
            for tile in range(TILES):
                own = coef[colour][box, tile, mid, :]
                near = nearby(coef, code, colour, box, tile)
                lost = (
                    end,
                    None,
                    (lane < 32) & none[0] if tile == 0 else None,
                    (lane >= 96) & none[1] if tile == TILES - 1 else None,
                    (depth == 0) & none[2],
                    (depth == 31) & none[3],
                )
                total = jnp.full((PAIRS, LANES), MASS_TERM, jnp.float32)
                kept = []
                for one, gone in zip(near, lost, strict=True):
                    if gone is None:
                        w = 0.5 * (own + one)
                        kept.append(w)
                    else:
                        w = 0.5 * (own + jnp.where(gone, own, one))
                        kept.append(jnp.where(gone, 0.0, w))
                    total = total + w
                inverse = 1.0 / total
                diagonal[colour, box, tile] = total
                source[colour, box, tile] = source[colour, box, tile] * inverse
                for d in range(6):
                    weight[colour, d, box, tile] = kept[d] * inverse


def smooth_kernel(
    shifts,
    links,
    parents,
    fields,
    near_a,
    near_b,
    far_a,
    far_b,
    weight,
    source,
    diagonal,
    code,
    red_out,
    black_out,
    red_left,
    black_left,
    coarse,
    raw,
    red,
    black,
):
    value = (red, black)
    position = lax.axis_index("box")
    offset = [shifts[k] for k in range(4)]
    _, here, after, _ = offset
    first_box = 2 * position
    even = position % 2 == 0
    lower = position % 4 < 2

    def place_local(box, row):
        for tile in range(TILES):
            raw[box, tile, PAD : PAD + OWN, :] = fields[0, 0, row, :, tile * LANES : (tile + 1) * LANES]

    def place_moved(box, ref):
        for tile in range(TILES):
            packed = ref[16 * tile : 16 * tile + 16, :]
            raw[box, tile, PAD : PAD + 16, :] = packed
            raw[box, tile, PAD + 16 : PAD + 32, :] = pltpu.roll(packed, 1, 0)

    place_own(here, after, even, place_local, place_moved, (near_a, near_b))
    swaps = (crossing(links, 0, first_box - 2)[1], crossing(links, 1, first_box + 2)[1])
    zeros = jnp.zeros((8, LANES), jnp.float32)
    for tile in range(TILES):
        ends = neighbour_ends(
            offset, even, lower, swaps, fields, (near_a, near_b), (far_a, far_b), tile,
            VALUE_ENDS, FAR_VALUES, VALUE_SIZES, value_end,
        )
        for box in range(2):
            raw[box, tile, 0:8, :] = zeros
            raw[box, tile, PAD + OWN : PAD + OWN + 8, :] = zeros
            for base, pieces in zip((4, PAD + OWN), ends[box], strict=True):
                for k in range(4):
                    raw[box, tile, base + k : base + k + 1, :] = pieces[k // 2]

    mid = slice(FIRST, FIRST + PAIRS)
    for box in range(2):
        for tile in range(TILES):
            red[box, tile, mid, :], black[box, tile, mid, :] = split_colours(raw, box, tile)

    def update(colour, box, tile):
        total = source[colour, box, tile]
        for d, one in enumerate(nearby(value, code, colour, box, tile)):
            total = total + weight[colour, d, box, tile] * one
        return total

    def sweep(step, carry):
        for colour in range(2):
            for box in range(2):
                for tile in range(TILES):
                    value[colour][box, tile, mid, :] = update(colour, box, tile)
        return carry

    lax.fori_loop(0, 2, sweep, 0)

    own_pairs = slice(PAIR_PAD, PAIR_PAD + 16)
    own_rows = slice(FIRST + PAIR_PAD, FIRST + PAIR_PAD + 16)
    halves = TILES // 2
    gathered = []
    for half in range(2):
        for box in range(2):
            sums = []
            for tile in range(half * halves, (half + 1) * halves):
                total = None
                for colour, out, left in ((0, red_out, red_left), (1, black_out, black_left)):
                    kept = value[colour][box, tile, own_rows, :]
                    out[box, tile] = kept
                    rest = diagonal[colour, box, tile, own_pairs, :] * (
                        update(colour, box, tile)[own_pairs] - kept
                    )
                    left[box, tile] = rest
                    total = rest if total is None else total + rest
                sums.append(total)
            gathered.append(jnp.concatenate(sums, axis=1))
    whole = jnp.concatenate(gathered, axis=0)
    first = whole.astype(jnp.bfloat16)
    rest = whole - first.astype(jnp.float32)
    second = rest.astype(jnp.bfloat16)
    third = (rest - second.astype(jnp.float32)).astype(jnp.bfloat16)
    width = halves * LANES
    cell = lax.broadcasted_iota(jnp.int32, (width, LANES), 0)
    block = lax.broadcasted_iota(jnp.int32, (width, LANES), 1)
    merge = jnp.where((cell >> 6) * 16 + ((cell & 31) >> 1) == block, 1.0, 0.0).astype(jnp.bfloat16)
    split = jnp.dot(
        jnp.concatenate([first, second, third], axis=0), merge, preferred_element_type=jnp.float32
    )
    mean = (split[:64] + split[64:128] + split[128:]) * 0.125
    for half in range(2):
        coarse[0:32, half * LANES : (half + 1) * LANES] = mean[32 * half : 32 * half + 32]
    for box in range(2):
        label = parents[0, box, 0] * 16 + parents[0, box, 1] * 8 + parents[0, box, 2]
        coarse[32 + 8 * box : 40 + 8 * box, :] = jnp.full((8, 2 * LANES), label.astype(jnp.float32))


def unpack_kernel(red, black, red_left, black_left, smoothed, residual, stage):
    boxes, tiles = red.shape[:2]
    odd = odd_lanes(red.shape[2])
    for k, one, two, out in ((0, red, black, smoothed), (1, red_left, black_left, residual)):
        for box in range(boxes):
            for tile in range(tiles):
                low, high = one[box, tile], two[box, tile]
                stage[k, box, tile, pl.ds(0, 16, 2), :] = jnp.where(odd == 1, high, low)
                stage[k, box, tile, pl.ds(1, 16, 2), :] = jnp.where(odd == 1, low, high)
                out[0, box, :, tile * LANES : (tile + 1) * LANES] = stage[k, box, tile]


def place_kernel(*refs):
    *got, source, out = refs
    group = lax.axis_index("grp")
    base = (group * 16).astype(jnp.float32)
    for octant in range(16):
        kept = source[0, octant // 8, octant % 8]
        for sender in got:
            for box in range(2):
                label = sender[32 + 8 * box : 40 + 8 * box, :]
                mine = jnp.concatenate([label, label], axis=0) == base + float(octant)
                kept = jnp.where(mine, sender[16 * box : 16 * box + 16, :], kept)
        out[0, octant // 8, octant % 8] = kept


def per_device(old_fields, old_count, neighbours, parents, coarse_source):
    f32 = jnp.float32
    curve = lax.axis_size("box")
    box_edge, plane_cells = old_fields.shape[3:]
    boxes = neighbours.shape[1]
    params = pltpu.CompilerParams(vmem_limit_bytes=40 << 20)

    def cost(flops, size):
        return pl.CostEstimate(flops=flops, bytes_accessed=size, transcendentals=0)

    def rows(count):
        return jax.ShapeDtypeStruct((count, LANES), f32)

    def swap(message, distance, shift):
        ids = [i for i in range(curve - distance) if (i - shift) % (2 * distance) < distance]
        both = [(i, i + distance) for i in ids] + [(i + distance, i) for i in ids]
        return lax.ppermute(message, "box", both)

    *first, shifts = pl.pallas_call(
        pack_first_kernel,
        out_shape=(rows(FIRST_ROWS),) * 2 + (jax.ShapeDtypeStruct((4,), jnp.int32),),
        in_specs=[HBM] * 3,
        out_specs=(VMEM, VMEM, SMEM),
        scratch_shapes=[
            pltpu.SMEM(old_count.shape, old_count.dtype),
            pltpu.SMEM(neighbours.shape, neighbours.dtype),
            pltpu.VMEM(old_fields.shape, f32),
            pltpu.SemaphoreType.DMA((2 + 2 * old_fields.shape[2] + 6,)),
        ],
        compiler_params=params,
        cost_estimate=cost(10**6, 2 << 20),
        name="pack_first",
    )(*[pltpu.with_memory_space_constraint(x, pltpu.HBM) for x in (old_count, neighbours, old_fields)])
    rest = pl.pallas_call(
        pack_rest_kernel,
        out_shape=(rows(REST_ROWS),) * 2 + (rows(FAR_ROWS),) * 2,
        in_specs=[SMEM, VMEM],
        out_specs=(VMEM,) * 4,
        compiler_params=params,
        cost_estimate=cost(10**6, 2 << 20),
        name="pack_rest",
    )(shifts, old_fields)
    first = [swap(message, 1, shift) for shift, message in enumerate(first)]
    far = [swap(rest[2], 2, 0), swap(rest[3], 2, 2)]
    rest = [swap(message, 1, shift) for shift, message in enumerate(rest[:2])]
    packed = (2, boxes, TILES, PAIRS, LANES)
    column = pltpu.VMEM((boxes, TILES, PAIRS + 2 * FIRST, LANES), f32)
    raw = pltpu.VMEM((boxes, TILES, OWN + 2 * PAD, LANES), f32)
    weights = pl.pallas_call(
        weigh_kernel,
        out_shape=[
            jax.ShapeDtypeStruct(shape, f32)
            for shape in ((2, 6, boxes, TILES, PAIRS, LANES), packed, packed, (boxes, 4, PAIRS, LANES))
        ],
        in_specs=[SMEM, SMEM] + [VMEM] * 5,
        out_specs=[VMEM] * 4,
        scratch_shapes=[raw, raw, column, column],
        compiler_params=params,
        cost_estimate=cost(10**7, 4 << 20),
        name="weigh",
    )(shifts, neighbours, old_fields, *first, *far)
    fine = jax.ShapeDtypeStruct((1, boxes, box_edge, plane_cells), f32)
    half = jax.ShapeDtypeStruct((boxes, TILES, box_edge // 2, LANES), f32)
    *halves, coarse = pl.pallas_call(
        smooth_kernel,
        out_shape=(half, half, half, half, jax.ShapeDtypeStruct((48, 2 * LANES), f32)),
        in_specs=[SMEM, SMEM, SMEM] + [VMEM] * 9,
        out_specs=(VMEM,) * 5,
        scratch_shapes=[raw, column, column],
        compiler_params=params,
        cost_estimate=cost(10**7, 6 << 20),
        name="smooth",
    )(shifts, neighbours, parents, old_fields, *rest, *far, *weights)
    groups = lax.axis_size("grp")
    got = [coarse] + [
        lax.ppermute(coarse, "grp", [(i, i ^ k) for i in range(groups)]) for k in range(1, groups)
    ]
    smoothed, residual = pl.pallas_call(
        unpack_kernel,
        out_shape=(fine, fine),
        in_specs=[VMEM] * 4,
        out_specs=(VMEM,) * 2,
        scratch_shapes=[pltpu.VMEM((2, boxes, TILES, OWN, LANES), f32)],
        compiler_params=params,
        cost_estimate=pl.CostEstimate(flops=10**6, bytes_accessed=3 << 20, transcendentals=0),
        name="unpack",
    )(*halves)
    coarse_rhs = pl.pallas_call(
        place_kernel,
        out_shape=jax.ShapeDtypeStruct(coarse_source.shape, f32),
        in_specs=[VMEM] * (groups + 1),
        out_specs=VMEM,
        compiler_params=params,
        cost_estimate=pl.CostEstimate(flops=10**6, bytes_accessed=1 << 20, transcendentals=0),
        name="place",
    )(*got, coarse_source)
    return smoothed, residual, coarse_rhs


def solution(mesh):
    in_specs = (
        P(None, "grp", "box", None, None),
        P("grp", None),
        P("grp", "box", None),
        P("grp", "box", None),
        P("grp", "box", None, None, None),
    )
    out_specs = (
        P("grp", "box", None, None),
        P("grp", "box", None, None),
        P("grp", "box", None, None, None),
    )
    return jax.shard_map(
        per_device, mesh=mesh, in_specs=in_specs, out_specs=out_specs, check_vma=False
    )
```

time: 35.2 us -> 40.2 us (1.14)
  the two profiles are of different devices: /device:TPU:128 before, /device:TPU:119 now
where the time goes in v3:
time: 40.2 us; the launch traced here: 40 us
  starting transfers between devices  21.6 us (54%)
  Pallas kernels  9.76 us (24%)
  waiting for transfers between devices  7.85 us (20%)
  between operations  0.78 us (2%)
    ppermute x6, starting transfers between devices, swap(): return lax.ppermute(message, 'box', both)  16.9 us
    ppermute x6, waiting for transfers between devices, swap(): return lax.ppermute(message, 'box', both)  5.71 us
    ppermute x3, starting transfers between devices, per_device(): lax.ppermute(coarse, 'grp', [(i, i ^ k) for i in range(groups)])  4.69 us
    pallas_call x1, Pallas kernels, per_device(): pl.pallas_call(smooth_kernel, out_shape=(half, half, half, half, jax.Shap...  3.25 us
    pallas_call x1, Pallas kernels, per_device(): pl.pallas_call(pack_first_kernel, out_shape=(rows(FIRST_ROWS),) * 2 + (ja...  2.34 us
    ppermute x3, waiting for transfers between devices, per_device(): lax.ppermute(coarse, 'grp', [(i, i ^ k) for i in range(groups)])  2.14 us
    pallas_call x1, Pallas kernels, per_device(): pl.pallas_call(weigh_kernel, out_shape=[jax.ShapeDtypeStruct(shape, f32)...  1.8 us
    pallas_call x1, Pallas kernels, per_device(): pl.pallas_call(unpack_kernel, out_shape=(fine, fine), in_specs=[VMEM] * 4...  0.85 us
  transfers between devices with their start and end apart: 9, of which 3 were waited for; matrix products, arithmetic and copies ran while one was open for 0% of the time, Pallas kernels for 8%

profile of v3, /device:TPU:119, one launch (start us, length us, event | category | flops | bytes accessed | tf_op | source)
XLA Modules:
  0.0 40.0 jit_solution(6634120369351169211)
XLA Ops:
  0.6 0.0 copy-start
  0.6 0.0 copy-start.2
  0.7 0.0 copy-start.3
  0.7 2.3 %pack_first.1 = (f32[648,128]{1,0:T(8,128)S(1)}, f32[648,128]{1,0:T(8,128)S(1)}, s32[4]{0:T(128)S(1)}) custom-call(s32[1,64]{1,0:T(1,128)} %counts_hbm.1, s32[1,2,6]{2,1,0:T(2,128)} %links.3, f32[3,1,4,32,1024]{4,3,2,1,0:T(8,128)} %fields.5), custom_call_target="tpu_custom_call" | custom-call | flops 1000000 | bytes 2097152 | tf_op jit(solution)/shard_map/pack_first/pallas_call | solution.py:575
  3.0 0.1 collective-permute-start.4
  3.1 7.3 %collective-permute-start.5 = (f32[648,128]{1,0:T(8,128)S(1)}, f32[648,128]{1,0:T(8,128)S(1)}, u32[]{:S(2)}, u32[]{:S(2)}) collective-permute-start(f32[648,128]{1,0:T(8,128)S(1)} %get-tuple-element.27), channel_id=1, source_target_pairs={{4,8},{12,16},{20,24},{28,32},{36,40},{44,48},{52,56},{60,64},{68,... | collective-permute-start | bytes 995336 | tf_op jit(solution)/shard_map/ppermute | solution.py:573
  10.4 0.0 copy-done
  10.5 0.7 %pack_rest.1 = (f32[160,128]{1,0:T(8,128)S(1)}, f32[160,128]{1,0:T(8,128)S(1)}, f32[80,128]{1,0:T(8,128)S(1)}, f32[80,128]{1,0:T(8,128)S(1)}) custom-call(s32[4]{0:T(128)S(1)} %get-tuple-element.21.shifts, f32[3,1,4,32,1024]{4,3,2,1,0:T(8,128)S(1)} %copy-done), custom_call_target="tpu_custom_call" | custom-call | flops 1000000 | bytes 2097152 | tf_op jit(solution)/shard_map/pack_rest/pallas_call | solution.py:590
  11.2 0.1 collective-permute-start.2
  11.3 0.1 collective-permute-start
  11.4 6.9 %collective-permute-start.1 = (f32[160,128]{1,0:T(8,128)S(1)}, f32[160,128]{1,0:T(8,128)S(1)}, u32[]{:S(2)}, u32[]{:S(2)}) collective-permute-start(f32[160,128]{1,0:T(8,128)S(1)} %get-tuple-element.23), channel_id=1, source_target_pairs={{4,8},{12,16},{20,24},{28,32},{36,40},{44,48},{52,56},{60,64},{68,... | collective-permute-start | bytes 245768 | tf_op jit(solution)/shard_map/ppermute | solution.py:573
  18.3 0.0 collective-permute-done.2.far_a
  18.3 2.4 %collective-permute-start.3 = (f32[80,128]{1,0:T(8,128)S(1)}, f32[80,128]{1,0:T(8,128)S(1)}, u32[]{:S(2)}, u32[]{:S(2)}) collective-permute-start(f32[80,128]{1,0:T(8,128)S(1)} %get-tuple-element.25), channel_id=1, source_target_pairs={{8,16},{12,20},{24,32},{28,36},{40,48},{44,52},{56,64},{60,68},{72... | collective-permute-start | bytes 122888 | tf_op jit(solution)/shard_map/ppermute | solution.py:573
  20.6 5.7 %collective-permute-done.3.far_b = f32[80,128]{1,0:T(8,128)S(1)} collective-permute-done((f32[80,128]{1,0:T(8,128)S(1)}, f32[80,128]{1,0:T(8,128)S(1)}, u32[]{:S(2)}, u32[]{:S(2)}) %collective-permute-start.3) | collective-permute-done | bytes 40992 | tf_op jit(solution)/shard_map/ppermute | solution.py:573
  26.3 0.0 collective-permute-done.4.near_a
  26.3 0.0 collective-permute-done.5.near_b
  26.3 0.0 copy-done.2
  26.4 1.8 %weigh.1 = (f32[2,6,2,8,24,128]{5,4,3,2,1,0:T(8,128)S(1)}, f32[2,2,8,24,128]{4,3,2,1,0:T(8,128)S(1)}, f32[2,2,8,24,128]{4,3,2,1,0:T(8,128)S(1)}, f32[2,4,24,128]{3,2,1,0:T(8,128)S(1)}) custom-call(s32[4]{0:T(128)S(1)} %get-tuple-element.21.shifts, s32[1,2,6]{2,1,0:T(2,128)S(1)} %copy-done.2, f32[3,1,4,32,1024]{4,3,2,1,0:T(8,128)S(1)} %copy-done, ...), custom_call_target="tpu_custom_call" | custom-call | flops 10000000 | bytes 4194304 | tf_op jit(solution)/shard_map/weigh/pallas_call | solution.py:605
  28.2 0.0 collective-permute-done.near_a
  28.2 0.0 collective-permute-done.1.near_b
  28.2 0.0 copy-done.3
  28.2 0.0 copy-start.1
  28.2 3.3 %smooth.1 = (f32[2,8,16,128]{3,2,1,0:T(8,128)S(1)}, f32[2,8,16,128]{3,2,1,0:T(8,128)S(1)}, f32[2,8,16,128]{3,2,1,0:T(8,128)S(1)}, f32[2,8,16,128]{3,2,1,0:T(8,128)S(1)}, f32[48,256]{1,0:T(8,128)S(1)}) custom-call(s32[4]{0:T(128)S(1)} %get-tuple-element.21.shifts, s32[1,2,6]{2,1,0:T(2,128)S(1)} %copy-done.2, s32[1,2,3]{2,1,0:T(2,128)S(1)} %copy-done.3, ...), custom_call_target="tpu_custom_call" | custom-call | flops 10000000 | bytes 6291456 | tf_op jit(solution)/shard_map/smooth/pallas_call | solution.py:620
  31.5 4.2 %collective-permute-start.8 = (f32[48,256]{1,0:T(8,128)S(1)}, f32[48,256]{1,0:T(8,128)S(1)}, u32[]{:S(2)}, u32[]{:S(2)}) collective-permute-start(f32[48,256]{1,0:T(8,128)S(1)} %get-tuple-element.38.refs_0_), channel_id=1, source_target_pairs={{0,3},{1,2},{2,1},{3,0},{4,7},{5,6},{6,5},{7,4},{8,11},{9,10},{10,... | collective-permute-start | bytes 147464 | tf_op jit(solution)/shard_map/ppermute | solution.py:632
  35.7 0.5 %collective-permute-start.7 = (f32[48,256]{1,0:T(8,128)S(1)}, f32[48,256]{1,0:T(8,128)S(1)}, u32[]{:S(2)}, u32[]{:S(2)}) collective-permute-start(f32[48,256]{1,0:T(8,128)S(1)} %get-tuple-element.38.refs_0_), channel_id=1, source_target_pairs={{0,2},{1,3},{2,0},{3,1},{4,6},{5,7},{6,4},{7,5},{8,10},{9,11},{10,... | collective-permute-start | bytes 147464 | tf_op jit(solution)/shard_map/ppermute | solution.py:632
  36.1 0.0 collective-permute-start.6
  36.2 0.8 %unpack.1 = (f32[1,2,32,1024]{3,2,1,0:T(8,128)}, f32[1,2,32,1024]{3,2,1,0:T(8,128)}) custom-call(f32[2,8,16,128]{3,2,1,0:T(8,128)S(1)} %get-tuple-element.32.red, f32[2,8,16,128]{3,2,1,0:T(8,128)S(1)} %get-tuple-element.33.black, f32[2,8,16,128]{3,2,1,0:T(8,128)S(1)} %get-tuple-element.34.red_left, f32[2,8,16,128]{3,2,1,0:T(8,128)S(1)} %get-tuple-element.35.black_left), custom_call_target="tpu_custom_call" | custom-call | flops 1000000 | bytes 3145728 | tf_op jit(solution)/shard_map/unpack/pallas_call | solution.py:634
  37.0 1.1 %collective-permute-done.8.refs_3_ = f32[48,256]{1,0:T(8,128)S(1)} collective-permute-done((f32[48,256]{1,0:T(8,128)S(1)}, f32[48,256]{1,0:T(8,128)S(1)}, u32[]{:S(2)}, u32[]{:S(2)}) %collective-permute-start.8) | collective-permute-done | bytes 49184 | tf_op jit(solution)/shard_map/ppermute | solution.py:632
  38.1 1.1 %collective-permute-done.7.refs_2_ = f32[48,256]{1,0:T(8,128)S(1)} collective-permute-done((f32[48,256]{1,0:T(8,128)S(1)}, f32[48,256]{1,0:T(8,128)S(1)}, u32[]{:S(2)}, u32[]{:S(2)}) %collective-permute-start.7) | collective-permute-done | bytes 49184 | tf_op jit(solution)/shard_map/ppermute | solution.py:632
  39.1 0.0 collective-permute-done.6.refs_1_
  39.1 0.0 copy-done.1
  39.1 0.8 %place.1 = f32[1,2,8,16,256]{4,3,2,1,0:T(8,128)} custom-call(f32[48,256]{1,0:T(8,128)S(1)} %get-tuple-element.38.refs_0_, f32[48,256]{1,0:T(8,128)S(1)} %collective-permute-done.6.refs_1_, f32[48,256]{1,0:T(8,128)S(1)} %collective-permute-done.7.refs_2_, f32[48,256]{1,0:T(8,128)S(1)} %collective-permute-done.8.refs_3_, f32[1,2,8,16,256]{4,3,2,1,0:T(8,128)S(1)} %copy-done.1), custom_call_target="tpu_custom_call" | custom-call | flops 1000000 | bytes 1048576 | tf_op jit(solution)/shard_map/place/pallas_call | solution.py:644
Async XLA Ops:
  0.6 9.8 %copy-start = (f32[3,1,4,32,1024]{4,3,2,1,0:T(8,128)S(1)}, f32[3,1,4,32,1024]{4,3,2,1,0:T(8,128)}, u32[]{:S(2)}) copy-start(f32[3,1,4,32,1024]{4,3,2,1,0:T(8,128)} %fields.5) | copy-start | bytes 4718596
  0.6 25.7 %copy-start.2 = (s32[1,2,6]{2,1,0:T(2,128)S(1)}, s32[1,2,6]{2,1,0:T(2,128)}, u32[]{:S(2)}) copy-start(s32[1,2,6]{2,1,0:T(2,128)} %links.3) | copy-start | bytes 148
  0.7 27.5 %copy-start.3 = (s32[1,2,3]{2,1,0:T(2,128)S(1)}, s32[1,2,3]{2,1,0:T(2,128)}, u32[]{:S(2)}) copy-start(s32[1,2,3]{2,1,0:T(2,128)} %parents.1) | copy-start | bytes 76
  3.0 23.3 %collective-permute-start.4 = (f32[648,128]{1,0:T(8,128)S(1)}, f32[648,128]{1,0:T(8,128)S(1)}, u32[]{:S(2)}, u32[]{:S(2)}) collective-permute-start(f32[648,128]{1,0:T(8,128)S(1)} %get-tuple-element.26), channel_id=1, source_target_pairs={{0,4},{8,12},{16,20},{24,28},{32,36},{40,44},{48,52},{56,60},{64,6... | collective-permute-start | bytes 995336 | tf_op jit(solution)/shard_map/ppermute | solution.py:573
  3.1 23.2 %collective-permute-start.5 = (f32[648,128]{1,0:T(8,128)S(1)}, f32[648,128]{1,0:T(8,128)S(1)}, u32[]{:S(2)}, u32[]{:S(2)}) collective-permute-start(f32[648,128]{1,0:T(8,128)S(1)} %get-tuple-element.27), channel_id=1, source_target_pairs={{4,8},{12,16},{20,24},{28,32},{36,40},{44,48},{52,56},{60,64},{68,... | collective-permute-start | bytes 995336 | tf_op jit(solution)/shard_map/ppermute | solution.py:573
  11.2 7.1 %collective-permute-start.2 = (f32[80,128]{1,0:T(8,128)S(1)}, f32[80,128]{1,0:T(8,128)S(1)}, u32[]{:S(2)}, u32[]{:S(2)}) collective-permute-start(f32[80,128]{1,0:T(8,128)S(1)} %get-tuple-element.24), channel_id=1, source_target_pairs={{0,8},{4,12},{16,24},{20,28},{32,40},{36,44},{48,56},{52,60},{64,7... | collective-permute-start | bytes 122888 | tf_op jit(solution)/shard_map/ppermute | solution.py:573
  11.3 16.9 %collective-permute-start = (f32[160,128]{1,0:T(8,128)S(1)}, f32[160,128]{1,0:T(8,128)S(1)}, u32[]{:S(2)}, u32[]{:S(2)}) collective-permute-start(f32[160,128]{1,0:T(8,128)S(1)} %get-tuple-element.22), channel_id=1, source_target_pairs={{0,4},{8,12},{16,20},{24,28},{32,36},{40,44},{48,52},{56,60},{64,6... | collective-permute-start | bytes 245768 | tf_op jit(solution)/shard_map/ppermute | solution.py:573
  11.4 16.8 %collective-permute-start.1 = (f32[160,128]{1,0:T(8,128)S(1)}, f32[160,128]{1,0:T(8,128)S(1)}, u32[]{:S(2)}, u32[]{:S(2)}) collective-permute-start(f32[160,128]{1,0:T(8,128)S(1)} %get-tuple-element.23), channel_id=1, source_target_pairs={{4,8},{12,16},{20,24},{28,32},{36,40},{44,48},{52,56},{60,64},{68,... | collective-permute-start | bytes 245768 | tf_op jit(solution)/shard_map/ppermute | solution.py:573
  18.3 8.1 %collective-permute-start.3 = (f32[80,128]{1,0:T(8,128)S(1)}, f32[80,128]{1,0:T(8,128)S(1)}, u32[]{:S(2)}, u32[]{:S(2)}) collective-permute-start(f32[80,128]{1,0:T(8,128)S(1)} %get-tuple-element.25), channel_id=1, source_target_pairs={{8,16},{12,20},{24,32},{28,36},{40,48},{44,52},{56,64},{60,68},{72... | collective-permute-start | bytes 122888 | tf_op jit(solution)/shard_map/ppermute | solution.py:573
  28.2 11.0 %copy-start.1 = (f32[1,2,8,16,256]{4,3,2,1,0:T(8,128)S(1)}, f32[1,2,8,16,256]{4,3,2,1,0:T(8,128)}, u32[]{:S(2)}) copy-start(f32[1,2,8,16,256]{4,3,2,1,0:T(8,128)} %refs_4_.1) | copy-start | bytes 786436
  31.5 6.6 %collective-permute-start.8 = (f32[48,256]{1,0:T(8,128)S(1)}, f32[48,256]{1,0:T(8,128)S(1)}, u32[]{:S(2)}, u32[]{:S(2)}) collective-permute-start(f32[48,256]{1,0:T(8,128)S(1)} %get-tuple-element.38.refs_0_), channel_id=1, source_target_pairs={{0,3},{1,2},{2,1},{3,0},{4,7},{5,6},{6,5},{7,4},{8,11},{9,10},{10,... | collective-permute-start | bytes 147464 | tf_op jit(solution)/shard_map/ppermute | solution.py:632
  35.7 3.5 %collective-permute-start.7 = (f32[48,256]{1,0:T(8,128)S(1)}, f32[48,256]{1,0:T(8,128)S(1)}, u32[]{:S(2)}, u32[]{:S(2)}) collective-permute-start(f32[48,256]{1,0:T(8,128)S(1)} %get-tuple-element.38.refs_0_), channel_id=1, source_target_pairs={{0,2},{1,3},{2,0},{3,1},{4,6},{5,7},{6,4},{7,5},{8,10},{9,11},{10,... | collective-permute-start | bytes 147464 | tf_op jit(solution)/shard_map/ppermute | solution.py:632
  36.1 3.0 %collective-permute-start.6 = (f32[48,256]{1,0:T(8,128)S(1)}, f32[48,256]{1,0:T(8,128)S(1)}, u32[]{:S(2)}, u32[]{:S(2)}) collective-permute-start(f32[48,256]{1,0:T(8,128)S(1)} %get-tuple-element.38.refs_0_), channel_id=1, source_target_pairs={{0,1},{1,0},{2,3},{3,2},{4,5},{5,4},{6,7},{7,6},{8,9},{9,8},{10,11... | collective-permute-start | bytes 147464 | tf_op jit(solution)/shard_map/ppermute | solution.py:632

commit v4 on v3

--- a/solution.py
+++ b/solution.py
@@ -14,9 +14,9 @@
 SIDE = OWN * TILES
 SIDE_ENDS = SIDE + OWN * TILES
 LINKS = SIDE_ENDS + 2 * SIDE_END * TILES
-FIRST_ROWS = LINKS + 8
-VALUE_ENDS = OWN // 2 * TILES
-REST_ROWS = VALUE_ENDS + 2 * VALUE_END * TILES
+VALUE = LINKS + 8
+VALUE_ENDS = VALUE + OWN // 2 * TILES
+NEAR_ROWS = VALUE_ENDS + 2 * VALUE_END * TILES
 FAR_VALUES = SIDE_END * TILES
 FAR_ROWS = FAR_VALUES + VALUE_END * TILES
 
@@ -104,7 +104,7 @@
     return (jnp.maximum(-here, 0), 1 - here), jnp.minimum(2 - here, 3)
 
 
-def pack_first_kernel(counts_hbm, links_hbm, fields_hbm, near_a, near_b, shifts, counts, links, fields, sems):
+def pack_kernel(counts_hbm, links_hbm, fields_hbm, near_a, near_b, shifts, counts, links, fields, sems):
     copies = []
 
     def fetch(source, target):
@@ -113,11 +113,8 @@
     fetch(counts_hbm, counts)
     fetch(links_hbm, links)
     for row in range(fields.shape[2]):
-        for field in (2, 1):
+        for field in range(3):
             fetch(fields_hbm.at[field, 0, row], fields.at[field, 0, row])
-    for row in range(3):
-        for rows in (pl.ds(0, 8), pl.ds(OWN - 8, 8)):
-            fetch(fields_hbm.at[0, 0, row, rows], fields.at[0, 0, row, rows])
     for copy in copies:
         copy.start()
     for copy in copies:
@@ -134,16 +131,24 @@
             mine = (row_ids(8) == box) & (lane_ids(8) == face - 2)
             codes = jnp.where(mine, link_code(links, box, face, 2 * position).astype(jnp.float32), codes)
 
+    mixed = (row_ids(16) + odd_lanes(16)) & 1
+
     def message(out, upper):
         row = move_up if upper else 0
         for tile in range(TILES):
             lanes = slice(tile * LANES, (tile + 1) * LANES)
+            low = fields[0, 0, row, 0:16, lanes]
+            high = pltpu.roll(fields[0, 0, row, 16:32, lanes], 15, 0)
+            out[VALUE + 16 * tile : VALUE + 16 * tile + 16, :] = jnp.where(mixed == 1, low, high)
             out[OWN * tile : OWN * (tile + 1), :] = fields[2, 0, row, :, lanes]
             out[SIDE + OWN * tile : SIDE + OWN * (tile + 1), :] = fields[1, 0, row, :, lanes]
             for box in range(2):
                 store_rows(
                     out, SIDE_ENDS + SIDE_END * (2 * tile + box), side_end(fields, held[box], tile, upper)
                 )
+                store_rows(
+                    out, VALUE_ENDS + VALUE_END * (2 * tile + box), value_end(fields, held[box], tile, upper)
+                )
         out[LINKS : LINKS + 8, :] = codes
 
     even = position % 2 == 0
@@ -159,23 +164,9 @@
         message(near_b, True)
 
 
-def pack_rest_kernel(shifts, fields, near_a, near_b, far_a, far_b):
+def pack_far_kernel(shifts, fields, far_a, far_b):
     position = lax.axis_index("box")
-    here = shifts[1]
-    held, move_up = slots(here)
-
-    def message(out, upper):
-        row = move_up if upper else 0
-        mixed = (row_ids(16) + odd_lanes(16)) & 1
-        for tile in range(TILES):
-            lanes = slice(tile * LANES, (tile + 1) * LANES)
-            low = fields[0, 0, row, 0:16, lanes]
-            high = pltpu.roll(fields[0, 0, row, 16:32, lanes], 15, 0)
-            out[16 * tile : 16 * tile + 16, :] = jnp.where(mixed == 1, low, high)
-            for box in range(2):
-                store_rows(
-                    out, VALUE_ENDS + VALUE_END * (2 * tile + box), value_end(fields, held[box], tile, upper)
-                )
+    move_up = slots(shifts[1])[1]
 
     def far_message(out, upper):
         row = move_up if upper else 0
@@ -183,7 +174,6 @@
             store_rows(out, SIDE_END * tile, side_end(fields, row, tile, upper))
             store_rows(out, FAR_VALUES + VALUE_END * tile, value_end(fields, row, tile, upper))
 
-    even = position % 2 == 0
     lower = position % 4 < 2
 
     @pl.when(lower)
@@ -195,16 +185,6 @@
     def _():
         far_message(far_a, False)
         far_message(far_b, True)
-
-    @pl.when(even)
-    def _():
-        message(near_a, True)
-        message(near_b, False)
-
-    @pl.when(jnp.logical_not(even))
-    def _():
-        message(near_a, False)
-        message(near_b, True)
 
 
 def choose(flag, one, other):
@@ -295,24 +275,10 @@
     )
 
 
-def weigh_kernel(
-    shifts,
-    links,
-    fields,
-    near_a,
-    near_b,
-    far_a,
-    far_b,
-    weight,
-    source,
-    diagonal,
-    code,
-    raw,
-    raw_side,
-    red_coef,
-    black_coef,
+def make_weights(
+    shifts, links, fields, near_a, near_b, far_a, far_b, weight, source, diagonal, code, raw, raw_side, coef
 ):
-    coef = (red_coef, black_coef)
+    red_coef, black_coef = coef
     position = lax.axis_index("box")
     offset = [shifts[k] for k in range(4)]
     _, here, after, _ = offset
@@ -423,19 +389,27 @@
     near_b,
     far_a,
     far_b,
-    weight,
-    source,
-    diagonal,
-    code,
     red_out,
     black_out,
     red_left,
     black_left,
     coarse,
+    raw_coef,
+    raw_side,
     raw,
+    red_coef,
+    black_coef,
     red,
     black,
+    weight,
+    source,
+    diagonal,
+    code,
 ):
+    make_weights(
+        shifts, links, fields, near_a, near_b, far_a, far_b,
+        weight, source, diagonal, code, raw_coef, raw_side, (red_coef, black_coef),
+    )
     value = (red, black)
     position = lax.axis_index("box")
     offset = [shifts[k] for k in range(4)]
@@ -450,7 +424,7 @@
 
     def place_moved(box, ref):
         for tile in range(TILES):
-            packed = ref[16 * tile : 16 * tile + 16, :]
+            packed = ref[VALUE + 16 * tile : VALUE + 16 * tile + 16, :]
             raw[box, tile, PAD : PAD + 16, :] = packed
             raw[box, tile, PAD + 16 : PAD + 32, :] = pltpu.roll(packed, 1, 0)
 
@@ -572,65 +546,54 @@
         both = [(i, i + distance) for i in ids] + [(i + distance, i) for i in ids]
         return lax.ppermute(message, "box", both)
 
-    *first, shifts = pl.pallas_call(
-        pack_first_kernel,
-        out_shape=(rows(FIRST_ROWS),) * 2 + (jax.ShapeDtypeStruct((4,), jnp.int32),),
+    near_a, near_b, shifts = pl.pallas_call(
+        pack_kernel,
+        out_shape=(rows(NEAR_ROWS), rows(NEAR_ROWS), jax.ShapeDtypeStruct((4,), jnp.int32)),
         in_specs=[HBM] * 3,
         out_specs=(VMEM, VMEM, SMEM),
         scratch_shapes=[
             pltpu.SMEM(old_count.shape, old_count.dtype),
             pltpu.SMEM(neighbours.shape, neighbours.dtype),
             pltpu.VMEM(old_fields.shape, f32),
-            pltpu.SemaphoreType.DMA((2 + 2 * old_fields.shape[2] + 6,)),
+            pltpu.SemaphoreType.DMA((2 + 3 * old_fields.shape[2],)),
         ],
         compiler_params=params,
         cost_estimate=cost(10**6, 2 << 20),
-        name="pack_first",
+        name="pack",
     )(*[pltpu.with_memory_space_constraint(x, pltpu.HBM) for x in (old_count, neighbours, old_fields)])
-    rest = pl.pallas_call(
-        pack_rest_kernel,
-        out_shape=(rows(REST_ROWS),) * 2 + (rows(FAR_ROWS),) * 2,
+    far_a, far_b = pl.pallas_call(
+        pack_far_kernel,
+        out_shape=(rows(FAR_ROWS),) * 2,
         in_specs=[SMEM, VMEM],
-        out_specs=(VMEM,) * 4,
+        out_specs=(VMEM,) * 2,
         compiler_params=params,
         cost_estimate=cost(10**6, 2 << 20),
-        name="pack_rest",
+        name="pack_far",
     )(shifts, old_fields)
-    first = [swap(message, 1, shift) for shift, message in enumerate(first)]
-    far = [swap(rest[2], 2, 0), swap(rest[3], 2, 2)]
-    rest = [swap(message, 1, shift) for shift, message in enumerate(rest[:2])]
-    packed = (2, boxes, TILES, PAIRS, LANES)
+    moved = [swap(near_a, 1, 0), swap(near_b, 1, 1), swap(far_a, 2, 0), swap(far_b, 2, 2)]
+    packed = pltpu.VMEM((2, boxes, TILES, PAIRS, LANES), f32)
     column = pltpu.VMEM((boxes, TILES, PAIRS + 2 * FIRST, LANES), f32)
     raw = pltpu.VMEM((boxes, TILES, OWN + 2 * PAD, LANES), f32)
-    weights = pl.pallas_call(
-        weigh_kernel,
-        out_shape=[
-            jax.ShapeDtypeStruct(shape, f32)
-            for shape in ((2, 6, boxes, TILES, PAIRS, LANES), packed, packed, (boxes, 4, PAIRS, LANES))
-        ],
-        in_specs=[SMEM, SMEM] + [VMEM] * 5,
-        out_specs=[VMEM] * 4,
-        scratch_shapes=[raw, raw, column, column],
-        compiler_params=params,
-        cost_estimate=cost(10**7, 4 << 20),
-        name="weigh",
-    )(shifts, neighbours, old_fields, *first, *far)
+    weight = pltpu.VMEM((2, 6, boxes, TILES, PAIRS, LANES), f32)
+    code = pltpu.VMEM((boxes, 4, PAIRS, LANES), f32)
     fine = jax.ShapeDtypeStruct((1, boxes, box_edge, plane_cells), f32)
     half = jax.ShapeDtypeStruct((boxes, TILES, box_edge // 2, LANES), f32)
     *halves, coarse = pl.pallas_call(
         smooth_kernel,
         out_shape=(half, half, half, half, jax.ShapeDtypeStruct((48, 2 * LANES), f32)),
-        in_specs=[SMEM, SMEM, SMEM] + [VMEM] * 9,
+        in_specs=[SMEM, SMEM, SMEM] + [VMEM] * 5,
         out_specs=(VMEM,) * 5,
-        scratch_shapes=[raw, column, column],
+        scratch_shapes=[raw] * 3 + [column] * 4 + [weight, packed, packed, code],
         compiler_params=params,
         cost_estimate=cost(10**7, 6 << 20),
         name="smooth",
-    )(shifts, neighbours, parents, old_fields, *rest, *far, *weights)
+    )(shifts, neighbours, parents, old_fields, *moved)
+    def across(message, bit):
+        return lax.ppermute(message, "grp", [(i, i ^ bit) for i in range(groups)])
+
     groups = lax.axis_size("grp")
-    got = [coarse] + [
-        lax.ppermute(coarse, "grp", [(i, i ^ k) for i in range(groups)]) for k in range(1, groups)
-    ]
+    over_link = across(coarse, 2)
+    got = [coarse, across(coarse, 1), over_link, across(over_link, 1)]
     smoothed, residual = pl.pallas_call(
         unpack_kernel,
         out_shape=(fine, fine),
@@ -644,7 +607,7 @@
     coarse_rhs = pl.pallas_call(
         place_kernel,
         out_shape=jax.ShapeDtypeStruct(coarse_source.shape, f32),
-        in_specs=[VMEM] * (groups + 1),
+        in_specs=[VMEM] * (len(got) + 1),
         out_specs=VMEM,
         compiler_params=params,
         cost_estimate=pl.CostEstimate(flops=10**6, bytes_accessed=1 << 20, transcendentals=0),

time: 40.2 us -> 36.5 us (0.908)
  the two profiles are of different devices: /device:TPU:119 before, /device:TPU:128 now
where the time goes in v4:
time: 36.5 us; the launch traced here: 36 us
  waiting for transfers between devices  14.5 us (40%)
  starting transfers between devices  11.7 us (32%)
  Pallas kernels  9.1 us (25%)
  between operations  0.72 us (2%)
    ppermute x4, waiting for transfers between devices, swap(): return lax.ppermute(message, 'box', both)  11 us
    ppermute x4, starting transfers between devices, swap(): return lax.ppermute(message, 'box', both)  10.6 us
    pallas_call x1, Pallas kernels, per_device(): pl.pallas_call(smooth_kernel, out_shape=(half, half, half, half, jax.Shap...  4.34 us
    ppermute x3, waiting for transfers between devices, across(): return lax.ppermute(message, 'grp', [(i, i ^ bit) for i in range(groups)])  3.48 us
    pallas_call x1, Pallas kernels, per_device(): pl.pallas_call(pack_kernel, out_shape=(rows(NEAR_ROWS), rows(NEAR_ROWS),...  2.42 us
    ppermute x3, starting transfers between devices, across(): return lax.ppermute(message, 'grp', [(i, i ^ bit) for i in range(groups)])  1.08 us
    pallas_call x1, Pallas kernels, per_device(): pl.pallas_call(unpack_kernel, out_shape=(fine, fine), in_specs=[VMEM] * 4...  0.85 us
    pallas_call x1, Pallas kernels, per_device(): pl.pallas_call(place_kernel, out_shape=jax.ShapeDtypeStruct(coarse_source...  0.83 us
  transfers between devices with their start and end apart: 7, of which 6 were waited for; matrix products, arithmetic and copies ran while one was open for 0% of the time, Pallas kernels for 4%

profile of v4, /device:TPU:128, one launch (start us, length us, event | category | flops | bytes accessed | tf_op | source)
XLA Modules:
  0.0 36.0 jit_solution(2834239328647160563)
XLA Ops:
  0.6 0.0 copy-start
  0.6 0.0 copy-start.2
  0.7 0.0 copy-start.3
  0.7 2.4 %pack.1 = (f32[808,128]{1,0:T(8,128)S(1)}, f32[808,128]{1,0:T(8,128)S(1)}, s32[4]{0:T(128)S(1)}) custom-call(s32[1,64]{1,0:T(1,128)} %counts_hbm.1, s32[1,2,6]{2,1,0:T(2,128)} %links.1, f32[3,1,4,32,1024]{4,3,2,1,0:T(8,128)} %fields.3), custom_call_target="tpu_custom_call" | custom-call | flops 1000000 | bytes 2097152 | tf_op jit(solution)/shard_map/pack/pallas_call | solution.py:549
  3.1 3.3 %collective-permute-start = (f32[808,128]{1,0:T(8,128)S(1)}, f32[808,128]{1,0:T(8,128)S(1)}, u32[]{:S(2)}, u32[]{:S(2)}) collective-permute-start(f32[808,128]{1,0:T(8,128)S(1)} %get-tuple-element.16), channel_id=1, source_target_pairs={{0,4},{8,12},{16,20},{24,28},{32,36},{40,44},{48,52},{56,60},{64,6... | collective-permute-start | bytes 1241096 | tf_op jit(solution)/shard_map/ppermute | solution.py:547
  6.4 4.0 %collective-permute-start.1 = (f32[808,128]{1,0:T(8,128)S(1)}, f32[808,128]{1,0:T(8,128)S(1)}, u32[]{:S(2)}, u32[]{:S(2)}) collective-permute-start(f32[808,128]{1,0:T(8,128)S(1)} %get-tuple-element.17), channel_id=1, source_target_pairs={{4,8},{12,16},{20,24},{28,32},{36,40},{44,48},{52,56},{60,64},{68,... | collective-permute-start | bytes 1241096 | tf_op jit(solution)/shard_map/ppermute | solution.py:547
  10.4 0.0 copy-done
  10.4 0.7 %pack_far.1 = (f32[80,128]{1,0:T(8,128)S(1)}, f32[80,128]{1,0:T(8,128)S(1)}) custom-call(s32[4]{0:T(128)S(1)} %get-tuple-element.15.shifts, f32[3,1,4,32,1024]{4,3,2,1,0:T(8,128)S(1)} %copy-done), custom_call_target="tpu_custom_call" | custom-call | flops 1000000 | bytes 2097152 | tf_op jit(solution)/shard_map/pack_far/pallas_call | solution.py:564
  11.0 0.0 copy-start.1
  11.0 0.1 collective-permute-start.2
  11.1 3.2 %collective-permute-start.3 = (f32[80,128]{1,0:T(8,128)S(1)}, f32[80,128]{1,0:T(8,128)S(1)}, u32[]{:S(2)}, u32[]{:S(2)}) collective-permute-start(f32[80,128]{1,0:T(8,128)S(1)} %get-tuple-element.19), channel_id=1, source_target_pairs={{8,16},{12,20},{24,32},{28,36},{40,48},{44,52},{56,64},{60,68},{72... | collective-permute-start | bytes 122888 | tf_op jit(solution)/shard_map/ppermute | solution.py:547
  14.4 5.6 %collective-permute-done.2.far_a = f32[80,128]{1,0:T(8,128)S(1)} collective-permute-done((f32[80,128]{1,0:T(8,128)S(1)}, f32[80,128]{1,0:T(8,128)S(1)}, u32[]{:S(2)}, u32[]{:S(2)}) %collective-permute-start.2) | collective-permute-done | bytes 40992 | tf_op jit(solution)/shard_map/ppermute | solution.py:547
  20.0 0.4 %collective-permute-done.3.far_b = f32[80,128]{1,0:T(8,128)S(1)} collective-permute-done((f32[80,128]{1,0:T(8,128)S(1)}, f32[80,128]{1,0:T(8,128)S(1)}, u32[]{:S(2)}, u32[]{:S(2)}) %collective-permute-start.3) | collective-permute-done | bytes 40992 | tf_op jit(solution)/shard_map/ppermute | solution.py:547
  20.4 3.7 %collective-permute-done.near_a = f32[808,128]{1,0:T(8,128)S(1)} collective-permute-done((f32[808,128]{1,0:T(8,128)S(1)}, f32[808,128]{1,0:T(8,128)S(1)}, u32[]{:S(2)}, u32[]{:S(2)}) %collective-permute-start) | collective-permute-done | bytes 413728 | tf_op jit(solution)/shard_map/ppermute | solution.py:547
  24.1 1.4 %collective-permute-done.1.near_b = f32[808,128]{1,0:T(8,128)S(1)} collective-permute-done((f32[808,128]{1,0:T(8,128)S(1)}, f32[808,128]{1,0:T(8,128)S(1)}, u32[]{:S(2)}, u32[]{:S(2)}) %collective-permute-start.1) | collective-permute-done | bytes 413728 | tf_op jit(solution)/shard_map/ppermute | solution.py:547
  25.4 0.0 copy-done.2
  25.4 0.0 copy-done.3
  25.4 4.3 %smooth.1 = (f32[2,8,16,128]{3,2,1,0:T(8,128)S(1)}, f32[2,8,16,128]{3,2,1,0:T(8,128)S(1)}, f32[2,8,16,128]{3,2,1,0:T(8,128)S(1)}, f32[2,8,16,128]{3,2,1,0:T(8,128)S(1)}, f32[48,256]{1,0:T(8,128)S(1)}) custom-call(s32[4]{0:T(128)S(1)} %get-tuple-element.15.shifts, s32[1,2,6]{2,1,0:T(2,128)S(1)} %copy-done.2, s32[1,2,3]{2,1,0:T(2,128)S(1)} %copy-done.3, ...), custom_call_target="tpu_custom_call" | custom-call | flops 10000000 | bytes 6291456 | tf_op jit(solution)/shard_map/smooth/pallas_call | solution.py:581
  29.8 1.1 %collective-permute-start.5 = (f32[48,256]{1,0:T(8,128)S(1)}, f32[48,256]{1,0:T(8,128)S(1)}, u32[]{:S(2)}, u32[]{:S(2)}) collective-permute-start(f32[48,256]{1,0:T(8,128)S(1)} %get-tuple-element.26.refs_0_), channel_id=1, source_target_pairs={{0,2},{1,3},{2,0},{3,1},{4,6},{5,7},{6,4},{7,5},{8,10},{9,11},{10,... | collective-permute-start | bytes 147464 | tf_op jit(solution)/shard_map/ppermute | solution.py:592
  30.9 0.0 collective-permute-start.4
  30.9 3.1 %collective-permute-done.5.refs_2_ = f32[48,256]{1,0:T(8,128)S(1)} collective-permute-done((f32[48,256]{1,0:T(8,128)S(1)}, f32[48,256]{1,0:T(8,128)S(1)}, u32[]{:S(2)}, u32[]{:S(2)}) %collective-permute-start.5) | collective-permute-done | bytes 49184 | tf_op jit(solution)/shard_map/ppermute | solution.py:592
  34.0 0.0 collective-permute-start.6
  34.0 0.8 %unpack.1 = (f32[1,2,32,1024]{3,2,1,0:T(8,128)}, f32[1,2,32,1024]{3,2,1,0:T(8,128)}) custom-call(f32[2,8,16,128]{3,2,1,0:T(8,128)S(1)} %get-tuple-element.20.red, f32[2,8,16,128]{3,2,1,0:T(8,128)S(1)} %get-tuple-element.21.black, f32[2,8,16,128]{3,2,1,0:T(8,128)S(1)} %get-tuple-element.22.red_left, f32[2,8,16,128]{3,2,1,0:T(8,128)S(1)} %get-tuple-element.23.black_left), custom_call_target="tpu_custom_call" | custom-call | flops 1000000 | bytes 3145728 | tf_op jit(solution)/shard_map/unpack/pallas_call | solution.py:597
  34.8 0.0 collective-permute-done.4.refs_1_
  34.8 0.4 %collective-permute-done.6.refs_3_ = f32[48,256]{1,0:T(8,128)S(1)} collective-permute-done((f32[48,256]{1,0:T(8,128)S(1)}, f32[48,256]{1,0:T(8,128)S(1)}, u32[]{:S(2)}, u32[]{:S(2)}) %collective-permute-start.6) | collective-permute-done | bytes 49184 | tf_op jit(solution)/shard_map/ppermute | solution.py:592
  35.2 0.0 copy-done.1
  35.2 0.8 %place.1 = f32[1,2,8,16,256]{4,3,2,1,0:T(8,128)} custom-call(f32[48,256]{1,0:T(8,128)S(1)} %get-tuple-element.26.refs_0_, f32[48,256]{1,0:T(8,128)S(1)} %collective-permute-done.4.refs_1_, f32[48,256]{1,0:T(8,128)S(1)} %collective-permute-done.5.refs_2_, f32[48,256]{1,0:T(8,128)S(1)} %collective-permute-done.6.refs_3_, f32[1,2,8,16,256]{4,3,2,1,0:T(8,128)S(1)} %copy-done.1), custom_call_target="tpu_custom_call" | custom-call | flops 1000000 | bytes 1048576 | tf_op jit(solution)/shard_map/place/pallas_call | solution.py:607
Async XLA Ops:
  0.6 9.7 %copy-start = (f32[3,1,4,32,1024]{4,3,2,1,0:T(8,128)S(1)}, f32[3,1,4,32,1024]{4,3,2,1,0:T(8,128)}, u32[]{:S(2)}) copy-start(f32[3,1,4,32,1024]{4,3,2,1,0:T(8,128)} %fields.3) | copy-start | bytes 4718596
  0.6 24.8 %copy-start.2 = (s32[1,2,6]{2,1,0:T(2,128)S(1)}, s32[1,2,6]{2,1,0:T(2,128)}, u32[]{:S(2)}) copy-start(s32[1,2,6]{2,1,0:T(2,128)} %links.1) | copy-start | bytes 148
  0.7 24.8 %copy-start.3 = (s32[1,2,3]{2,1,0:T(2,128)S(1)}, s32[1,2,3]{2,1,0:T(2,128)}, u32[]{:S(2)}) copy-start(s32[1,2,3]{2,1,0:T(2,128)} %parents.1) | copy-start | bytes 76
  3.1 21.0 %collective-permute-start = (f32[808,128]{1,0:T(8,128)S(1)}, f32[808,128]{1,0:T(8,128)S(1)}, u32[]{:S(2)}, u32[]{:S(2)}) collective-permute-start(f32[808,128]{1,0:T(8,128)S(1)} %get-tuple-element.16), channel_id=1, source_target_pairs={{0,4},{8,12},{16,20},{24,28},{32,36},{40,44},{48,52},{56,60},{64,6... | collective-permute-start | bytes 1241096 | tf_op jit(solution)/shard_map/ppermute | solution.py:547
  6.4 19.1 %collective-permute-start.1 = (f32[808,128]{1,0:T(8,128)S(1)}, f32[808,128]{1,0:T(8,128)S(1)}, u32[]{:S(2)}, u32[]{:S(2)}) collective-permute-start(f32[808,128]{1,0:T(8,128)S(1)} %get-tuple-element.17), channel_id=1, source_target_pairs={{4,8},{12,16},{20,24},{28,32},{36,40},{44,48},{52,56},{60,64},{68,... | collective-permute-start | bytes 1241096 | tf_op jit(solution)/shard_map/ppermute | solution.py:547
  11.0 24.2 %copy-start.1 = (f32[1,2,8,16,256]{4,3,2,1,0:T(8,128)S(1)}, f32[1,2,8,16,256]{4,3,2,1,0:T(8,128)}, u32[]{:S(2)}) copy-start(f32[1,2,8,16,256]{4,3,2,1,0:T(8,128)} %refs_4_.1) | copy-start | bytes 786436
  11.0 8.9 %collective-permute-start.2 = (f32[80,128]{1,0:T(8,128)S(1)}, f32[80,128]{1,0:T(8,128)S(1)}, u32[]{:S(2)}, u32[]{:S(2)}) collective-permute-start(f32[80,128]{1,0:T(8,128)S(1)} %get-tuple-element.18), channel_id=1, source_target_pairs={{0,8},{4,12},{16,24},{20,28},{32,40},{36,44},{48,56},{52,60},{64,7... | collective-permute-start | bytes 122888 | tf_op jit(solution)/shard_map/ppermute | solution.py:547
  11.1 9.2 %collective-permute-start.3 = (f32[80,128]{1,0:T(8,128)S(1)}, f32[80,128]{1,0:T(8,128)S(1)}, u32[]{:S(2)}, u32[]{:S(2)}) collective-permute-start(f32[80,128]{1,0:T(8,128)S(1)} %get-tuple-element.19), channel_id=1, source_target_pairs={{8,16},{12,20},{24,32},{28,36},{40,48},{44,52},{56,64},{60,68},{72... | collective-permute-start | bytes 122888 | tf_op jit(solution)/shard_map/ppermute | solution.py:547
  29.8 4.2 %collective-permute-start.5 = (f32[48,256]{1,0:T(8,128)S(1)}, f32[48,256]{1,0:T(8,128)S(1)}, u32[]{:S(2)}, u32[]{:S(2)}) collective-permute-start(f32[48,256]{1,0:T(8,128)S(1)} %get-tuple-element.26.refs_0_), channel_id=1, source_target_pairs={{0,2},{1,3},{2,0},{3,1},{4,6},{5,7},{6,4},{7,5},{8,10},{9,11},{10,... | collective-permute-start | bytes 147464 | tf_op jit(solution)/shard_map/ppermute | solution.py:592
  30.9 4.0 %collective-permute-start.4 = (f32[48,256]{1,0:T(8,128)S(1)}, f32[48,256]{1,0:T(8,128)S(1)}, u32[]{:S(2)}, u32[]{:S(2)}) collective-permute-start(f32[48,256]{1,0:T(8,128)S(1)} %get-tuple-element.26.refs_0_), channel_id=1, source_target_pairs={{0,1},{1,0},{2,3},{3,2},{4,5},{5,4},{6,7},{7,6},{8,9},{9,8},{10,11... | collective-permute-start | bytes 147464 | tf_op jit(solution)/shard_map/ppermute | solution.py:592
  34.0 1.2 %collective-permute-start.6 = (f32[48,256]{1,0:T(8,128)S(1)}, f32[48,256]{1,0:T(8,128)S(1)}, u32[]{:S(2)}, u32[]{:S(2)}) collective-permute-start(f32[48,256]{1,0:T(8,128)S(1)} %collective-permute-done.5.refs_2_), channel_id=1, source_target_pairs={{0,1},{1,0},{2,3},{3,2},{4,5},{5,4},{6,7},{7,6},{8,9},{9,8},{10,11... | collective-permute-start | bytes 147464 | tf_op jit(solution)/shard_map/ppermute | solution.py:592

commit v5 on v4

--- a/solution.py
+++ b/solution.py
@@ -7,8 +7,8 @@
 
 MASS_TERM = 0.25
 LANES = 128
-PAD, PAIR_PAD = 8, 4
-OWN, PAIRS, FIRST = 32, 24, 8
+OWN, ROWS, PAIRS, FIRST = 32, 48, 24, 8
+LOAD_AHEAD, TURN_AHEAD = 20, 4
 TILES = 8
 SIDE_END, VALUE_END = 8, 2
 SIDE = OWN * TILES
@@ -104,7 +104,7 @@
     return (jnp.maximum(-here, 0), 1 - here), jnp.minimum(2 - here, 3)
 
 
-def pack_kernel(counts_hbm, links_hbm, fields_hbm, near_a, near_b, shifts, counts, links, fields, sems):
+def pack_kernel(counts_hbm, links_hbm, fields_hbm, near_a, near_b, counts, links, fields, sems):
     copies = []
 
     def fetch(source, target):
@@ -120,10 +120,7 @@
     for copy in copies:
         copy.wait()
     position = lax.axis_index("box")
-    found = offsets(counts, position)
-    for k in range(4):
-        shifts[k] = found[k]
-    here = found[1]
+    here = offsets(counts, position)[1]
     held, move_up = slots(here)
     codes = jnp.zeros((8, LANES), jnp.float32)
     for box in range(2):
@@ -164,9 +161,9 @@
         message(near_b, True)
 
 
-def pack_far_kernel(shifts, fields, far_a, far_b):
+def pack_far_kernel(counts, fields, _, far_a, far_b):
     position = lax.axis_index("box")
-    move_up = slots(shifts[1])[1]
+    move_up = slots(offsets(counts, position)[1])[1]
 
     def far_message(out, upper):
         row = move_up if upper else 0
@@ -245,143 +242,76 @@
     return jnp.where(odd == 1, high, low), jnp.where(odd == 1, low, high)
 
 
-def nearby(ref, code, colour, box, tile):
-    mid = slice(FIRST, FIRST + PAIRS)
-    lane = lane_ids(PAIRS)
+def store_column(out, box, tile, cells):
+    out[box, tile, FIRST : FIRST + PAIRS, :] = cells
+    out[box, tile, FIRST - 1 : FIRST, :] = cells[PAIRS - 1 : PAIRS]
+    out[box, tile, FIRST + PAIRS : FIRST + PAIRS + 1, :] = cells[0:1]
+
+
+def block_rows(block, by=0):
+    return slice(FIRST + 8 * block + by, FIRST + 8 * block + 8 + by)
+
+
+def around(ref, colour, blocks, code, use):
+    lane = lane_ids(8)
     depth = lane & 31
-    ref = ref[1 - colour]
-    here_ = ref[box, tile, mid, :]
-    there = ref[1 - box, tile, mid, :]
-    across = jnp.where(
-        odd_lanes(PAIRS) == colour,
-        ref[box, tile, FIRST - 1 : FIRST - 1 + PAIRS, :],
-        ref[box, tile, FIRST + 1 : FIRST + 1 + PAIRS, :],
-    )
-    y_low = ref[box, (tile - 1) % TILES, mid, :]
-    if tile == 0:
-        y_low = jnp.where(code[box, 0] == 2, ref[1 - box, TILES - 1, mid, :], y_low)
-    y_high = ref[box, (tile + 1) % TILES, mid, :]
-    if tile == TILES - 1:
-        y_high = jnp.where(code[box, 1] == 2, ref[1 - box, 0, mid, :], y_high)
-    z_low = jnp.where(code[box, 2] == 2, there, here_)
-    z_high = jnp.where(code[box, 3] == 2, there, here_)
-    return (
-        across,
-        here_,
-        pltpu.roll(jnp.where(lane >= 96, y_low, here_), 32, 1),
-        pltpu.roll(jnp.where(lane < 32, y_high, here_), 96, 1),
-        jnp.where(depth == 0, pltpu.roll(z_low, 97, 1), pltpu.roll(here_, 1, 1)),
-        jnp.where(depth == 31, pltpu.roll(z_high, 31, 1), pltpu.roll(here_, 127, 1)),
-    )
-
-
-def make_weights(
-    shifts, links, fields, near_a, near_b, far_a, far_b, weight, source, diagonal, code, raw, raw_side, coef
-):
-    red_coef, black_coef = coef
-    position = lax.axis_index("box")
-    offset = [shifts[k] for k in range(4)]
-    _, here, after, _ = offset
-    first_box = 2 * position
-    even = position % 2 == 0
-    lower = position % 4 < 2
-
-    def place_local(box, row):
-        for tile in range(TILES):
-            lanes = slice(tile * LANES, (tile + 1) * LANES)
-            raw[box, tile, PAD : PAD + OWN, :] = fields[2, 0, row, :, lanes]
-            raw_side[box, tile, PAD : PAD + OWN, :] = fields[1, 0, row, :, lanes]
-
-    def place_moved(box, ref):
-        for tile in range(TILES):
-            raw[box, tile, PAD : PAD + OWN, :] = ref[OWN * tile : OWN * (tile + 1), :]
-            raw_side[box, tile, PAD : PAD + OWN, :] = ref[SIDE + OWN * tile : SIDE + OWN * (tile + 1), :]
-
-    place_own(here, after, even, place_local, place_moved, (near_a, near_b))
-    low_linked, low_swap = crossing(links, 0, first_box - 2)
-    high_linked, high_swap = crossing(links, 1, first_box + 2)
-    ones = jnp.ones((8, LANES), jnp.float32)
-    odd = odd_lanes(1)
-    for tile in range(TILES):
-        ends = neighbour_ends(
-            offset, even, lower, (low_swap, high_swap), fields, (near_a, near_b), (far_a, far_b), tile,
-            SIDE_ENDS, 0, SIDE_SIZES, side_end,
-        )
+    low_layer = odd_lanes(8) == colour
+    cells, up, down, turned = {}, {}, {}, {}
+
+    def load(block, tile):
         for box in range(2):
-            (below, side_below), (above, side_above) = ends[box]
-            for one in (raw, raw_side):
-                one[box, tile, 0:8, :] = ones
-                one[box, tile, PAD + OWN : PAD + OWN + 8, :] = ones
-            raw[box, tile, 3:4, :] = jnp.where(odd == 0, swap_depth(side_below[0:1]), below[0:1])
-            raw[box, tile, 4:8, :] = below
-            raw_side[box, tile, 4:8, :] = side_below
-            raw[box, tile, 40:44, :] = above
-            raw[box, tile, 44:45, :] = jnp.where(odd == 1, swap_depth(side_above[3:4]), above[3:4])
-            raw_side[box, tile, 40:44, :] = side_above
-
-    pair = row_ids(PAIRS)
-    tile_a, tile_b = near_a[LINKS : LINKS + 8, :], near_b[LINKS : LINKS + 8, :]
-    codes_below, codes_above = jnp.where(even, tile_b, tile_a), jnp.where(even, tile_a, tile_b)
-    for face in range(4):
-        spread = [
-            [jnp.broadcast_to(one[i : i + 1, face : face + 1], (PAIRS, LANES)) for i in range(2)]
-            for one in (codes_below, codes_above)
-        ]
+            at = block, box, tile
+            cells[at] = ref[box, tile, block_rows(block), :]
+            up[at] = pltpu.roll(cells[at], 32, 1)
+            down[at] = pltpu.roll(cells[at], 96, 1)
+
+    def turn(block, tile):
         for box in range(2):
-            below = jnp.where(low_swap, spread[0][1 - box], spread[0][box])
-            above = jnp.where(high_swap, spread[1][1 - box], spread[1][box])
-            own = link_code(links, box, face + 2, first_box).astype(jnp.float32)
-            code[box, face] = jnp.where(
-                pair < PAIR_PAD, below, jnp.where(pair < PAIR_PAD + 16, own, above)
+            at, there = (block, box, tile), (block, 1 - box, tile)
+            z_low = jnp.where(code(block, box, 2) == 2, down[there], down[at])
+            z_high = jnp.where(code(block, box, 3) == 2, up[there], up[at])
+            turned[at] = (
+                pltpu.roll(jnp.where(depth == 31, z_low, cells[at]), 1, 1),
+                pltpu.roll(jnp.where(depth == 0, z_high, cells[at]), LANES - 1, 1),
             )
 
-    odd = odd_lanes(PAIRS)
-    lane = lane_ids(PAIRS)
-    depth = lane & 31
-    mid = slice(FIRST, FIRST + PAIRS)
-    for box in range(2):
-        for tile in range(TILES):
-            red_coef[box, tile, mid, :], black_coef[box, tile, mid, :] = split_colours(raw, box, tile)
-            source[0, box, tile], source[1, box, tile] = split_colours(raw_side, box, tile)
-
-    for colour in range(2):
+    def finish(block, tile):
         for box in range(2):
-            cut_low = jnp.logical_not(low_linked[box])
-            cut_high = jnp.logical_not(high_linked[box])
-            low_rows = ((pair == PAIR_PAD) & cut_low) | ((pair == PAIR_PAD + 16) & cut_high)
-            high_rows = ((pair == PAIR_PAD + 15) & cut_high) | ((pair == PAIR_PAD - 1) & cut_low)
-            end = jnp.where(odd == colour, low_rows.astype(jnp.int32), high_rows.astype(jnp.int32)) == 1
-            none = [code[box, k] == 0 for k in range(4)]
-            for tile in range(TILES):
-                own = coef[colour][box, tile, mid, :]
-                near = nearby(coef, code, colour, box, tile)
-                lost = (
-                    end,
-                    None,
-                    (lane < 32) & none[0] if tile == 0 else None,
-                    (lane >= 96) & none[1] if tile == TILES - 1 else None,
-                    (depth == 0) & none[2],
-                    (depth == 31) & none[3],
-                )
-                total = jnp.full((PAIRS, LANES), MASS_TERM, jnp.float32)
-                kept = []
-                for one, gone in zip(near, lost, strict=True):
-                    if gone is None:
-                        w = 0.5 * (own + one)
-                        kept.append(w)
-                    else:
-                        w = 0.5 * (own + jnp.where(gone, own, one))
-                        kept.append(jnp.where(gone, 0.0, w))
-                    total = total + w
-                inverse = 1.0 / total
-                diagonal[colour, box, tile] = total
-                source[colour, box, tile] = source[colour, box, tile] * inverse
-                for d in range(6):
-                    weight[colour, d, box, tile] = kept[d] * inverse
+            at = block, box, tile
+            y_low, y_high = up[block, box, (tile - 1) % TILES], down[block, box, (tile + 1) % TILES]
+            if tile == 0:
+                y_low = jnp.where(code(block, box, 0) == 2, up[block, 1 - box, TILES - 1], y_low)
+            if tile == TILES - 1:
+                y_high = jnp.where(code(block, box, 1) == 2, down[block, 1 - box, 0], y_high)
+            across = jnp.where(
+                low_layer, ref[box, tile, block_rows(block, -1), :], ref[box, tile, block_rows(block, 1), :]
+            )
+            use(
+                block,
+                box,
+                tile,
+                (
+                    across,
+                    cells[at],
+                    jnp.where(lane >= 32, up[at], y_low),
+                    jnp.where(lane < 96, down[at], y_high),
+                    *turned[at],
+                ),
+            )
+
+    loads = [(block, (tile - 1) % TILES) for block in range(blocks) for tile in range(TILES)]
+    steps = [(block, tile) for block in range(blocks) for tile in range(TILES)]
+    for k in range(len(steps) + LOAD_AHEAD):
+        if k < len(loads):
+            load(*loads[k])
+        if 0 <= k - LOAD_AHEAD + TURN_AHEAD < len(steps):
+            turn(*steps[k - LOAD_AHEAD + TURN_AHEAD])
+        if k >= LOAD_AHEAD:
+            finish(*steps[k - LOAD_AHEAD])
 
 
 def smooth_kernel(
-    shifts,
+    counts,
     links,
     parents,
     fields,
@@ -396,7 +326,7 @@
     coarse,
     raw_coef,
     raw_side,
-    raw,
+    raw_value,
     red_coef,
     black_coef,
     red,
@@ -404,85 +334,171 @@
     weight,
     source,
     diagonal,
-    code,
+    halo_code,
+    sums,
 ):
-    make_weights(
-        shifts, links, fields, near_a, near_b, far_a, far_b,
-        weight, source, diagonal, code, raw_coef, raw_side, (red_coef, black_coef),
-    )
-    value = (red, black)
+    value, coef = (red, black), (red_coef, black_coef)
     position = lax.axis_index("box")
-    offset = [shifts[k] for k in range(4)]
+    offset = offsets(counts, position)
     _, here, after, _ = offset
     first_box = 2 * position
     even = position % 2 == 0
     lower = position % 4 < 2
+    near, far = (near_a, near_b), (far_a, far_b)
 
     def place_local(box, row):
         for tile in range(TILES):
-            raw[box, tile, PAD : PAD + OWN, :] = fields[0, 0, row, :, tile * LANES : (tile + 1) * LANES]
+            lanes = slice(tile * LANES, (tile + 1) * LANES)
+            raw_value[box, tile, 0:OWN, :] = fields[0, 0, row, :, lanes]
+            raw_side[box, tile, 0:OWN, :] = fields[1, 0, row, :, lanes]
+            raw_coef[box, tile, 0:OWN, :] = fields[2, 0, row, :, lanes]
 
     def place_moved(box, ref):
         for tile in range(TILES):
             packed = ref[VALUE + 16 * tile : VALUE + 16 * tile + 16, :]
-            raw[box, tile, PAD : PAD + 16, :] = packed
-            raw[box, tile, PAD + 16 : PAD + 32, :] = pltpu.roll(packed, 1, 0)
-
-    place_own(here, after, even, place_local, place_moved, (near_a, near_b))
-    swaps = (crossing(links, 0, first_box - 2)[1], crossing(links, 1, first_box + 2)[1])
-    zeros = jnp.zeros((8, LANES), jnp.float32)
+            raw_value[box, tile, 0:16, :] = packed
+            raw_value[box, tile, 16:32, :] = pltpu.roll(packed, 1, 0)
+            raw_side[box, tile, 0:OWN, :] = ref[SIDE + OWN * tile : SIDE + OWN * (tile + 1), :]
+            raw_coef[box, tile, 0:OWN, :] = ref[OWN * tile : OWN * (tile + 1), :]
+
+    place_own(here, after, even, place_local, place_moved, near)
+    low_linked, low_swap = crossing(links, 0, first_box - 2)
+    high_linked, high_swap = crossing(links, 1, first_box + 2)
+    swaps = (low_swap, high_swap)
+    ones = jnp.ones((16, LANES), jnp.float32)
+    zeros = jnp.zeros((16, LANES), jnp.float32)
+    odd = odd_lanes(1)
     for tile in range(TILES):
-        ends = neighbour_ends(
-            offset, even, lower, swaps, fields, (near_a, near_b), (far_a, far_b), tile,
-            VALUE_ENDS, FAR_VALUES, VALUE_SIZES, value_end,
+        sides = neighbour_ends(
+            offset, even, lower, swaps, fields, near, far, tile, SIDE_ENDS, 0, SIDE_SIZES, side_end
+        )
+        values = neighbour_ends(
+            offset, even, lower, swaps, fields, near, far, tile, VALUE_ENDS, FAR_VALUES, VALUE_SIZES, value_end
         )
         for box in range(2):
-            raw[box, tile, 0:8, :] = zeros
-            raw[box, tile, PAD + OWN : PAD + OWN + 8, :] = zeros
-            for base, pieces in zip((4, PAD + OWN), ends[box], strict=True):
+            (below, side_below), (above, side_above) = sides[box]
+            raw_coef[box, tile, 32:48, :] = ones
+            raw_side[box, tile, 32:48, :] = ones
+            raw_value[box, tile, 32:48, :] = zeros
+            raw_coef[box, tile, 43:44, :] = jnp.where(odd == 0, swap_depth(side_below[0:1]), below[0:1])
+            raw_coef[box, tile, 44:48, :] = below
+            raw_side[box, tile, 44:48, :] = side_below
+            raw_coef[box, tile, 32:36, :] = above
+            raw_coef[box, tile, 36:37, :] = jnp.where(odd == 1, swap_depth(side_above[3:4]), above[3:4])
+            raw_side[box, tile, 32:36, :] = side_above
+            for base, pieces in zip((44, 32), values[box], strict=True):
                 for k in range(4):
-                    raw[box, tile, base + k : base + k + 1, :] = pieces[k // 2]
-
-    mid = slice(FIRST, FIRST + PAIRS)
+                    raw_value[box, tile, base + k : base + k + 1, :] = pieces[k // 2]
+
+    own_code = [[link_code(links, box, face, first_box) for face in range(2, 6)] for box in range(2)]
+    tile_a, tile_b = near_a[LINKS : LINKS + 8, :], near_b[LINKS : LINKS + 8, :]
+    codes_below, codes_above = jnp.where(even, tile_b, tile_a), jnp.where(even, tile_a, tile_b)
+    for face in range(4):
+        spread = [
+            [jnp.broadcast_to(one[i : i + 1, face : face + 1], (8, LANES)) for i in range(2)]
+            for one in (codes_below, codes_above)
+        ]
+        for box in range(2):
+            below = jnp.where(low_swap, spread[0][1 - box], spread[0][box])
+            above = jnp.where(high_swap, spread[1][1 - box], spread[1][box])
+            halo_code[box, face] = jnp.where(row_ids(8) < 4, above, below)
+
+    def code(block, box, face):
+        return own_code[box][face] if block < 2 else halo_code[box, face]
+
     for box in range(2):
         for tile in range(TILES):
-            red[box, tile, mid, :], black[box, tile, mid, :] = split_colours(raw, box, tile)
-
-    def update(colour, box, tile):
-        total = source[colour, box, tile]
-        for d, one in enumerate(nearby(value, code, colour, box, tile)):
-            total = total + weight[colour, d, box, tile] * one
-        return total
+            for raw, out in ((raw_value, value), (raw_coef, coef)):
+                for colour, cells in enumerate(split_colours(raw, box, tile)):
+                    store_column(out[colour], box, tile, cells)
+            source[0, box, tile], source[1, box, tile] = split_colours(raw_side, box, tile)
+
+    lane = lane_ids(8)
+    depth = lane & 31
+    row = row_ids(8)
+
+    def weigh(colour):
+        low_layer = odd_lanes(8) == colour
+
+        def use(block, box, tile, near_coef):
+            rows = slice(8 * block, 8 * block + 8)
+            cut_low = jnp.logical_not(low_linked[box])
+            cut_high = jnp.logical_not(high_linked[box])
+            first_row, last_row = (row == 0) & low_layer, (row == 7) & jnp.logical_not(low_layer)
+            end = (
+                first_row & cut_low,
+                last_row & cut_high,
+                (first_row & cut_high) | (last_row & cut_low),
+            )[block]
+            lost = (
+                end,
+                None,
+                (lane < 32) & (code(block, box, 0) == 0) if tile == 0 else None,
+                (lane >= 96) & (code(block, box, 1) == 0) if tile == TILES - 1 else None,
+                (depth == 0) & (code(block, box, 2) == 0),
+                (depth == 31) & (code(block, box, 3) == 0),
+            )
+            own = coef[colour][box, tile, block_rows(block), :]
+            total = jnp.full((8, LANES), MASS_TERM, jnp.float32)
+            kept = []
+            for one, gone in zip(near_coef, lost, strict=True):
+                if gone is None:
+                    w = 0.5 * (own + one)
+                    kept.append(w)
+                else:
+                    w = 0.5 * (own + jnp.where(gone, own, one))
+                    kept.append(jnp.where(gone, 0.0, w))
+                total = total + w
+            inverse = 1.0 / total
+            diagonal[colour, box, tile, rows, :] = total
+            source[colour, box, tile, rows, :] = source[colour, box, tile, rows, :] * inverse
+            for d in range(6):
+                weight[colour, d, box, tile, rows, :] = kept[d] * inverse
+
+        around(coef[1 - colour], colour, 3, code, use)
+
+    weigh(0)
+    weigh(1)
+
+    def update(colour, blocks, take):
+        def use(block, box, tile, near_value):
+            rows = slice(8 * block, 8 * block + 8)
+            terms = [weight[colour, d, box, tile, rows, :] * one for d, one in enumerate(near_value)]
+            total = (terms[0] + terms[1]) + (terms[2] + terms[3]) + (terms[4] + terms[5])
+            take(block, box, tile, rows, source[colour, box, tile, rows, :] + total)
+
+        around(value[1 - colour], colour, blocks, code, use)
 
     def sweep(step, carry):
         for colour in range(2):
-            for box in range(2):
-                for tile in range(TILES):
-                    value[colour][box, tile, mid, :] = update(colour, box, tile)
+
+            def take(block, box, tile, rows, fresh, out=value[colour]):
+                out[box, tile, block_rows(block), :] = fresh
+                if block == 0:
+                    out[box, tile, FIRST + PAIRS : FIRST + PAIRS + 1, :] = fresh[0:1]
+                if block == 2:
+                    out[box, tile, FIRST - 1 : FIRST, :] = fresh[7:8]
+
+            update(colour, 3, take)
         return carry
 
     lax.fori_loop(0, 2, sweep, 0)
 
-    own_pairs = slice(PAIR_PAD, PAIR_PAD + 16)
-    own_rows = slice(FIRST + PAIR_PAD, FIRST + PAIR_PAD + 16)
     halves = TILES // 2
-    gathered = []
-    for half in range(2):
-        for box in range(2):
-            sums = []
-            for tile in range(half * halves, (half + 1) * halves):
-                total = None
-                for colour, out, left in ((0, red_out, red_left), (1, black_out, black_left)):
-                    kept = value[colour][box, tile, own_rows, :]
-                    out[box, tile] = kept
-                    rest = diagonal[colour, box, tile, own_pairs, :] * (
-                        update(colour, box, tile)[own_pairs] - kept
-                    )
-                    left[box, tile] = rest
-                    total = rest if total is None else total + rest
-                sums.append(total)
-            gathered.append(jnp.concatenate(sums, axis=1))
-    whole = jnp.concatenate(gathered, axis=0)
+    for colour, out, left in ((0, red_out, red_left), (1, black_out, black_left)):
+
+        def take(block, box, tile, rows, fresh, colour=colour, out=out, left=left):
+            kept = value[colour][box, tile, block_rows(block), :]
+            rest = diagonal[colour, box, tile, rows, :] * (fresh - kept)
+            out[box, tile, rows, :] = kept
+            left[box, tile, rows, :] = rest
+            if colour == 1:
+                at = 32 * (tile // halves) + 16 * box + 8 * block
+                lanes = slice(tile % halves * LANES, (tile % halves + 1) * LANES)
+                sums[at : at + 8, lanes] = red_left[box, tile, rows, :] + rest
+
+        update(colour, 2, take)
+    whole = sums[...]
     first = whole.astype(jnp.bfloat16)
     rest = whole - first.astype(jnp.float32)
     second = rest.astype(jnp.bfloat16)
@@ -546,11 +562,11 @@
         both = [(i, i + distance) for i in ids] + [(i + distance, i) for i in ids]
         return lax.ppermute(message, "box", both)
 
-    near_a, near_b, shifts = pl.pallas_call(
+    near_a, near_b = pl.pallas_call(
         pack_kernel,
-        out_shape=(rows(NEAR_ROWS), rows(NEAR_ROWS), jax.ShapeDtypeStruct((4,), jnp.int32)),
+        out_shape=(rows(NEAR_ROWS),) * 2,
         in_specs=[HBM] * 3,
-        out_specs=(VMEM, VMEM, SMEM),
+        out_specs=(VMEM,) * 2,
         scratch_shapes=[
             pltpu.SMEM(old_count.shape, old_count.dtype),
             pltpu.SMEM(neighbours.shape, neighbours.dtype),
@@ -564,18 +580,19 @@
     far_a, far_b = pl.pallas_call(
         pack_far_kernel,
         out_shape=(rows(FAR_ROWS),) * 2,
-        in_specs=[SMEM, VMEM],
+        in_specs=[SMEM, VMEM, pl.BlockSpec(memory_space=pl.ANY)],
         out_specs=(VMEM,) * 2,
         compiler_params=params,
         cost_estimate=cost(10**6, 2 << 20),
         name="pack_far",
-    )(shifts, old_fields)
+    )(old_count, old_fields, near_a)
     moved = [swap(near_a, 1, 0), swap(near_b, 1, 1), swap(far_a, 2, 0), swap(far_b, 2, 2)]
     packed = pltpu.VMEM((2, boxes, TILES, PAIRS, LANES), f32)
     column = pltpu.VMEM((boxes, TILES, PAIRS + 2 * FIRST, LANES), f32)
-    raw = pltpu.VMEM((boxes, TILES, OWN + 2 * PAD, LANES), f32)
+    raw = pltpu.VMEM((boxes, TILES, ROWS, LANES), f32)
     weight = pltpu.VMEM((2, 6, boxes, TILES, PAIRS, LANES), f32)
-    code = pltpu.VMEM((boxes, 4, PAIRS, LANES), f32)
+    code = pltpu.VMEM((boxes, 4, 8, LANES), f32)
+    sums = pltpu.VMEM((32 * boxes, TILES // 2 * LANES), f32)
     fine = jax.ShapeDtypeStruct((1, boxes, box_edge, plane_cells), f32)
     half = jax.ShapeDtypeStruct((boxes, TILES, box_edge // 2, LANES), f32)
     *halves, coarse = pl.pallas_call(
@@ -583,17 +600,16 @@
         out_shape=(half, half, half, half, jax.ShapeDtypeStruct((48, 2 * LANES), f32)),
         in_specs=[SMEM, SMEM, SMEM] + [VMEM] * 5,
         out_specs=(VMEM,) * 5,
-        scratch_shapes=[raw] * 3 + [column] * 4 + [weight, packed, packed, code],
+        scratch_shapes=[raw] * 3 + [column] * 4 + [weight, packed, packed, code, sums],
         compiler_params=params,
         cost_estimate=cost(10**7, 6 << 20),
         name="smooth",
-    )(shifts, neighbours, parents, old_fields, *moved)
-    def across(message, bit):
-        return lax.ppermute(message, "grp", [(i, i ^ bit) for i in range(groups)])
-
+    )(old_count, neighbours, parents, old_fields, *moved)
     groups = lax.axis_size("grp")
-    over_link = across(coarse, 2)
-    got = [coarse, across(coarse, 1), over_link, across(over_link, 1)]
+    got = [coarse] + [
+        lax.ppermute(coarse, "grp", [(i, (i + k) % groups) for i in range(groups)])
+        for k in range(1, groups)
+    ]
     smoothed, residual = pl.pallas_call(
         unpack_kernel,
         out_shape=(fine, fine),

time: 36.5 us -> 40 us (1.096)
  waiting for transfers between devices: 14.5 us -> 17.4 us
  starting transfers between devices: 11.7 us -> 14 us
  Pallas kernels: 9.1 us -> 7.67 us
    ppermute x4, waiting for transfers between devices: 11 us -> 14.7 us  [swap(): return lax.ppermute(message, 'box', both)]
    ppermute x4, starting transfers between devices: 10.6 us -> 12.3 us  [swap(): return lax.ppermute(message, 'box', both)]
    pallas_call x1, Pallas kernels: 4.34 us -> 3.44 us  [per_device(): pl.pallas_call(smooth_kernel, out_shape=(half, half, half, half, jax.Shap...]
    ppermute x3, waiting for transfers between devices: 3.48 us -> 2.71 us  [per_device(): lax.ppermute(coarse, 'grp', [(i, (i + k) % groups) for i in range(groups)])]
    ppermute x3, starting transfers between devices: 1.08 us -> 1.73 us  [per_device(): lax.ppermute(coarse, 'grp', [(i, (i + k) % groups) for i in range(groups)])]
    pallas_call x1, Pallas kernels: 2.42 us -> 1.83 us  [per_device(): pl.pallas_call(pack_kernel, out_shape=(rows(NEAR_ROWS),) * 2, in_specs=[H...]
where the time goes in v5:
time: 40 us; the launch traced here: 39.9 us
  waiting for transfers between devices  17.4 us (43%)
  starting transfers between devices  14 us (35%)
  Pallas kernels  7.67 us (19%)
  between operations  0.74 us (2%)
    ppermute x4, waiting for transfers between devices, swap(): return lax.ppermute(message, 'box', both)  14.7 us
    ppermute x4, starting transfers between devices, swap(): return lax.ppermute(message, 'box', both)  12.3 us
    pallas_call x1, Pallas kernels, per_device(): pl.pallas_call(smooth_kernel, out_shape=(half, half, half, half, jax.Shap...  3.44 us
    ppermute x3, waiting for transfers between devices, per_device(): lax.ppermute(coarse, 'grp', [(i, (i + k) % groups) for i in range(groups)])  2.71 us
    pallas_call x1, Pallas kernels, per_device(): pl.pallas_call(pack_kernel, out_shape=(rows(NEAR_ROWS),) * 2, in_specs=[H...  1.83 us
    ppermute x3, starting transfers between devices, per_device(): lax.ppermute(coarse, 'grp', [(i, (i + k) % groups) for i in range(groups)])  1.73 us
    pallas_call x1, Pallas kernels, per_device(): pl.pallas_call(unpack_kernel, out_shape=(fine, fine), in_specs=[VMEM] * 4...  0.85 us
    pallas_call x1, Pallas kernels, per_device(): pl.pallas_call(place_kernel, out_shape=jax.ShapeDtypeStruct(coarse_source...  0.82 us
  transfers between devices with their start and end apart: 7, of which 6 were waited for; matrix products, arithmetic and copies ran while one was open for 0% of the time, Pallas kernels for 4%

profile of v5, /device:TPU:128, one launch (start us, length us, event | category | flops | bytes accessed | tf_op | source)
XLA Modules:
  0.0 39.9 jit_solution(6767313410885098412)
XLA Ops:
  0.6 0.0 copy-start.2
  0.6 0.0 copy-start
  0.7 0.0 copy-start.3
  0.7 0.0 copy-start.4
  0.7 1.8 %pack.1 = (f32[808,128]{1,0:T(8,128)S(1)}, f32[808,128]{1,0:T(8,128)S(1)}) custom-call(s32[1,64]{1,0:T(1,128)} %counts.3, s32[1,2,6]{2,1,0:T(2,128)} %links.1, f32[3,1,4,32,1024]{4,3,2,1,0:T(8,128)} %fields.3), custom_call_target="tpu_custom_call" | custom-call | flops 1000000 | bytes 2097152 | tf_op jit(solution)/shard_map/pack/pallas_call | solution.py:565
  2.5 6.8 %collective-permute-start.1 = (f32[808,128]{1,0:T(8,128)S(1)}, f32[808,128]{1,0:T(8,128)S(1)}, u32[]{:S(2)}, u32[]{:S(2)}) collective-permute-start(f32[808,128]{1,0:T(8,128)S(1)} %get-tuple-element.15), channel_id=1, source_target_pairs={{4,8},{12,16},{20,24},{28,32},{36,40},{44,48},{52,56},{60,64},{68,... | collective-permute-start | bytes 1241096 | tf_op jit(solution)/shard_map/ppermute | solution.py:563
  9.4 0.1 collective-permute-start
  9.5 0.0 copy-done.2
  9.5 0.0 copy-done
  9.5 0.7 %pack_far.1 = (f32[80,128]{1,0:T(8,128)S(1)}, f32[80,128]{1,0:T(8,128)S(1)}) custom-call(s32[1,64]{1,0:T(1,128)S(1)} %copy-done.2, f32[3,1,4,32,1024]{4,3,2,1,0:T(8,128)S(1)} %copy-done, f32[808,128]{1,0:T(8,128)S(1)} %get-tuple-element.14._), custom_call_target="tpu_custom_call" | custom-call | flops 1000000 | bytes 2097152 | tf_op jit(solution)/shard_map/pack_far/pallas_call | solution.py:580
  10.2 0.0 copy-start.1
  10.2 1.1 %collective-permute-start.2 = (f32[80,128]{1,0:T(8,128)S(1)}, f32[80,128]{1,0:T(8,128)S(1)}, u32[]{:S(2)}, u32[]{:S(2)}) collective-permute-start(f32[80,128]{1,0:T(8,128)S(1)} %get-tuple-element.16), channel_id=1, source_target_pairs={{0,8},{4,12},{16,24},{20,28},{32,40},{36,44},{48,56},{52,60},{64,7... | collective-permute-start | bytes 122888 | tf_op jit(solution)/shard_map/ppermute | solution.py:563
  11.3 4.3 %collective-permute-start.3 = (f32[80,128]{1,0:T(8,128)S(1)}, f32[80,128]{1,0:T(8,128)S(1)}, u32[]{:S(2)}, u32[]{:S(2)}) collective-permute-start(f32[80,128]{1,0:T(8,128)S(1)} %get-tuple-element.17), channel_id=1, source_target_pairs={{8,16},{12,20},{24,32},{28,36},{40,48},{44,52},{56,64},{60,68},{72... | collective-permute-start | bytes 122888 | tf_op jit(solution)/shard_map/ppermute | solution.py:563
  15.6 3.7 %collective-permute-done.2.far_a = f32[80,128]{1,0:T(8,128)S(1)} collective-permute-done((f32[80,128]{1,0:T(8,128)S(1)}, f32[80,128]{1,0:T(8,128)S(1)}, u32[]{:S(2)}, u32[]{:S(2)}) %collective-permute-start.2) | collective-permute-done | bytes 40992 | tf_op jit(solution)/shard_map/ppermute | solution.py:563
  19.3 1.2 %collective-permute-done.3.far_b = f32[80,128]{1,0:T(8,128)S(1)} collective-permute-done((f32[80,128]{1,0:T(8,128)S(1)}, f32[80,128]{1,0:T(8,128)S(1)}, u32[]{:S(2)}, u32[]{:S(2)}) %collective-permute-start.3) | collective-permute-done | bytes 40992 | tf_op jit(solution)/shard_map/ppermute | solution.py:563
  20.5 1.4 %collective-permute-done.1.near_b = f32[808,128]{1,0:T(8,128)S(1)} collective-permute-done((f32[808,128]{1,0:T(8,128)S(1)}, f32[808,128]{1,0:T(8,128)S(1)}, u32[]{:S(2)}, u32[]{:S(2)}) %collective-permute-start.1) | collective-permute-done | bytes 413728 | tf_op jit(solution)/shard_map/ppermute | solution.py:563
  21.9 8.4 %collective-permute-done.near_a = f32[808,128]{1,0:T(8,128)S(1)} collective-permute-done((f32[808,128]{1,0:T(8,128)S(1)}, f32[808,128]{1,0:T(8,128)S(1)}, u32[]{:S(2)}, u32[]{:S(2)}) %collective-permute-start) | collective-permute-done | bytes 413728 | tf_op jit(solution)/shard_map/ppermute | solution.py:563
  30.3 0.0 copy-done.3
  30.3 0.0 copy-done.4
  30.3 3.4 %smooth.1 = (f32[2,8,16,128]{3,2,1,0:T(8,128)S(1)}, f32[2,8,16,128]{3,2,1,0:T(8,128)S(1)}, f32[2,8,16,128]{3,2,1,0:T(8,128)S(1)}, f32[2,8,16,128]{3,2,1,0:T(8,128)S(1)}, f32[48,256]{1,0:T(8,128)S(1)}) custom-call(s32[1,64]{1,0:T(1,128)S(1)} %copy-done.2, s32[1,2,6]{2,1,0:T(2,128)S(1)} %copy-done.3, s32[1,2,3]{2,1,0:T(2,128)S(1)} %copy-done.4, ...), custom_call_target="tpu_custom_call" | custom-call | flops 10000000 | bytes 6291456 | tf_op jit(solution)/shard_map/smooth/pallas_call | solution.py:598
  33.7 0.5 %collective-permute-start.6 = (f32[48,256]{1,0:T(8,128)S(1)}, f32[48,256]{1,0:T(8,128)S(1)}, u32[]{:S(2)}, u32[]{:S(2)}) collective-permute-start(f32[48,256]{1,0:T(8,128)S(1)} %get-tuple-element.24.refs_0_), channel_id=1, source_target_pairs={{0,3},{1,0},{2,1},{3,2},{4,7},{5,4},{6,5},{7,6},{8,11},{9,8},{10,9... | collective-permute-start | bytes 147464 | tf_op jit(solution)/shard_map/ppermute | solution.py:610
  34.3 1.2 %collective-permute-start.5 = (f32[48,256]{1,0:T(8,128)S(1)}, f32[48,256]{1,0:T(8,128)S(1)}, u32[]{:S(2)}, u32[]{:S(2)}) collective-permute-start(f32[48,256]{1,0:T(8,128)S(1)} %get-tuple-element.24.refs_0_), channel_id=1, source_target_pairs={{0,2},{1,3},{2,0},{3,1},{4,6},{5,7},{6,4},{7,5},{8,10},{9,11},{10,... | collective-permute-start | bytes 147464 | tf_op jit(solution)/shard_map/ppermute | solution.py:610
  35.5 0.0 collective-permute-start.4
  35.5 0.8 %unpack.1 = (f32[1,2,32,1024]{3,2,1,0:T(8,128)}, f32[1,2,32,1024]{3,2,1,0:T(8,128)}) custom-call(f32[2,8,16,128]{3,2,1,0:T(8,128)S(1)} %get-tuple-element.18.red, f32[2,8,16,128]{3,2,1,0:T(8,128)S(1)} %get-tuple-element.19.black, f32[2,8,16,128]{3,2,1,0:T(8,128)S(1)} %get-tuple-element.20.red_left, f32[2,8,16,128]{3,2,1,0:T(8,128)S(1)} %get-tuple-element.21.black_left), custom_call_target="tpu_custom_call" | custom-call | flops 1000000 | bytes 3145728 | tf_op jit(solution)/shard_map/unpack/pallas_call | solution.py:613
  36.3 0.0 collective-permute-done.6.refs_3_
  36.3 2.2 %collective-permute-done.5.refs_2_ = f32[48,256]{1,0:T(8,128)S(1)} collective-permute-done((f32[48,256]{1,0:T(8,128)S(1)}, f32[48,256]{1,0:T(8,128)S(1)}, u32[]{:S(2)}, u32[]{:S(2)}) %collective-permute-start.5) | collective-permute-done | bytes 49184 | tf_op jit(solution)/shard_map/ppermute | solution.py:610
  38.5 0.5 %collective-permute-done.4.refs_1_ = f32[48,256]{1,0:T(8,128)S(1)} collective-permute-done((f32[48,256]{1,0:T(8,128)S(1)}, f32[48,256]{1,0:T(8,128)S(1)}, u32[]{:S(2)}, u32[]{:S(2)}) %collective-permute-start.4) | collective-permute-done | bytes 49184 | tf_op jit(solution)/shard_map/ppermute | solution.py:610
  39.0 0.0 copy-done.1
  39.0 0.8 %place.1 = f32[1,2,8,16,256]{4,3,2,1,0:T(8,128)} custom-call(f32[48,256]{1,0:T(8,128)S(1)} %get-tuple-element.24.refs_0_, f32[48,256]{1,0:T(8,128)S(1)} %collective-permute-done.4.refs_1_, f32[48,256]{1,0:T(8,128)S(1)} %collective-permute-done.5.refs_2_, f32[48,256]{1,0:T(8,128)S(1)} %collective-permute-done.6.refs_3_, f32[1,2,8,16,256]{4,3,2,1,0:T(8,128)S(1)} %copy-done.1), custom_call_target="tpu_custom_call" | custom-call | flops 1000000 | bytes 1048576 | tf_op jit(solution)/shard_map/place/pallas_call | solution.py:623
Async XLA Ops:
  0.6 8.8 %copy-start.2 = (s32[1,64]{1,0:T(1,128)S(1)}, s32[1,64]{1,0:T(1,128)}, u32[]{:S(2)}) copy-start(s32[1,64]{1,0:T(1,128)} %counts.3) | copy-start | bytes 772
  0.6 8.8 %copy-start = (f32[3,1,4,32,1024]{4,3,2,1,0:T(8,128)S(1)}, f32[3,1,4,32,1024]{4,3,2,1,0:T(8,128)}, u32[]{:S(2)}) copy-start(f32[3,1,4,32,1024]{4,3,2,1,0:T(8,128)} %fields.3) | copy-start | bytes 4718596
  0.7 29.6 %copy-start.3 = (s32[1,2,6]{2,1,0:T(2,128)S(1)}, s32[1,2,6]{2,1,0:T(2,128)}, u32[]{:S(2)}) copy-start(s32[1,2,6]{2,1,0:T(2,128)} %links.1) | copy-start | bytes 148
  0.7 29.6 %copy-start.4 = (s32[1,2,3]{2,1,0:T(2,128)S(1)}, s32[1,2,3]{2,1,0:T(2,128)}, u32[]{:S(2)}) copy-start(s32[1,2,3]{2,1,0:T(2,128)} %parents.1) | copy-start | bytes 76
  2.5 19.4 %collective-permute-start.1 = (f32[808,128]{1,0:T(8,128)S(1)}, f32[808,128]{1,0:T(8,128)S(1)}, u32[]{:S(2)}, u32[]{:S(2)}) collective-permute-start(f32[808,128]{1,0:T(8,128)S(1)} %get-tuple-element.15), channel_id=1, source_target_pairs={{4,8},{12,16},{20,24},{28,32},{36,40},{44,48},{52,56},{60,64},{68,... | collective-permute-start | bytes 1241096 | tf_op jit(solution)/shard_map/ppermute | solution.py:563
  9.4 20.9 %collective-permute-start = (f32[808,128]{1,0:T(8,128)S(1)}, f32[808,128]{1,0:T(8,128)S(1)}, u32[]{:S(2)}, u32[]{:S(2)}) collective-permute-start(f32[808,128]{1,0:T(8,128)S(1)} %get-tuple-element.14._), channel_id=1, source_target_pairs={{0,4},{8,12},{16,20},{24,28},{32,36},{40,44},{48,52},{56,60},{64,6... | collective-permute-start | bytes 1241096 | tf_op jit(solution)/shard_map/ppermute | solution.py:563
  10.2 28.8 %copy-start.1 = (f32[1,2,8,16,256]{4,3,2,1,0:T(8,128)S(1)}, f32[1,2,8,16,256]{4,3,2,1,0:T(8,128)}, u32[]{:S(2)}) copy-start(f32[1,2,8,16,256]{4,3,2,1,0:T(8,128)} %refs_4_.1) | copy-start | bytes 786436
  10.2 9.0 %collective-permute-start.2 = (f32[80,128]{1,0:T(8,128)S(1)}, f32[80,128]{1,0:T(8,128)S(1)}, u32[]{:S(2)}, u32[]{:S(2)}) collective-permute-start(f32[80,128]{1,0:T(8,128)S(1)} %get-tuple-element.16), channel_id=1, source_target_pairs={{0,8},{4,12},{16,24},{20,28},{32,40},{36,44},{48,56},{52,60},{64,7... | collective-permute-start | bytes 122888 | tf_op jit(solution)/shard_map/ppermute | solution.py:563
  11.3 9.2 %collective-permute-start.3 = (f32[80,128]{1,0:T(8,128)S(1)}, f32[80,128]{1,0:T(8,128)S(1)}, u32[]{:S(2)}, u32[]{:S(2)}) collective-permute-start(f32[80,128]{1,0:T(8,128)S(1)} %get-tuple-element.17), channel_id=1, source_target_pairs={{8,16},{12,20},{24,32},{28,36},{40,48},{44,52},{56,64},{60,68},{72... | collective-permute-start | bytes 122888 | tf_op jit(solution)/shard_map/ppermute | solution.py:563
  33.7 2.6 %collective-permute-start.6 = (f32[48,256]{1,0:T(8,128)S(1)}, f32[48,256]{1,0:T(8,128)S(1)}, u32[]{:S(2)}, u32[]{:S(2)}) collective-permute-start(f32[48,256]{1,0:T(8,128)S(1)} %get-tuple-element.24.refs_0_), channel_id=1, source_target_pairs={{0,3},{1,0},{2,1},{3,2},{4,7},{5,4},{6,5},{7,6},{8,11},{9,8},{10,9... | collective-permute-start | bytes 147464 | tf_op jit(solution)/shard_map/ppermute | solution.py:610
  34.3 4.2 %collective-permute-start.5 = (f32[48,256]{1,0:T(8,128)S(1)}, f32[48,256]{1,0:T(8,128)S(1)}, u32[]{:S(2)}, u32[]{:S(2)}) collective-permute-start(f32[48,256]{1,0:T(8,128)S(1)} %get-tuple-element.24.refs_0_), channel_id=1, source_target_pairs={{0,2},{1,3},{2,0},{3,1},{4,6},{5,7},{6,4},{7,5},{8,10},{9,11},{10,... | collective-permute-start | bytes 147464 | tf_op jit(solution)/shard_map/ppermute | solution.py:610
  35.5 3.6 %collective-permute-start.4 = (f32[48,256]{1,0:T(8,128)S(1)}, f32[48,256]{1,0:T(8,128)S(1)}, u32[]{:S(2)}, u32[]{:S(2)}) collective-permute-start(f32[48,256]{1,0:T(8,128)S(1)} %get-tuple-element.24.refs_0_), channel_id=1, source_target_pairs={{0,1},{1,2},{2,3},{3,0},{4,5},{5,6},{6,7},{7,4},{8,9},{9,10},{10,1... | collective-permute-start | bytes 147464 | tf_op jit(solution)/shard_map/ppermute | solution.py:610

commit v6 on v5

--- a/solution.py
+++ b/solution.py
@@ -585,7 +585,7 @@
         compiler_params=params,
         cost_estimate=cost(10**6, 2 << 20),
         name="pack_far",
-    )(old_count, old_fields, near_a)
+    )(old_count, old_fields, near_b)
     moved = [swap(near_a, 1, 0), swap(near_b, 1, 1), swap(far_a, 2, 0), swap(far_b, 2, 2)]
     packed = pltpu.VMEM((2, boxes, TILES, PAIRS, LANES), f32)
     column = pltpu.VMEM((boxes, TILES, PAIRS + 2 * FIRST, LANES), f32)

time: 40 us -> 34.1 us (0.85)
  waiting for transfers between devices: 17.4 us -> 13.6 us
  starting transfers between devices: 14 us -> 11.9 us
    ppermute x4, waiting for transfers between devices: 14.7 us -> 11 us  [swap(): return lax.ppermute(message, 'box', both)]
    ppermute x4, starting transfers between devices: 12.3 us -> 10.6 us  [swap(): return lax.ppermute(message, 'box', both)]
    ppermute x3, starting transfers between devices: 1.73 us -> 1.31 us  [per_device(): lax.ppermute(coarse, 'grp', [(i, (i + k) % groups) for i in range(groups)])]
  transfers between devices with their start and end apart: 7 -> 7, of which waited for: 6 -> 6; matrix products, arithmetic and copies ran while one was open for 0% -> 0% of each run, Pallas kernels for 4% -> 5%
where the time goes in v6:
time: 34.1 us; the launch traced here: 33.9 us
  waiting for transfers between devices  13.6 us (40%)
  starting transfers between devices  11.9 us (35%)
  Pallas kernels  7.66 us (22%)
  between operations  0.75 us (2%)
    ppermute x4, waiting for transfers between devices, swap(): return lax.ppermute(message, 'box', both)  11 us
    ppermute x4, starting transfers between devices, swap(): return lax.ppermute(message, 'box', both)  10.6 us
    pallas_call x1, Pallas kernels, per_device(): pl.pallas_call(smooth_kernel, out_shape=(half, half, half, half, jax.Shap...  3.44 us
    ppermute x3, waiting for transfers between devices, per_device(): lax.ppermute(coarse, 'grp', [(i, (i + k) % groups) for i in range(groups)])  2.63 us
    pallas_call x1, Pallas kernels, per_device(): pl.pallas_call(pack_kernel, out_shape=(rows(NEAR_ROWS),) * 2, in_specs=[H...  1.83 us
    ppermute x3, starting transfers between devices, per_device(): lax.ppermute(coarse, 'grp', [(i, (i + k) % groups) for i in range(groups)])  1.31 us
    pallas_call x1, Pallas kernels, per_device(): pl.pallas_call(unpack_kernel, out_shape=(fine, fine), in_specs=[VMEM] * 4...  0.84 us
    pallas_call x1, Pallas kernels, per_device(): pl.pallas_call(place_kernel, out_shape=jax.ShapeDtypeStruct(coarse_source...  0.82 us
  transfers between devices with their start and end apart: 7, of which 6 were waited for; matrix products, arithmetic and copies ran while one was open for 0% of the time, Pallas kernels for 5%

profile of v6, /device:TPU:128, one launch (start us, length us, event | category | flops | bytes accessed | tf_op | source)
XLA Modules:
  0.0 33.9 jit_solution(7918498425561682284)
XLA Ops:
  0.6 0.0 copy-start.2
  0.6 0.0 copy-start
  0.7 0.0 copy-start.3
  0.7 0.0 copy-start.4
  0.7 1.8 %pack.1 = (f32[808,128]{1,0:T(8,128)S(1)}, f32[808,128]{1,0:T(8,128)S(1)}) custom-call(s32[1,64]{1,0:T(1,128)} %counts.3, s32[1,2,6]{2,1,0:T(2,128)} %links.1, f32[3,1,4,32,1024]{4,3,2,1,0:T(8,128)} %fields.3), custom_call_target="tpu_custom_call" | custom-call | flops 1000000 | bytes 2097152 | tf_op jit(solution)/shard_map/pack/pallas_call | solution.py:565
  2.5 3.3 %collective-permute-start = (f32[808,128]{1,0:T(8,128)S(1)}, f32[808,128]{1,0:T(8,128)S(1)}, u32[]{:S(2)}, u32[]{:S(2)}) collective-permute-start(f32[808,128]{1,0:T(8,128)S(1)} %get-tuple-element.14), channel_id=1, source_target_pairs={{0,4},{8,12},{16,20},{24,28},{32,36},{40,44},{48,52},{56,60},{64,6... | collective-permute-start | bytes 1241096 | tf_op jit(solution)/shard_map/ppermute | solution.py:563
  5.8 4.0 %collective-permute-start.1 = (f32[808,128]{1,0:T(8,128)S(1)}, f32[808,128]{1,0:T(8,128)S(1)}, u32[]{:S(2)}, u32[]{:S(2)}) collective-permute-start(f32[808,128]{1,0:T(8,128)S(1)} %get-tuple-element.15._), channel_id=1, source_target_pairs={{4,8},{12,16},{20,24},{28,32},{36,40},{44,48},{52,56},{60,64},{68,... | collective-permute-start | bytes 1241096 | tf_op jit(solution)/shard_map/ppermute | solution.py:563
  9.8 0.0 copy-done.2
  9.8 0.0 copy-done
  9.8 0.7 %pack_far.1 = (f32[80,128]{1,0:T(8,128)S(1)}, f32[80,128]{1,0:T(8,128)S(1)}) custom-call(s32[1,64]{1,0:T(1,128)S(1)} %copy-done.2, f32[3,1,4,32,1024]{4,3,2,1,0:T(8,128)S(1)} %copy-done, f32[808,128]{1,0:T(8,128)S(1)} %get-tuple-element.15._), custom_call_target="tpu_custom_call" | custom-call | flops 1000000 | bytes 2097152 | tf_op jit(solution)/shard_map/pack_far/pallas_call | solution.py:580
  10.5 0.0 copy-start.1
  10.5 0.1 collective-permute-start.2
  10.6 3.2 %collective-permute-start.3 = (f32[80,128]{1,0:T(8,128)S(1)}, f32[80,128]{1,0:T(8,128)S(1)}, u32[]{:S(2)}, u32[]{:S(2)}) collective-permute-start(f32[80,128]{1,0:T(8,128)S(1)} %get-tuple-element.17), channel_id=1, source_target_pairs={{8,16},{12,20},{24,32},{28,36},{40,48},{44,52},{56,64},{60,68},{72... | collective-permute-start | bytes 122888 | tf_op jit(solution)/shard_map/ppermute | solution.py:563
  13.9 5.5 %collective-permute-done.2.far_a = f32[80,128]{1,0:T(8,128)S(1)} collective-permute-done((f32[80,128]{1,0:T(8,128)S(1)}, f32[80,128]{1,0:T(8,128)S(1)}, u32[]{:S(2)}, u32[]{:S(2)}) %collective-permute-start.2) | collective-permute-done | bytes 40992 | tf_op jit(solution)/shard_map/ppermute | solution.py:563
  19.4 0.5 %collective-permute-done.3.far_b = f32[80,128]{1,0:T(8,128)S(1)} collective-permute-done((f32[80,128]{1,0:T(8,128)S(1)}, f32[80,128]{1,0:T(8,128)S(1)}, u32[]{:S(2)}, u32[]{:S(2)}) %collective-permute-start.3) | collective-permute-done | bytes 40992 | tf_op jit(solution)/shard_map/ppermute | solution.py:563
  19.9 3.6 %collective-permute-done.near_a = f32[808,128]{1,0:T(8,128)S(1)} collective-permute-done((f32[808,128]{1,0:T(8,128)S(1)}, f32[808,128]{1,0:T(8,128)S(1)}, u32[]{:S(2)}, u32[]{:S(2)}) %collective-permute-start) | collective-permute-done | bytes 413728 | tf_op jit(solution)/shard_map/ppermute | solution.py:563
  23.5 1.4 %collective-permute-done.1.near_b = f32[808,128]{1,0:T(8,128)S(1)} collective-permute-done((f32[808,128]{1,0:T(8,128)S(1)}, f32[808,128]{1,0:T(8,128)S(1)}, u32[]{:S(2)}, u32[]{:S(2)}) %collective-permute-start.1) | collective-permute-done | bytes 413728 | tf_op jit(solution)/shard_map/ppermute | solution.py:563
  24.9 0.0 copy-done.3
  24.9 0.0 copy-done.4
  24.9 3.4 %smooth.1 = (f32[2,8,16,128]{3,2,1,0:T(8,128)S(1)}, f32[2,8,16,128]{3,2,1,0:T(8,128)S(1)}, f32[2,8,16,128]{3,2,1,0:T(8,128)S(1)}, f32[2,8,16,128]{3,2,1,0:T(8,128)S(1)}, f32[48,256]{1,0:T(8,128)S(1)}) custom-call(s32[1,64]{1,0:T(1,128)S(1)} %copy-done.2, s32[1,2,6]{2,1,0:T(2,128)S(1)} %copy-done.3, s32[1,2,3]{2,1,0:T(2,128)S(1)} %copy-done.4, ...), custom_call_target="tpu_custom_call" | custom-call | flops 10000000 | bytes 6291456 | tf_op jit(solution)/shard_map/smooth/pallas_call | solution.py:598
  28.3 0.1 collective-permute-start.6
  28.4 1.1 %collective-permute-start.5 = (f32[48,256]{1,0:T(8,128)S(1)}, f32[48,256]{1,0:T(8,128)S(1)}, u32[]{:S(2)}, u32[]{:S(2)}) collective-permute-start(f32[48,256]{1,0:T(8,128)S(1)} %get-tuple-element.24.refs_0_), channel_id=1, source_target_pairs={{0,2},{1,3},{2,0},{3,1},{4,6},{5,7},{6,4},{7,5},{8,10},{9,11},{10,... | collective-permute-start | bytes 147464 | tf_op jit(solution)/shard_map/ppermute | solution.py:610
  29.5 0.1 collective-permute-start.4
  29.6 0.8 %unpack.1 = (f32[1,2,32,1024]{3,2,1,0:T(8,128)}, f32[1,2,32,1024]{3,2,1,0:T(8,128)}) custom-call(f32[2,8,16,128]{3,2,1,0:T(8,128)S(1)} %get-tuple-element.18.red, f32[2,8,16,128]{3,2,1,0:T(8,128)S(1)} %get-tuple-element.19.black, f32[2,8,16,128]{3,2,1,0:T(8,128)S(1)} %get-tuple-element.20.red_left, f32[2,8,16,128]{3,2,1,0:T(8,128)S(1)} %get-tuple-element.21.black_left), custom_call_target="tpu_custom_call" | custom-call | flops 1000000 | bytes 3145728 | tf_op jit(solution)/shard_map/unpack/pallas_call | solution.py:613
  30.5 0.0 collective-permute-done.6.refs_3_
  30.5 2.3 %collective-permute-done.5.refs_2_ = f32[48,256]{1,0:T(8,128)S(1)} collective-permute-done((f32[48,256]{1,0:T(8,128)S(1)}, f32[48,256]{1,0:T(8,128)S(1)}, u32[]{:S(2)}, u32[]{:S(2)}) %collective-permute-start.5) | collective-permute-done | bytes 49184 | tf_op jit(solution)/shard_map/ppermute | solution.py:610
  32.8 0.3 %collective-permute-done.4.refs_1_ = f32[48,256]{1,0:T(8,128)S(1)} collective-permute-done((f32[48,256]{1,0:T(8,128)S(1)}, f32[48,256]{1,0:T(8,128)S(1)}, u32[]{:S(2)}, u32[]{:S(2)}) %collective-permute-start.4) | collective-permute-done | bytes 49184 | tf_op jit(solution)/shard_map/ppermute | solution.py:610
  33.1 0.0 copy-done.1
  33.1 0.8 %place.1 = f32[1,2,8,16,256]{4,3,2,1,0:T(8,128)} custom-call(f32[48,256]{1,0:T(8,128)S(1)} %get-tuple-element.24.refs_0_, f32[48,256]{1,0:T(8,128)S(1)} %collective-permute-done.4.refs_1_, f32[48,256]{1,0:T(8,128)S(1)} %collective-permute-done.5.refs_2_, f32[48,256]{1,0:T(8,128)S(1)} %collective-permute-done.6.refs_3_, f32[1,2,8,16,256]{4,3,2,1,0:T(8,128)S(1)} %copy-done.1), custom_call_target="tpu_custom_call" | custom-call | flops 1000000 | bytes 1048576 | tf_op jit(solution)/shard_map/place/pallas_call | solution.py:623
Async XLA Ops:
  0.6 9.1 %copy-start.2 = (s32[1,64]{1,0:T(1,128)S(1)}, s32[1,64]{1,0:T(1,128)}, u32[]{:S(2)}) copy-start(s32[1,64]{1,0:T(1,128)} %counts.3) | copy-start | bytes 772
  0.6 9.1 %copy-start = (f32[3,1,4,32,1024]{4,3,2,1,0:T(8,128)S(1)}, f32[3,1,4,32,1024]{4,3,2,1,0:T(8,128)}, u32[]{:S(2)}) copy-start(f32[3,1,4,32,1024]{4,3,2,1,0:T(8,128)} %fields.3) | copy-start | bytes 4718596
  0.7 24.2 %copy-start.3 = (s32[1,2,6]{2,1,0:T(2,128)S(1)}, s32[1,2,6]{2,1,0:T(2,128)}, u32[]{:S(2)}) copy-start(s32[1,2,6]{2,1,0:T(2,128)} %links.1) | copy-start | bytes 148
  0.7 24.2 %copy-start.4 = (s32[1,2,3]{2,1,0:T(2,128)S(1)}, s32[1,2,3]{2,1,0:T(2,128)}, u32[]{:S(2)}) copy-start(s32[1,2,3]{2,1,0:T(2,128)} %parents.1) | copy-start | bytes 76
  2.5 21.0 %collective-permute-start = (f32[808,128]{1,0:T(8,128)S(1)}, f32[808,128]{1,0:T(8,128)S(1)}, u32[]{:S(2)}, u32[]{:S(2)}) collective-permute-start(f32[808,128]{1,0:T(8,128)S(1)} %get-tuple-element.14), channel_id=1, source_target_pairs={{0,4},{8,12},{16,20},{24,28},{32,36},{40,44},{48,52},{56,60},{64,6... | collective-permute-start | bytes 1241096 | tf_op jit(solution)/shard_map/ppermute | solution.py:563
  5.8 19.1 %collective-permute-start.1 = (f32[808,128]{1,0:T(8,128)S(1)}, f32[808,128]{1,0:T(8,128)S(1)}, u32[]{:S(2)}, u32[]{:S(2)}) collective-permute-start(f32[808,128]{1,0:T(8,128)S(1)} %get-tuple-element.15._), channel_id=1, source_target_pairs={{4,8},{12,16},{20,24},{28,32},{36,40},{44,48},{52,56},{60,64},{68,... | collective-permute-start | bytes 1241096 | tf_op jit(solution)/shard_map/ppermute | solution.py:563
  10.5 22.6 %copy-start.1 = (f32[1,2,8,16,256]{4,3,2,1,0:T(8,128)S(1)}, f32[1,2,8,16,256]{4,3,2,1,0:T(8,128)}, u32[]{:S(2)}) copy-start(f32[1,2,8,16,256]{4,3,2,1,0:T(8,128)} %refs_4_.1) | copy-start | bytes 786436
  10.5 8.8 %collective-permute-start.2 = (f32[80,128]{1,0:T(8,128)S(1)}, f32[80,128]{1,0:T(8,128)S(1)}, u32[]{:S(2)}, u32[]{:S(2)}) collective-permute-start(f32[80,128]{1,0:T(8,128)S(1)} %get-tuple-element.16), channel_id=1, source_target_pairs={{0,8},{4,12},{16,24},{20,28},{32,40},{36,44},{48,56},{52,60},{64,7... | collective-permute-start | bytes 122888 | tf_op jit(solution)/shard_map/ppermute | solution.py:563
  10.6 9.2 %collective-permute-start.3 = (f32[80,128]{1,0:T(8,128)S(1)}, f32[80,128]{1,0:T(8,128)S(1)}, u32[]{:S(2)}, u32[]{:S(2)}) collective-permute-start(f32[80,128]{1,0:T(8,128)S(1)} %get-tuple-element.17), channel_id=1, source_target_pairs={{8,16},{12,20},{24,32},{28,36},{40,48},{44,52},{56,64},{60,68},{72... | collective-permute-start | bytes 122888 | tf_op jit(solution)/shard_map/ppermute | solution.py:563
  28.3 2.2 %collective-permute-start.6 = (f32[48,256]{1,0:T(8,128)S(1)}, f32[48,256]{1,0:T(8,128)S(1)}, u32[]{:S(2)}, u32[]{:S(2)}) collective-permute-start(f32[48,256]{1,0:T(8,128)S(1)} %get-tuple-element.24.refs_0_), channel_id=1, source_target_pairs={{0,3},{1,0},{2,1},{3,2},{4,7},{5,4},{6,5},{7,6},{8,11},{9,8},{10,9... | collective-permute-start | bytes 147464 | tf_op jit(solution)/shard_map/ppermute | solution.py:610
  28.4 4.4 %collective-permute-start.5 = (f32[48,256]{1,0:T(8,128)S(1)}, f32[48,256]{1,0:T(8,128)S(1)}, u32[]{:S(2)}, u32[]{:S(2)}) collective-permute-start(f32[48,256]{1,0:T(8,128)S(1)} %get-tuple-element.24.refs_0_), channel_id=1, source_target_pairs={{0,2},{1,3},{2,0},{3,1},{4,6},{5,7},{6,4},{7,5},{8,10},{9,11},{10,... | collective-permute-start | bytes 147464 | tf_op jit(solution)/shard_map/ppermute | solution.py:610
  29.5 3.6 %collective-permute-start.4 = (f32[48,256]{1,0:T(8,128)S(1)}, f32[48,256]{1,0:T(8,128)S(1)}, u32[]{:S(2)}, u32[]{:S(2)}) collective-permute-start(f32[48,256]{1,0:T(8,128)S(1)} %get-tuple-element.24.refs_0_), channel_id=1, source_target_pairs={{0,1},{1,2},{2,3},{3,0},{4,5},{5,6},{6,7},{7,4},{8,9},{9,10},{10,1... | collective-permute-start | bytes 147464 | tf_op jit(solution)/shard_map/ppermute | solution.py:610

commit v7 on v6

--- a/solution.py
+++ b/solution.py
@@ -104,22 +104,7 @@
     return (jnp.maximum(-here, 0), 1 - here), jnp.minimum(2 - here, 3)
 
 
-def pack_kernel(counts_hbm, links_hbm, fields_hbm, near_a, near_b, counts, links, fields, sems):
-    copies = []
-
-    def fetch(source, target):
-        copies.append(pltpu.make_async_copy(source, target, sems.at[len(copies)]))
-
-    fetch(counts_hbm, counts)
-    fetch(links_hbm, links)
-    for row in range(fields.shape[2]):
-        for field in range(3):
-            fetch(fields_hbm.at[field, 0, row], fields.at[field, 0, row])
-    for copy in copies:
-        copy.start()
-    for copy in copies:
-        copy.wait()
-    position = lax.axis_index("box")
+def near_messages(counts, links, fields, position):
     here = offsets(counts, position)[1]
     held, move_up = slots(here)
     codes = jnp.zeros((8, LANES), jnp.float32)
@@ -148,22 +133,50 @@
                 )
         out[LINKS : LINKS + 8, :] = codes
 
+    return message
+
+
+def pack_kernel(counts_hbm, links_hbm, fields_hbm, near_a, counts, links, fields, sems):
+    copies = []
+
+    def fetch(source, target):
+        copies.append(pltpu.make_async_copy(source, target, sems.at[len(copies)]))
+
+    fetch(counts_hbm, counts)
+    fetch(links_hbm, links)
+    for row in range(fields.shape[2]):
+        for field in range(3):
+            fetch(fields_hbm.at[field, 0, row], fields.at[field, 0, row])
+    for copy in copies:
+        copy.start()
+    for copy in copies:
+        copy.wait()
+    position = lax.axis_index("box")
+    message = near_messages(counts, links, fields, position)
     even = position % 2 == 0
 
     @pl.when(even)
     def _():
         message(near_a, True)
-        message(near_b, False)
 
     @pl.when(jnp.logical_not(even))
     def _():
         message(near_a, False)
-        message(near_b, True)
-
-
-def pack_far_kernel(counts, fields, _, far_a, far_b):
+
+
+def pack_rest_kernel(counts, links, fields, _, near_b, far_a, far_b):
     position = lax.axis_index("box")
     move_up = slots(offsets(counts, position)[1])[1]
+    message = near_messages(counts, links, fields, position)
+    even = position % 2 == 0
+
+    @pl.when(even)
+    def _():
+        message(near_b, False)
+
+    @pl.when(jnp.logical_not(even))
+    def _():
+        message(near_b, True)
 
     def far_message(out, upper):
         row = move_up if upper else 0
@@ -515,7 +528,7 @@
         coarse[0:32, half * LANES : (half + 1) * LANES] = mean[32 * half : 32 * half + 32]
     for box in range(2):
         label = parents[0, box, 0] * 16 + parents[0, box, 1] * 8 + parents[0, box, 2]
-        coarse[32 + 8 * box : 40 + 8 * box, :] = jnp.full((8, 2 * LANES), label.astype(jnp.float32))
+        coarse[32 + 4 * box : 36 + 4 * box, :] = jnp.full((4, 2 * LANES), label.astype(jnp.float32))
 
 
 def unpack_kernel(red, black, red_left, black_left, smoothed, residual, stage):
@@ -534,12 +547,14 @@
     *got, source, out = refs
     group = lax.axis_index("grp")
     base = (group * 16).astype(jnp.float32)
+    marks = [
+        [jnp.broadcast_to(one[32 + 4 * box : 33 + 4 * box, :], (16, one.shape[1])) for box in range(2)] for one in got
+    ]
     for octant in range(16):
         kept = source[0, octant // 8, octant % 8]
-        for sender in got:
+        for sender, labels in zip(got, marks, strict=True):
             for box in range(2):
-                label = sender[32 + 8 * box : 40 + 8 * box, :]
-                mine = jnp.concatenate([label, label], axis=0) == base + float(octant)
+                mine = labels[box] == base + float(octant)
                 kept = jnp.where(mine, sender[16 * box : 16 * box + 16, :], kept)
         out[0, octant // 8, octant % 8] = kept
 
@@ -562,11 +577,11 @@
         both = [(i, i + distance) for i in ids] + [(i + distance, i) for i in ids]
         return lax.ppermute(message, "box", both)
 
-    near_a, near_b = pl.pallas_call(
+    near_a = pl.pallas_call(
         pack_kernel,
-        out_shape=(rows(NEAR_ROWS),) * 2,
+        out_shape=rows(NEAR_ROWS),
         in_specs=[HBM] * 3,
-        out_specs=(VMEM,) * 2,
+        out_specs=VMEM,
         scratch_shapes=[
             pltpu.SMEM(old_count.shape, old_count.dtype),
             pltpu.SMEM(neighbours.shape, neighbours.dtype),
@@ -577,15 +592,15 @@
         cost_estimate=cost(10**6, 2 << 20),
         name="pack",
     )(*[pltpu.with_memory_space_constraint(x, pltpu.HBM) for x in (old_count, neighbours, old_fields)])
-    far_a, far_b = pl.pallas_call(
-        pack_far_kernel,
-        out_shape=(rows(FAR_ROWS),) * 2,
-        in_specs=[SMEM, VMEM, pl.BlockSpec(memory_space=pl.ANY)],
-        out_specs=(VMEM,) * 2,
+    near_b, far_a, far_b = pl.pallas_call(
+        pack_rest_kernel,
+        out_shape=(rows(NEAR_ROWS), rows(FAR_ROWS), rows(FAR_ROWS)),
+        in_specs=[SMEM, SMEM, VMEM, pl.BlockSpec(memory_space=pl.ANY)],
+        out_specs=(VMEM,) * 3,
         compiler_params=params,
         cost_estimate=cost(10**6, 2 << 20),
-        name="pack_far",
-    )(old_count, old_fields, near_b)
+        name="pack_rest",
+    )(old_count, neighbours, old_fields, near_a)
     moved = [swap(near_a, 1, 0), swap(near_b, 1, 1), swap(far_a, 2, 0), swap(far_b, 2, 2)]
     packed = pltpu.VMEM((2, boxes, TILES, PAIRS, LANES), f32)
     column = pltpu.VMEM((boxes, TILES, PAIRS + 2 * FIRST, LANES), f32)
@@ -597,7 +612,7 @@
     half = jax.ShapeDtypeStruct((boxes, TILES, box_edge // 2, LANES), f32)
     *halves, coarse = pl.pallas_call(
         smooth_kernel,
-        out_shape=(half, half, half, half, jax.ShapeDtypeStruct((48, 2 * LANES), f32)),
+        out_shape=(half, half, half, half, jax.ShapeDtypeStruct((40, 2 * LANES), f32)),
         in_specs=[SMEM, SMEM, SMEM] + [VMEM] * 5,
         out_specs=(VMEM,) * 5,
         scratch_shapes=[raw] * 3 + [column] * 4 + [weight, packed, packed, code, sums],

time: 34.1 us -> 34.9 us (1.023)
  waiting for transfers between devices: 13.6 us -> 14.5 us
    ppermute x4, waiting for transfers between devices: 11 us -> 11.7 us  [swap(): return lax.ppermute(message, 'box', both)]
  transfers between devices with their start and end apart: 7 -> 7, of which waited for: 6 -> 5; matrix products, arithmetic and copies ran while one was open for 0% -> 0% of each run, Pallas kernels for 5% -> 5%
where the time goes in v7:
time: 34.9 us; the launch traced here: 34.7 us
  waiting for transfers between devices  14.5 us (42%)
  starting transfers between devices  11.7 us (34%)
  Pallas kernels  7.77 us (22%)
  between operations  0.73 us (2%)
    ppermute x4, waiting for transfers between devices, swap(): return lax.ppermute(message, 'box', both)  11.7 us
    ppermute x4, starting transfers between devices, swap(): return lax.ppermute(message, 'box', both)  10.7 us
    pallas_call x1, Pallas kernels, per_device(): pl.pallas_call(smooth_kernel, out_shape=(half, half, half, half, jax.Shap...  3.44 us
    ppermute x3, waiting for transfers between devices, per_device(): lax.ppermute(coarse, 'grp', [(i, (i + k) % groups) for i in range(groups)])  2.77 us
    pallas_call x1, Pallas kernels, per_device(): pl.pallas_call(pack_kernel, out_shape=rows(NEAR_ROWS), in_specs=[HBM] * 3...  1.8 us
    ppermute x3, starting transfers between devices, per_device(): lax.ppermute(coarse, 'grp', [(i, (i + k) % groups) for i in range(groups)])  1 us
    pallas_call x1, Pallas kernels, per_device(): pl.pallas_call(pack_rest_kernel, out_shape=(rows(NEAR_ROWS), rows(FAR_ROW...  0.86 us
    pallas_call x1, Pallas kernels, per_device(): pl.pallas_call(unpack_kernel, out_shape=(fine, fine), in_specs=[VMEM] * 4...  0.84 us
  transfers between devices with their start and end apart: 7, of which 5 were waited for; matrix products, arithmetic and copies ran while one was open for 0% of the time, Pallas kernels for 5%

profile of v7, /device:TPU:128, one launch (start us, length us, event | category | flops | bytes accessed | tf_op | source)
XLA Modules:
  0.0 34.7 jit_solution(1604445060733824218)
XLA Ops:
  0.6 0.0 copy-start.2
  0.6 0.0 copy-start.3
  0.7 0.0 copy-start
  0.7 0.0 copy-start.4
  0.7 1.8 %pack.1._ = f32[808,128]{1,0:T(8,128)S(1)} custom-call(s32[1,64]{1,0:T(1,128)} %counts.3, s32[1,2,6]{2,1,0:T(2,128)} %links.3, f32[3,1,4,32,1024]{4,3,2,1,0:T(8,128)} %fields.3), custom_call_target="tpu_custom_call" | custom-call | flops 1000000 | bytes 2097152 | tf_op jit(solution)/shard_map/pack/pallas_call | solution.py:580
  2.5 3.3 %collective-permute-start = (f32[808,128]{1,0:T(8,128)S(1)}, f32[808,128]{1,0:T(8,128)S(1)}, u32[]{:S(2)}, u32[]{:S(2)}) collective-permute-start(f32[808,128]{1,0:T(8,128)S(1)} %pack.1._), channel_id=1, source_target_pairs={{0,4},{8,12},{16,20},{24,28},{32,36},{40,44},{48,52},{56,60},{64,6... | collective-permute-start | bytes 1241096 | tf_op jit(solution)/shard_map/ppermute | solution.py:578
  5.8 0.0 copy-done.2
  5.8 0.0 copy-done.3
  5.8 0.0 copy-done
  5.8 0.9 %pack_rest.1 = (f32[808,128]{1,0:T(8,128)S(1)}, f32[80,128]{1,0:T(8,128)S(1)}, f32[80,128]{1,0:T(8,128)S(1)}) custom-call(s32[1,64]{1,0:T(1,128)S(1)} %copy-done.3, s32[1,2,6]{2,1,0:T(2,128)S(1)} %copy-done.2, f32[3,1,4,32,1024]{4,3,2,1,0:T(8,128)S(1)} %copy-done, f32[808,128]{1,0:T(8,128)S(1)} %pack.1._), custom_call_target="tpu_custom_call" | custom-call | flops 1000000 | bytes 2097152 | tf_op jit(solution)/shard_map/pack_rest/pallas_call | solution.py:595
  6.6 0.0 copy-start.1
  6.6 4.1 %collective-permute-start.1 = (f32[808,128]{1,0:T(8,128)S(1)}, f32[808,128]{1,0:T(8,128)S(1)}, u32[]{:S(2)}, u32[]{:S(2)}) collective-permute-start(f32[808,128]{1,0:T(8,128)S(1)} %get-tuple-element.13), channel_id=1, source_target_pairs={{4,8},{12,16},{20,24},{28,32},{36,40},{44,48},{52,56},{60,64},{68,... | collective-permute-start | bytes 1241096 | tf_op jit(solution)/shard_map/ppermute | solution.py:578
  10.8 0.1 collective-permute-start.2
  10.9 3.2 %collective-permute-start.3 = (f32[80,128]{1,0:T(8,128)S(1)}, f32[80,128]{1,0:T(8,128)S(1)}, u32[]{:S(2)}, u32[]{:S(2)}) collective-permute-start(f32[80,128]{1,0:T(8,128)S(1)} %get-tuple-element.15), channel_id=1, source_target_pairs={{8,16},{12,20},{24,32},{28,36},{40,48},{44,52},{56,64},{60,68},{72... | collective-permute-start | bytes 122888 | tf_op jit(solution)/shard_map/ppermute | solution.py:578
  14.1 6.3 %collective-permute-done.2.far_a = f32[80,128]{1,0:T(8,128)S(1)} collective-permute-done((f32[80,128]{1,0:T(8,128)S(1)}, f32[80,128]{1,0:T(8,128)S(1)}, u32[]{:S(2)}, u32[]{:S(2)}) %collective-permute-start.2) | collective-permute-done | bytes 40992 | tf_op jit(solution)/shard_map/ppermute | solution.py:578
  20.4 0.0 collective-permute-done.3.far_b
  20.4 3.0 %collective-permute-done.near_a = f32[808,128]{1,0:T(8,128)S(1)} collective-permute-done((f32[808,128]{1,0:T(8,128)S(1)}, f32[808,128]{1,0:T(8,128)S(1)}, u32[]{:S(2)}, u32[]{:S(2)}) %collective-permute-start) | collective-permute-done | bytes 413728 | tf_op jit(solution)/shard_map/ppermute | solution.py:578
  23.4 2.4 %collective-permute-done.1.near_b = f32[808,128]{1,0:T(8,128)S(1)} collective-permute-done((f32[808,128]{1,0:T(8,128)S(1)}, f32[808,128]{1,0:T(8,128)S(1)}, u32[]{:S(2)}, u32[]{:S(2)}) %collective-permute-start.1) | collective-permute-done | bytes 413728 | tf_op jit(solution)/shard_map/ppermute | solution.py:578
  25.9 0.0 copy-done.4
  25.9 3.4 %smooth.1 = (f32[2,8,16,128]{3,2,1,0:T(8,128)S(1)}, f32[2,8,16,128]{3,2,1,0:T(8,128)S(1)}, f32[2,8,16,128]{3,2,1,0:T(8,128)S(1)}, f32[2,8,16,128]{3,2,1,0:T(8,128)S(1)}, f32[40,256]{1,0:T(8,128)S(1)}) custom-call(s32[1,64]{1,0:T(1,128)S(1)} %copy-done.3, s32[1,2,6]{2,1,0:T(2,128)S(1)} %copy-done.2, s32[1,2,3]{2,1,0:T(2,128)S(1)} %copy-done.4, ...), custom_call_target="tpu_custom_call" | custom-call | flops 10000000 | bytes 6291456 | tf_op jit(solution)/shard_map/smooth/pallas_call | solution.py:613
  29.3 0.1 collective-permute-start.6
  29.4 0.8 %collective-permute-start.5 = (f32[40,256]{1,0:T(8,128)S(1)}, f32[40,256]{1,0:T(8,128)S(1)}, u32[]{:S(2)}, u32[]{:S(2)}) collective-permute-start(f32[40,256]{1,0:T(8,128)S(1)} %get-tuple-element.22.refs_0_), channel_id=1, source_target_pairs={{0,2},{1,3},{2,0},{3,1},{4,6},{5,7},{6,4},{7,5},{8,10},{9,11},{10,... | collective-permute-start | bytes 122888 | tf_op jit(solution)/shard_map/ppermute | solution.py:625
  30.2 0.1 collective-permute-start.4
  30.3 0.8 %unpack.1 = (f32[1,2,32,1024]{3,2,1,0:T(8,128)}, f32[1,2,32,1024]{3,2,1,0:T(8,128)}) custom-call(f32[2,8,16,128]{3,2,1,0:T(8,128)S(1)} %get-tuple-element.16.red, f32[2,8,16,128]{3,2,1,0:T(8,128)S(1)} %get-tuple-element.17.black, f32[2,8,16,128]{3,2,1,0:T(8,128)S(1)} %get-tuple-element.18.red_left, f32[2,8,16,128]{3,2,1,0:T(8,128)S(1)} %get-tuple-element.19.black_left), custom_call_target="tpu_custom_call" | custom-call | flops 1000000 | bytes 3145728 | tf_op jit(solution)/shard_map/unpack/pallas_call | solution.py:628
  31.1 0.0 collective-permute-done.6.refs_3_
  31.2 2.7 %collective-permute-done.5.refs_2_ = f32[40,256]{1,0:T(8,128)S(1)} collective-permute-done((f32[40,256]{1,0:T(8,128)S(1)}, f32[40,256]{1,0:T(8,128)S(1)}, u32[]{:S(2)}, u32[]{:S(2)}) %collective-permute-start.5) | collective-permute-done | bytes 40992 | tf_op jit(solution)/shard_map/ppermute | solution.py:625
  33.8 0.1 collective-permute-done.4.refs_1_
  33.9 0.0 copy-done.1
  33.9 0.8 %place.1 = f32[1,2,8,16,256]{4,3,2,1,0:T(8,128)} custom-call(f32[40,256]{1,0:T(8,128)S(1)} %get-tuple-element.22.refs_0_, f32[40,256]{1,0:T(8,128)S(1)} %collective-permute-done.4.refs_1_, f32[40,256]{1,0:T(8,128)S(1)} %collective-permute-done.5.refs_2_, f32[40,256]{1,0:T(8,128)S(1)} %collective-permute-done.6.refs_3_, f32[1,2,8,16,256]{4,3,2,1,0:T(8,128)S(1)} %copy-done.1), custom_call_target="tpu_custom_call" | custom-call | flops 1000000 | bytes 1048576 | tf_op jit(solution)/shard_map/place/pallas_call | solution.py:638
Async XLA Ops:
  0.6 5.1 %copy-start.2 = (s32[1,2,6]{2,1,0:T(2,128)S(1)}, s32[1,2,6]{2,1,0:T(2,128)}, u32[]{:S(2)}) copy-start(s32[1,2,6]{2,1,0:T(2,128)} %links.3) | copy-start | bytes 148
  0.6 5.1 %copy-start.3 = (s32[1,64]{1,0:T(1,128)S(1)}, s32[1,64]{1,0:T(1,128)}, u32[]{:S(2)}) copy-start(s32[1,64]{1,0:T(1,128)} %counts.3) | copy-start | bytes 772
  0.7 5.1 %copy-start = (f32[3,1,4,32,1024]{4,3,2,1,0:T(8,128)S(1)}, f32[3,1,4,32,1024]{4,3,2,1,0:T(8,128)}, u32[]{:S(2)}) copy-start(f32[3,1,4,32,1024]{4,3,2,1,0:T(8,128)} %fields.3) | copy-start | bytes 4718596
  0.7 25.2 %copy-start.4 = (s32[1,2,3]{2,1,0:T(2,128)S(1)}, s32[1,2,3]{2,1,0:T(2,128)}, u32[]{:S(2)}) copy-start(s32[1,2,3]{2,1,0:T(2,128)} %parents.1) | copy-start | bytes 76
  2.5 21.0 %collective-permute-start = (f32[808,128]{1,0:T(8,128)S(1)}, f32[808,128]{1,0:T(8,128)S(1)}, u32[]{:S(2)}, u32[]{:S(2)}) collective-permute-start(f32[808,128]{1,0:T(8,128)S(1)} %pack.1._), channel_id=1, source_target_pairs={{0,4},{8,12},{16,20},{24,28},{32,36},{40,44},{48,52},{56,60},{64,6... | collective-permute-start | bytes 1241096 | tf_op jit(solution)/shard_map/ppermute | solution.py:578
  6.6 27.3 %copy-start.1 = (f32[1,2,8,16,256]{4,3,2,1,0:T(8,128)S(1)}, f32[1,2,8,16,256]{4,3,2,1,0:T(8,128)}, u32[]{:S(2)}) copy-start(f32[1,2,8,16,256]{4,3,2,1,0:T(8,128)} %refs_4_.1) | copy-start | bytes 786436
  6.6 19.2 %collective-permute-start.1 = (f32[808,128]{1,0:T(8,128)S(1)}, f32[808,128]{1,0:T(8,128)S(1)}, u32[]{:S(2)}, u32[]{:S(2)}) collective-permute-start(f32[808,128]{1,0:T(8,128)S(1)} %get-tuple-element.13), channel_id=1, source_target_pairs={{4,8},{12,16},{20,24},{28,32},{36,40},{44,48},{52,56},{60,64},{68,... | collective-permute-start | bytes 1241096 | tf_op jit(solution)/shard_map/ppermute | solution.py:578
  10.8 9.6 %collective-permute-start.2 = (f32[80,128]{1,0:T(8,128)S(1)}, f32[80,128]{1,0:T(8,128)S(1)}, u32[]{:S(2)}, u32[]{:S(2)}) collective-permute-start(f32[80,128]{1,0:T(8,128)S(1)} %get-tuple-element.14), channel_id=1, source_target_pairs={{0,8},{4,12},{16,24},{20,28},{32,40},{36,44},{48,56},{52,60},{64,7... | collective-permute-start | bytes 122888 | tf_op jit(solution)/shard_map/ppermute | solution.py:578
  10.9 9.5 %collective-permute-start.3 = (f32[80,128]{1,0:T(8,128)S(1)}, f32[80,128]{1,0:T(8,128)S(1)}, u32[]{:S(2)}, u32[]{:S(2)}) collective-permute-start(f32[80,128]{1,0:T(8,128)S(1)} %get-tuple-element.15), channel_id=1, source_target_pairs={{8,16},{12,20},{24,32},{28,36},{40,48},{44,52},{56,64},{60,68},{72... | collective-permute-start | bytes 122888 | tf_op jit(solution)/shard_map/ppermute | solution.py:578
  29.3 1.9 %collective-permute-start.6 = (f32[40,256]{1,0:T(8,128)S(1)}, f32[40,256]{1,0:T(8,128)S(1)}, u32[]{:S(2)}, u32[]{:S(2)}) collective-permute-start(f32[40,256]{1,0:T(8,128)S(1)} %get-tuple-element.22.refs_0_), channel_id=1, source_target_pairs={{0,3},{1,0},{2,1},{3,2},{4,7},{5,4},{6,5},{7,6},{8,11},{9,8},{10,9... | collective-permute-start | bytes 122888 | tf_op jit(solution)/shard_map/ppermute | solution.py:625
  29.4 4.4 %collective-permute-start.5 = (f32[40,256]{1,0:T(8,128)S(1)}, f32[40,256]{1,0:T(8,128)S(1)}, u32[]{:S(2)}, u32[]{:S(2)}) collective-permute-start(f32[40,256]{1,0:T(8,128)S(1)} %get-tuple-element.22.refs_0_), channel_id=1, source_target_pairs={{0,2},{1,3},{2,0},{3,1},{4,6},{5,7},{6,4},{7,5},{8,10},{9,11},{10,... | collective-permute-start | bytes 122888 | tf_op jit(solution)/shard_map/ppermute | solution.py:625
  30.2 3.8 %collective-permute-start.4 = (f32[40,256]{1,0:T(8,128)S(1)}, f32[40,256]{1,0:T(8,128)S(1)}, u32[]{:S(2)}, u32[]{:S(2)}) collective-permute-start(f32[40,256]{1,0:T(8,128)S(1)} %get-tuple-element.22.refs_0_), channel_id=1, source_target_pairs={{0,1},{1,2},{2,3},{3,0},{4,5},{5,6},{6,7},{7,4},{8,9},{9,10},{10,1... | collective-permute-start | bytes 122888 | tf_op jit(solution)/shard_map/ppermute | solution.py:625

commit v8 on v6

--- a/solution.py
+++ b/solution.py
@@ -515,7 +515,7 @@
         coarse[0:32, half * LANES : (half + 1) * LANES] = mean[32 * half : 32 * half + 32]
     for box in range(2):
         label = parents[0, box, 0] * 16 + parents[0, box, 1] * 8 + parents[0, box, 2]
-        coarse[32 + 8 * box : 40 + 8 * box, :] = jnp.full((8, 2 * LANES), label.astype(jnp.float32))
+        coarse[32 + 4 * box : 36 + 4 * box, :] = jnp.full((4, 2 * LANES), label.astype(jnp.float32))
 
 
 def unpack_kernel(red, black, red_left, black_left, smoothed, residual, stage):
@@ -534,12 +534,14 @@
     *got, source, out = refs
     group = lax.axis_index("grp")
     base = (group * 16).astype(jnp.float32)
+    marks = [
+        [jnp.broadcast_to(one[32 + 4 * box : 33 + 4 * box, :], (16, one.shape[1])) for box in range(2)] for one in got
+    ]
     for octant in range(16):
         kept = source[0, octant // 8, octant % 8]
-        for sender in got:
+        for sender, labels in zip(got, marks, strict=True):
             for box in range(2):
-                label = sender[32 + 8 * box : 40 + 8 * box, :]
-                mine = jnp.concatenate([label, label], axis=0) == base + float(octant)
+                mine = labels[box] == base + float(octant)
                 kept = jnp.where(mine, sender[16 * box : 16 * box + 16, :], kept)
         out[0, octant // 8, octant % 8] = kept
 
@@ -597,7 +599,7 @@
     half = jax.ShapeDtypeStruct((boxes, TILES, box_edge // 2, LANES), f32)
     *halves, coarse = pl.pallas_call(
         smooth_kernel,
-        out_shape=(half, half, half, half, jax.ShapeDtypeStruct((48, 2 * LANES), f32)),
+        out_shape=(half, half, half, half, jax.ShapeDtypeStruct((40, 2 * LANES), f32)),
         in_specs=[SMEM, SMEM, SMEM] + [VMEM] * 5,
         out_specs=(VMEM,) * 5,
         scratch_shapes=[raw] * 3 + [column] * 4 + [weight, packed, packed, code, sums],

time: 34.1 us -> 33.9 us (level)
  no operation moved by 1% of the time
where the time goes in v8:
time: 33.9 us; the launch traced here: 33.8 us
  waiting for transfers between devices  13.4 us (40%)
  starting transfers between devices  11.9 us (35%)
  Pallas kernels  7.66 us (23%)
  between operations  0.75 us (2%)
    ppermute x4, waiting for transfers between devices, swap(): return lax.ppermute(message, 'box', both)  11 us
    ppermute x4, starting transfers between devices, swap(): return lax.ppermute(message, 'box', both)  10.6 us
    pallas_call x1, Pallas kernels, per_device(): pl.pallas_call(smooth_kernel, out_shape=(half, half, half, half, jax.Shap...  3.44 us
    ppermute x3, waiting for transfers between devices, per_device(): lax.ppermute(coarse, 'grp', [(i, (i + k) % groups) for i in range(groups)])  2.45 us
    pallas_call x1, Pallas kernels, per_device(): pl.pallas_call(pack_kernel, out_shape=(rows(NEAR_ROWS),) * 2, in_specs=[H...  1.83 us
    ppermute x3, starting transfers between devices, per_device(): lax.ppermute(coarse, 'grp', [(i, (i + k) % groups) for i in range(groups)])  1.31 us
    pallas_call x1, Pallas kernels, per_device(): pl.pallas_call(unpack_kernel, out_shape=(fine, fine), in_specs=[VMEM] * 4...  0.84 us
    pallas_call x1, Pallas kernels, per_device(): pl.pallas_call(place_kernel, out_shape=jax.ShapeDtypeStruct(coarse_source...  0.82 us
  transfers between devices with their start and end apart: 7, of which 6 were waited for; matrix products, arithmetic and copies ran while one was open for 0% of the time, Pallas kernels for 5%

profile of v8, /device:TPU:128, one launch (start us, length us, event | category | flops | bytes accessed | tf_op | source)
XLA Modules:
  0.0 33.8 jit_solution(9564247721464819002)
XLA Ops:
  0.6 0.0 copy-start.2
  0.6 0.0 copy-start
  0.7 0.0 copy-start.3
  0.7 0.0 copy-start.4
  0.7 1.8 %pack.1 = (f32[808,128]{1,0:T(8,128)S(1)}, f32[808,128]{1,0:T(8,128)S(1)}) custom-call(s32[1,64]{1,0:T(1,128)} %counts.3, s32[1,2,6]{2,1,0:T(2,128)} %links.1, f32[3,1,4,32,1024]{4,3,2,1,0:T(8,128)} %fields.3), custom_call_target="tpu_custom_call" | custom-call | flops 1000000 | bytes 2097152 | tf_op jit(solution)/shard_map/pack/pallas_call | solution.py:567
  2.5 3.3 %collective-permute-start = (f32[808,128]{1,0:T(8,128)S(1)}, f32[808,128]{1,0:T(8,128)S(1)}, u32[]{:S(2)}, u32[]{:S(2)}) collective-permute-start(f32[808,128]{1,0:T(8,128)S(1)} %get-tuple-element.14), channel_id=1, source_target_pairs={{0,4},{8,12},{16,20},{24,28},{32,36},{40,44},{48,52},{56,60},{64,6... | collective-permute-start | bytes 1241096 | tf_op jit(solution)/shard_map/ppermute | solution.py:565
  5.8 4.0 %collective-permute-start.1 = (f32[808,128]{1,0:T(8,128)S(1)}, f32[808,128]{1,0:T(8,128)S(1)}, u32[]{:S(2)}, u32[]{:S(2)}) collective-permute-start(f32[808,128]{1,0:T(8,128)S(1)} %get-tuple-element.15._), channel_id=1, source_target_pairs={{4,8},{12,16},{20,24},{28,32},{36,40},{44,48},{52,56},{60,64},{68,... | collective-permute-start | bytes 1241096 | tf_op jit(solution)/shard_map/ppermute | solution.py:565
  9.8 0.0 copy-done.2
  9.8 0.0 copy-done
  9.8 0.7 %pack_far.1 = (f32[80,128]{1,0:T(8,128)S(1)}, f32[80,128]{1,0:T(8,128)S(1)}) custom-call(s32[1,64]{1,0:T(1,128)S(1)} %copy-done.2, f32[3,1,4,32,1024]{4,3,2,1,0:T(8,128)S(1)} %copy-done, f32[808,128]{1,0:T(8,128)S(1)} %get-tuple-element.15._), custom_call_target="tpu_custom_call" | custom-call | flops 1000000 | bytes 2097152 | tf_op jit(solution)/shard_map/pack_far/pallas_call | solution.py:582
  10.5 0.0 copy-start.1
  10.5 0.1 collective-permute-start.2
  10.6 3.2 %collective-permute-start.3 = (f32[80,128]{1,0:T(8,128)S(1)}, f32[80,128]{1,0:T(8,128)S(1)}, u32[]{:S(2)}, u32[]{:S(2)}) collective-permute-start(f32[80,128]{1,0:T(8,128)S(1)} %get-tuple-element.17), channel_id=1, source_target_pairs={{8,16},{12,20},{24,32},{28,36},{40,48},{44,52},{56,64},{60,68},{72... | collective-permute-start | bytes 122888 | tf_op jit(solution)/shard_map/ppermute | solution.py:565
  13.9 5.5 %collective-permute-done.2.far_a = f32[80,128]{1,0:T(8,128)S(1)} collective-permute-done((f32[80,128]{1,0:T(8,128)S(1)}, f32[80,128]{1,0:T(8,128)S(1)}, u32[]{:S(2)}, u32[]{:S(2)}) %collective-permute-start.2) | collective-permute-done | bytes 40992 | tf_op jit(solution)/shard_map/ppermute | solution.py:565
  19.4 0.5 %collective-permute-done.3.far_b = f32[80,128]{1,0:T(8,128)S(1)} collective-permute-done((f32[80,128]{1,0:T(8,128)S(1)}, f32[80,128]{1,0:T(8,128)S(1)}, u32[]{:S(2)}, u32[]{:S(2)}) %collective-permute-start.3) | collective-permute-done | bytes 40992 | tf_op jit(solution)/shard_map/ppermute | solution.py:565
  19.9 3.6 %collective-permute-done.near_a = f32[808,128]{1,0:T(8,128)S(1)} collective-permute-done((f32[808,128]{1,0:T(8,128)S(1)}, f32[808,128]{1,0:T(8,128)S(1)}, u32[]{:S(2)}, u32[]{:S(2)}) %collective-permute-start) | collective-permute-done | bytes 413728 | tf_op jit(solution)/shard_map/ppermute | solution.py:565
  23.5 1.4 %collective-permute-done.1.near_b = f32[808,128]{1,0:T(8,128)S(1)} collective-permute-done((f32[808,128]{1,0:T(8,128)S(1)}, f32[808,128]{1,0:T(8,128)S(1)}, u32[]{:S(2)}, u32[]{:S(2)}) %collective-permute-start.1) | collective-permute-done | bytes 413728 | tf_op jit(solution)/shard_map/ppermute | solution.py:565
  24.9 0.0 copy-done.3
  24.9 0.0 copy-done.4
  24.9 3.4 %smooth.1 = (f32[2,8,16,128]{3,2,1,0:T(8,128)S(1)}, f32[2,8,16,128]{3,2,1,0:T(8,128)S(1)}, f32[2,8,16,128]{3,2,1,0:T(8,128)S(1)}, f32[2,8,16,128]{3,2,1,0:T(8,128)S(1)}, f32[40,256]{1,0:T(8,128)S(1)}) custom-call(s32[1,64]{1,0:T(1,128)S(1)} %copy-done.2, s32[1,2,6]{2,1,0:T(2,128)S(1)} %copy-done.3, s32[1,2,3]{2,1,0:T(2,128)S(1)} %copy-done.4, ...), custom_call_target="tpu_custom_call" | custom-call | flops 10000000 | bytes 6291456 | tf_op jit(solution)/shard_map/smooth/pallas_call | solution.py:600
  28.3 0.1 collective-permute-start.6
  28.4 1.1 %collective-permute-start.5 = (f32[40,256]{1,0:T(8,128)S(1)}, f32[40,256]{1,0:T(8,128)S(1)}, u32[]{:S(2)}, u32[]{:S(2)}) collective-permute-start(f32[40,256]{1,0:T(8,128)S(1)} %get-tuple-element.24.refs_0_), channel_id=1, source_target_pairs={{0,2},{1,3},{2,0},{3,1},{4,6},{5,7},{6,4},{7,5},{8,10},{9,11},{10,... | collective-permute-start | bytes 122888 | tf_op jit(solution)/shard_map/ppermute | solution.py:612
  29.5 0.1 collective-permute-start.4
  29.6 0.8 %unpack.1 = (f32[1,2,32,1024]{3,2,1,0:T(8,128)}, f32[1,2,32,1024]{3,2,1,0:T(8,128)}) custom-call(f32[2,8,16,128]{3,2,1,0:T(8,128)S(1)} %get-tuple-element.18.red, f32[2,8,16,128]{3,2,1,0:T(8,128)S(1)} %get-tuple-element.19.black, f32[2,8,16,128]{3,2,1,0:T(8,128)S(1)} %get-tuple-element.20.red_left, f32[2,8,16,128]{3,2,1,0:T(8,128)S(1)} %get-tuple-element.21.black_left), custom_call_target="tpu_custom_call" | custom-call | flops 1000000 | bytes 3145728 | tf_op jit(solution)/shard_map/unpack/pallas_call | solution.py:615
  30.5 0.0 collective-permute-done.6.refs_3_
  30.5 2.1 %collective-permute-done.5.refs_2_ = f32[40,256]{1,0:T(8,128)S(1)} collective-permute-done((f32[40,256]{1,0:T(8,128)S(1)}, f32[40,256]{1,0:T(8,128)S(1)}, u32[]{:S(2)}, u32[]{:S(2)}) %collective-permute-start.5) | collective-permute-done | bytes 40992 | tf_op jit(solution)/shard_map/ppermute | solution.py:612
  32.6 0.3 %collective-permute-done.4.refs_1_ = f32[40,256]{1,0:T(8,128)S(1)} collective-permute-done((f32[40,256]{1,0:T(8,128)S(1)}, f32[40,256]{1,0:T(8,128)S(1)}, u32[]{:S(2)}, u32[]{:S(2)}) %collective-permute-start.4) | collective-permute-done | bytes 40992 | tf_op jit(solution)/shard_map/ppermute | solution.py:612
  32.9 0.0 copy-done.1
  32.9 0.8 %place.1 = f32[1,2,8,16,256]{4,3,2,1,0:T(8,128)} custom-call(f32[40,256]{1,0:T(8,128)S(1)} %get-tuple-element.24.refs_0_, f32[40,256]{1,0:T(8,128)S(1)} %collective-permute-done.4.refs_1_, f32[40,256]{1,0:T(8,128)S(1)} %collective-permute-done.5.refs_2_, f32[40,256]{1,0:T(8,128)S(1)} %collective-permute-done.6.refs_3_, f32[1,2,8,16,256]{4,3,2,1,0:T(8,128)S(1)} %copy-done.1), custom_call_target="tpu_custom_call" | custom-call | flops 1000000 | bytes 1048576 | tf_op jit(solution)/shard_map/place/pallas_call | solution.py:625
Async XLA Ops:
  0.6 9.1 %copy-start.2 = (s32[1,64]{1,0:T(1,128)S(1)}, s32[1,64]{1,0:T(1,128)}, u32[]{:S(2)}) copy-start(s32[1,64]{1,0:T(1,128)} %counts.3) | copy-start | bytes 772
  0.6 9.1 %copy-start = (f32[3,1,4,32,1024]{4,3,2,1,0:T(8,128)S(1)}, f32[3,1,4,32,1024]{4,3,2,1,0:T(8,128)}, u32[]{:S(2)}) copy-start(f32[3,1,4,32,1024]{4,3,2,1,0:T(8,128)} %fields.3) | copy-start | bytes 4718596
  0.7 24.2 %copy-start.3 = (s32[1,2,6]{2,1,0:T(2,128)S(1)}, s32[1,2,6]{2,1,0:T(2,128)}, u32[]{:S(2)}) copy-start(s32[1,2,6]{2,1,0:T(2,128)} %links.1) | copy-start | bytes 148
  0.7 24.2 %copy-start.4 = (s32[1,2,3]{2,1,0:T(2,128)S(1)}, s32[1,2,3]{2,1,0:T(2,128)}, u32[]{:S(2)}) copy-start(s32[1,2,3]{2,1,0:T(2,128)} %parents.1) | copy-start | bytes 76
  2.5 21.0 %collective-permute-start = (f32[808,128]{1,0:T(8,128)S(1)}, f32[808,128]{1,0:T(8,128)S(1)}, u32[]{:S(2)}, u32[]{:S(2)}) collective-permute-start(f32[808,128]{1,0:T(8,128)S(1)} %get-tuple-element.14), channel_id=1, source_target_pairs={{0,4},{8,12},{16,20},{24,28},{32,36},{40,44},{48,52},{56,60},{64,6... | collective-permute-start | bytes 1241096 | tf_op jit(solution)/shard_map/ppermute | solution.py:565
  5.8 19.1 %collective-permute-start.1 = (f32[808,128]{1,0:T(8,128)S(1)}, f32[808,128]{1,0:T(8,128)S(1)}, u32[]{:S(2)}, u32[]{:S(2)}) collective-permute-start(f32[808,128]{1,0:T(8,128)S(1)} %get-tuple-element.15._), channel_id=1, source_target_pairs={{4,8},{12,16},{20,24},{28,32},{36,40},{44,48},{52,56},{60,64},{68,... | collective-permute-start | bytes 1241096 | tf_op jit(solution)/shard_map/ppermute | solution.py:565
  10.5 22.4 %copy-start.1 = (f32[1,2,8,16,256]{4,3,2,1,0:T(8,128)S(1)}, f32[1,2,8,16,256]{4,3,2,1,0:T(8,128)}, u32[]{:S(2)}) copy-start(f32[1,2,8,16,256]{4,3,2,1,0:T(8,128)} %refs_4_.1) | copy-start | bytes 786436
  10.5 8.8 %collective-permute-start.2 = (f32[80,128]{1,0:T(8,128)S(1)}, f32[80,128]{1,0:T(8,128)S(1)}, u32[]{:S(2)}, u32[]{:S(2)}) collective-permute-start(f32[80,128]{1,0:T(8,128)S(1)} %get-tuple-element.16), channel_id=1, source_target_pairs={{0,8},{4,12},{16,24},{20,28},{32,40},{36,44},{48,56},{52,60},{64,7... | collective-permute-start | bytes 122888 | tf_op jit(solution)/shard_map/ppermute | solution.py:565
  10.6 9.2 %collective-permute-start.3 = (f32[80,128]{1,0:T(8,128)S(1)}, f32[80,128]{1,0:T(8,128)S(1)}, u32[]{:S(2)}, u32[]{:S(2)}) collective-permute-start(f32[80,128]{1,0:T(8,128)S(1)} %get-tuple-element.17), channel_id=1, source_target_pairs={{8,16},{12,20},{24,32},{28,36},{40,48},{44,52},{56,64},{60,68},{72... | collective-permute-start | bytes 122888 | tf_op jit(solution)/shard_map/ppermute | solution.py:565
  28.3 2.2 %collective-permute-start.6 = (f32[40,256]{1,0:T(8,128)S(1)}, f32[40,256]{1,0:T(8,128)S(1)}, u32[]{:S(2)}, u32[]{:S(2)}) collective-permute-start(f32[40,256]{1,0:T(8,128)S(1)} %get-tuple-element.24.refs_0_), channel_id=1, source_target_pairs={{0,3},{1,0},{2,1},{3,2},{4,7},{5,4},{6,5},{7,6},{8,11},{9,8},{10,9... | collective-permute-start | bytes 122888 | tf_op jit(solution)/shard_map/ppermute | solution.py:612
  28.4 4.2 %collective-permute-start.5 = (f32[40,256]{1,0:T(8,128)S(1)}, f32[40,256]{1,0:T(8,128)S(1)}, u32[]{:S(2)}, u32[]{:S(2)}) collective-permute-start(f32[40,256]{1,0:T(8,128)S(1)} %get-tuple-element.24.refs_0_), channel_id=1, source_target_pairs={{0,2},{1,3},{2,0},{3,1},{4,6},{5,7},{6,4},{7,5},{8,10},{9,11},{10,... | collective-permute-start | bytes 122888 | tf_op jit(solution)/shard_map/ppermute | solution.py:612
  29.5 3.4 %collective-permute-start.4 = (f32[40,256]{1,0:T(8,128)S(1)}, f32[40,256]{1,0:T(8,128)S(1)}, u32[]{:S(2)}, u32[]{:S(2)}) collective-permute-start(f32[40,256]{1,0:T(8,128)S(1)} %get-tuple-element.24.refs_0_), channel_id=1, source_target_pairs={{0,1},{1,2},{2,3},{3,0},{4,5},{5,6},{6,7},{7,4},{8,9},{9,10},{10,1... | collective-permute-start | bytes 122888 | tf_op jit(solution)/shard_map/ppermute | solution.py:612

commit v9 on v8

--- a/solution.py
+++ b/solution.py
@@ -117,7 +117,7 @@
             fetch(fields_hbm.at[field, 0, row], fields.at[field, 0, row])
     for copy in copies:
         copy.start()
-    for copy in copies:
+    for copy in copies[:2]:
         copy.wait()
     position = lax.axis_index("box")
     here = offsets(counts, position)[1]
@@ -129,6 +129,9 @@
             codes = jnp.where(mine, link_code(links, box, face, 2 * position).astype(jnp.float32), codes)
 
     mixed = (row_ids(16) + odd_lanes(16)) & 1
+
+    for copy in copies[2:]:
+        copy.wait()
 
     def message(out, upper):
         row = move_up if upper else 0

time: 33.9 us -> 33.9 us (level)
  no operation moved by 1% of the time
where the time goes in v9:
time: 33.9 us; the launch traced here: 33.7 us
  waiting for transfers between devices  13.4 us (40%)
  starting transfers between devices  11.9 us (35%)
  Pallas kernels  7.64 us (23%)
  between operations  0.75 us (2%)
    ppermute x4, waiting for transfers between devices, swap(): return lax.ppermute(message, 'box', both)  11 us
    ppermute x4, starting transfers between devices, swap(): return lax.ppermute(message, 'box', both)  10.6 us
    pallas_call x1, Pallas kernels, per_device(): pl.pallas_call(smooth_kernel, out_shape=(half, half, half, half, jax.Shap...  3.44 us
    ppermute x3, waiting for transfers between devices, per_device(): lax.ppermute(coarse, 'grp', [(i, (i + k) % groups) for i in range(groups)])  2.45 us
    pallas_call x1, Pallas kernels, per_device(): pl.pallas_call(pack_kernel, out_shape=(rows(NEAR_ROWS),) * 2, in_specs=[H...  1.81 us
    ppermute x3, starting transfers between devices, per_device(): lax.ppermute(coarse, 'grp', [(i, (i + k) % groups) for i in range(groups)])  1.32 us
    pallas_call x1, Pallas kernels, per_device(): pl.pallas_call(unpack_kernel, out_shape=(fine, fine), in_specs=[VMEM] * 4...  0.84 us
    pallas_call x1, Pallas kernels, per_device(): pl.pallas_call(place_kernel, out_shape=jax.ShapeDtypeStruct(coarse_source...  0.82 us
  transfers between devices with their start and end apart: 7, of which 6 were waited for; matrix products, arithmetic and copies ran while one was open for 0% of the time, Pallas kernels for 5%

profile of v9, /device:TPU:128, one launch (start us, length us, event | category | flops | bytes accessed | tf_op | source)
XLA Modules:
  0.0 33.7 jit_solution(5981135815645507216)
XLA Ops:
  0.6 0.0 copy-start.2
  0.6 0.0 copy-start
  0.7 0.0 copy-start.3
  0.7 0.0 copy-start.4
  0.7 1.8 %pack.1 = (f32[808,128]{1,0:T(8,128)S(1)}, f32[808,128]{1,0:T(8,128)S(1)}) custom-call(s32[1,64]{1,0:T(1,128)} %counts.3, s32[1,2,6]{2,1,0:T(2,128)} %links.1, f32[3,1,4,32,1024]{4,3,2,1,0:T(8,128)} %fields.3), custom_call_target="tpu_custom_call" | custom-call | flops 1000000 | bytes 2097152 | tf_op jit(solution)/shard_map/pack/pallas_call | solution.py:570
  2.5 3.3 %collective-permute-start = (f32[808,128]{1,0:T(8,128)S(1)}, f32[808,128]{1,0:T(8,128)S(1)}, u32[]{:S(2)}, u32[]{:S(2)}) collective-permute-start(f32[808,128]{1,0:T(8,128)S(1)} %get-tuple-element.14), channel_id=1, source_target_pairs={{0,4},{8,12},{16,20},{24,28},{32,36},{40,44},{48,52},{56,60},{64,6... | collective-permute-start | bytes 1241096 | tf_op jit(solution)/shard_map/ppermute | solution.py:568
  5.8 4.0 %collective-permute-start.1 = (f32[808,128]{1,0:T(8,128)S(1)}, f32[808,128]{1,0:T(8,128)S(1)}, u32[]{:S(2)}, u32[]{:S(2)}) collective-permute-start(f32[808,128]{1,0:T(8,128)S(1)} %get-tuple-element.15._), channel_id=1, source_target_pairs={{4,8},{12,16},{20,24},{28,32},{36,40},{44,48},{52,56},{60,64},{68,... | collective-permute-start | bytes 1241096 | tf_op jit(solution)/shard_map/ppermute | solution.py:568
  9.8 0.0 copy-done.2
  9.8 0.0 copy-done
  9.8 0.7 %pack_far.1 = (f32[80,128]{1,0:T(8,128)S(1)}, f32[80,128]{1,0:T(8,128)S(1)}) custom-call(s32[1,64]{1,0:T(1,128)S(1)} %copy-done.2, f32[3,1,4,32,1024]{4,3,2,1,0:T(8,128)S(1)} %copy-done, f32[808,128]{1,0:T(8,128)S(1)} %get-tuple-element.15._), custom_call_target="tpu_custom_call" | custom-call | flops 1000000 | bytes 2097152 | tf_op jit(solution)/shard_map/pack_far/pallas_call | solution.py:585
  10.5 0.0 copy-start.1
  10.5 0.1 collective-permute-start.2
  10.6 3.2 %collective-permute-start.3 = (f32[80,128]{1,0:T(8,128)S(1)}, f32[80,128]{1,0:T(8,128)S(1)}, u32[]{:S(2)}, u32[]{:S(2)}) collective-permute-start(f32[80,128]{1,0:T(8,128)S(1)} %get-tuple-element.17), channel_id=1, source_target_pairs={{8,16},{12,20},{24,32},{28,36},{40,48},{44,52},{56,64},{60,68},{72... | collective-permute-start | bytes 122888 | tf_op jit(solution)/shard_map/ppermute | solution.py:568
  13.9 5.5 %collective-permute-done.2.far_a = f32[80,128]{1,0:T(8,128)S(1)} collective-permute-done((f32[80,128]{1,0:T(8,128)S(1)}, f32[80,128]{1,0:T(8,128)S(1)}, u32[]{:S(2)}, u32[]{:S(2)}) %collective-permute-start.2) | collective-permute-done | bytes 40992 | tf_op jit(solution)/shard_map/ppermute | solution.py:568
  19.4 0.5 %collective-permute-done.3.far_b = f32[80,128]{1,0:T(8,128)S(1)} collective-permute-done((f32[80,128]{1,0:T(8,128)S(1)}, f32[80,128]{1,0:T(8,128)S(1)}, u32[]{:S(2)}, u32[]{:S(2)}) %collective-permute-start.3) | collective-permute-done | bytes 40992 | tf_op jit(solution)/shard_map/ppermute | solution.py:568
  19.8 3.6 %collective-permute-done.near_a = f32[808,128]{1,0:T(8,128)S(1)} collective-permute-done((f32[808,128]{1,0:T(8,128)S(1)}, f32[808,128]{1,0:T(8,128)S(1)}, u32[]{:S(2)}, u32[]{:S(2)}) %collective-permute-start) | collective-permute-done | bytes 413728 | tf_op jit(solution)/shard_map/ppermute | solution.py:568
  23.5 1.4 %collective-permute-done.1.near_b = f32[808,128]{1,0:T(8,128)S(1)} collective-permute-done((f32[808,128]{1,0:T(8,128)S(1)}, f32[808,128]{1,0:T(8,128)S(1)}, u32[]{:S(2)}, u32[]{:S(2)}) %collective-permute-start.1) | collective-permute-done | bytes 413728 | tf_op jit(solution)/shard_map/ppermute | solution.py:568
  24.8 0.0 copy-done.3
  24.8 0.0 copy-done.4
  24.8 3.4 %smooth.1 = (f32[2,8,16,128]{3,2,1,0:T(8,128)S(1)}, f32[2,8,16,128]{3,2,1,0:T(8,128)S(1)}, f32[2,8,16,128]{3,2,1,0:T(8,128)S(1)}, f32[2,8,16,128]{3,2,1,0:T(8,128)S(1)}, f32[40,256]{1,0:T(8,128)S(1)}) custom-call(s32[1,64]{1,0:T(1,128)S(1)} %copy-done.2, s32[1,2,6]{2,1,0:T(2,128)S(1)} %copy-done.3, s32[1,2,3]{2,1,0:T(2,128)S(1)} %copy-done.4, ...), custom_call_target="tpu_custom_call" | custom-call | flops 10000000 | bytes 6291456 | tf_op jit(solution)/shard_map/smooth/pallas_call | solution.py:603
  28.3 0.1 collective-permute-start.6
  28.4 1.1 %collective-permute-start.5 = (f32[40,256]{1,0:T(8,128)S(1)}, f32[40,256]{1,0:T(8,128)S(1)}, u32[]{:S(2)}, u32[]{:S(2)}) collective-permute-start(f32[40,256]{1,0:T(8,128)S(1)} %get-tuple-element.24.refs_0_), channel_id=1, source_target_pairs={{0,2},{1,3},{2,0},{3,1},{4,6},{5,7},{6,4},{7,5},{8,10},{9,11},{10,... | collective-permute-start | bytes 122888 | tf_op jit(solution)/shard_map/ppermute | solution.py:615
  29.5 0.1 collective-permute-start.4
  29.6 0.8 %unpack.1 = (f32[1,2,32,1024]{3,2,1,0:T(8,128)}, f32[1,2,32,1024]{3,2,1,0:T(8,128)}) custom-call(f32[2,8,16,128]{3,2,1,0:T(8,128)S(1)} %get-tuple-element.18.red, f32[2,8,16,128]{3,2,1,0:T(8,128)S(1)} %get-tuple-element.19.black, f32[2,8,16,128]{3,2,1,0:T(8,128)S(1)} %get-tuple-element.20.red_left, f32[2,8,16,128]{3,2,1,0:T(8,128)S(1)} %get-tuple-element.21.black_left), custom_call_target="tpu_custom_call" | custom-call | flops 1000000 | bytes 3145728 | tf_op jit(solution)/shard_map/unpack/pallas_call | solution.py:618
  30.5 0.0 collective-permute-done.6.refs_3_
  30.5 2.1 %collective-permute-done.5.refs_2_ = f32[40,256]{1,0:T(8,128)S(1)} collective-permute-done((f32[40,256]{1,0:T(8,128)S(1)}, f32[40,256]{1,0:T(8,128)S(1)}, u32[]{:S(2)}, u32[]{:S(2)}) %collective-permute-start.5) | collective-permute-done | bytes 40992 | tf_op jit(solution)/shard_map/ppermute | solution.py:615
  32.6 0.3 %collective-permute-done.4.refs_1_ = f32[40,256]{1,0:T(8,128)S(1)} collective-permute-done((f32[40,256]{1,0:T(8,128)S(1)}, f32[40,256]{1,0:T(8,128)S(1)}, u32[]{:S(2)}, u32[]{:S(2)}) %collective-permute-start.4) | collective-permute-done | bytes 40992 | tf_op jit(solution)/shard_map/ppermute | solution.py:615
  32.9 0.0 copy-done.1
  32.9 0.8 %place.1 = f32[1,2,8,16,256]{4,3,2,1,0:T(8,128)} custom-call(f32[40,256]{1,0:T(8,128)S(1)} %get-tuple-element.24.refs_0_, f32[40,256]{1,0:T(8,128)S(1)} %collective-permute-done.4.refs_1_, f32[40,256]{1,0:T(8,128)S(1)} %collective-permute-done.5.refs_2_, f32[40,256]{1,0:T(8,128)S(1)} %collective-permute-done.6.refs_3_, f32[1,2,8,16,256]{4,3,2,1,0:T(8,128)S(1)} %copy-done.1), custom_call_target="tpu_custom_call" | custom-call | flops 1000000 | bytes 1048576 | tf_op jit(solution)/shard_map/place/pallas_call | solution.py:628
Async XLA Ops:
  0.6 9.1 %copy-start.2 = (s32[1,64]{1,0:T(1,128)S(1)}, s32[1,64]{1,0:T(1,128)}, u32[]{:S(2)}) copy-start(s32[1,64]{1,0:T(1,128)} %counts.3) | copy-start | bytes 772
  0.6 9.1 %copy-start = (f32[3,1,4,32,1024]{4,3,2,1,0:T(8,128)S(1)}, f32[3,1,4,32,1024]{4,3,2,1,0:T(8,128)}, u32[]{:S(2)}) copy-start(f32[3,1,4,32,1024]{4,3,2,1,0:T(8,128)} %fields.3) | copy-start | bytes 4718596
  0.7 24.2 %copy-start.3 = (s32[1,2,6]{2,1,0:T(2,128)S(1)}, s32[1,2,6]{2,1,0:T(2,128)}, u32[]{:S(2)}) copy-start(s32[1,2,6]{2,1,0:T(2,128)} %links.1) | copy-start | bytes 148
  0.7 24.2 %copy-start.4 = (s32[1,2,3]{2,1,0:T(2,128)S(1)}, s32[1,2,3]{2,1,0:T(2,128)}, u32[]{:S(2)}) copy-start(s32[1,2,3]{2,1,0:T(2,128)} %parents.1) | copy-start | bytes 76
  2.5 21.0 %collective-permute-start = (f32[808,128]{1,0:T(8,128)S(1)}, f32[808,128]{1,0:T(8,128)S(1)}, u32[]{:S(2)}, u32[]{:S(2)}) collective-permute-start(f32[808,128]{1,0:T(8,128)S(1)} %get-tuple-element.14), channel_id=1, source_target_pairs={{0,4},{8,12},{16,20},{24,28},{32,36},{40,44},{48,52},{56,60},{64,6... | collective-permute-start | bytes 1241096 | tf_op jit(solution)/shard_map/ppermute | solution.py:568
  5.8 19.1 %collective-permute-start.1 = (f32[808,128]{1,0:T(8,128)S(1)}, f32[808,128]{1,0:T(8,128)S(1)}, u32[]{:S(2)}, u32[]{:S(2)}) collective-permute-start(f32[808,128]{1,0:T(8,128)S(1)} %get-tuple-element.15._), channel_id=1, source_target_pairs={{4,8},{12,16},{20,24},{28,32},{36,40},{44,48},{52,56},{60,64},{68,... | collective-permute-start | bytes 1241096 | tf_op jit(solution)/shard_map/ppermute | solution.py:568
  10.5 22.4 %copy-start.1 = (f32[1,2,8,16,256]{4,3,2,1,0:T(8,128)S(1)}, f32[1,2,8,16,256]{4,3,2,1,0:T(8,128)}, u32[]{:S(2)}) copy-start(f32[1,2,8,16,256]{4,3,2,1,0:T(8,128)} %refs_4_.1) | copy-start | bytes 786436
  10.5 8.8 %collective-permute-start.2 = (f32[80,128]{1,0:T(8,128)S(1)}, f32[80,128]{1,0:T(8,128)S(1)}, u32[]{:S(2)}, u32[]{:S(2)}) collective-permute-start(f32[80,128]{1,0:T(8,128)S(1)} %get-tuple-element.16), channel_id=1, source_target_pairs={{0,8},{4,12},{16,24},{20,28},{32,40},{36,44},{48,56},{52,60},{64,7... | collective-permute-start | bytes 122888 | tf_op jit(solution)/shard_map/ppermute | solution.py:568
  10.6 9.2 %collective-permute-start.3 = (f32[80,128]{1,0:T(8,128)S(1)}, f32[80,128]{1,0:T(8,128)S(1)}, u32[]{:S(2)}, u32[]{:S(2)}) collective-permute-start(f32[80,128]{1,0:T(8,128)S(1)} %get-tuple-element.17), channel_id=1, source_target_pairs={{8,16},{12,20},{24,32},{28,36},{40,48},{44,52},{56,64},{60,68},{72... | collective-permute-start | bytes 122888 | tf_op jit(solution)/shard_map/ppermute | solution.py:568
  28.3 2.2 %collective-permute-start.6 = (f32[40,256]{1,0:T(8,128)S(1)}, f32[40,256]{1,0:T(8,128)S(1)}, u32[]{:S(2)}, u32[]{:S(2)}) collective-permute-start(f32[40,256]{1,0:T(8,128)S(1)} %get-tuple-element.24.refs_0_), channel_id=1, source_target_pairs={{0,3},{1,0},{2,1},{3,2},{4,7},{5,4},{6,5},{7,6},{8,11},{9,8},{10,9... | collective-permute-start | bytes 122888 | tf_op jit(solution)/shard_map/ppermute | solution.py:615
  28.4 4.2 %collective-permute-start.5 = (f32[40,256]{1,0:T(8,128)S(1)}, f32[40,256]{1,0:T(8,128)S(1)}, u32[]{:S(2)}, u32[]{:S(2)}) collective-permute-start(f32[40,256]{1,0:T(8,128)S(1)} %get-tuple-element.24.refs_0_), channel_id=1, source_target_pairs={{0,2},{1,3},{2,0},{3,1},{4,6},{5,7},{6,4},{7,5},{8,10},{9,11},{10,... | collective-permute-start | bytes 122888 | tf_op jit(solution)/shard_map/ppermute | solution.py:615
  29.5 3.4 %collective-permute-start.4 = (f32[40,256]{1,0:T(8,128)S(1)}, f32[40,256]{1,0:T(8,128)S(1)}, u32[]{:S(2)}, u32[]{:S(2)}) collective-permute-start(f32[40,256]{1,0:T(8,128)S(1)} %get-tuple-element.24.refs_0_), channel_id=1, source_target_pairs={{0,1},{1,2},{2,3},{3,0},{4,5},{5,6},{6,7},{7,4},{8,9},{9,10},{10,1... | collective-permute-start | bytes 122888 | tf_op jit(solution)/shard_map/ppermute | solution.py:615

commit v10 on v9

--- a/solution.py
+++ b/solution.py
@@ -485,7 +485,8 @@
             update(colour, 3, take)
         return carry
 
-    lax.fori_loop(0, 2, sweep, 0)
+    for step in range(2):
+        sweep(step, 0)
 
     halves = TILES // 2
     for colour, out, left in ((0, red_out, red_left), (1, black_out, black_left)):

time: 33.9 us -> 33.7 us (level)
  no operation moved by 1% of the time
where the time goes in v10:
time: 33.7 us; the launch traced here: 33.5 us
  waiting for transfers between devices  13.4 us (40%)
  starting transfers between devices  11.9 us (35%)
  Pallas kernels  7.43 us (22%)
  between operations  0.75 us (2%)
    ppermute x4, waiting for transfers between devices, swap(): return lax.ppermute(message, 'box', both)  11 us
    ppermute x4, starting transfers between devices, swap(): return lax.ppermute(message, 'box', both)  10.6 us
    pallas_call x1, Pallas kernels, per_device(): pl.pallas_call(smooth_kernel, out_shape=(half, half, half, half, jax.Shap...  3.22 us
    ppermute x3, waiting for transfers between devices, per_device(): lax.ppermute(coarse, 'grp', [(i, (i + k) % groups) for i in range(groups)])  2.45 us
    pallas_call x1, Pallas kernels, per_device(): pl.pallas_call(pack_kernel, out_shape=(rows(NEAR_ROWS),) * 2, in_specs=[H...  1.81 us
    ppermute x3, starting transfers between devices, per_device(): lax.ppermute(coarse, 'grp', [(i, (i + k) % groups) for i in range(groups)])  1.31 us
    pallas_call x1, Pallas kernels, per_device(): pl.pallas_call(unpack_kernel, out_shape=(fine, fine), in_specs=[VMEM] * 4...  0.84 us
    pallas_call x1, Pallas kernels, per_device(): pl.pallas_call(place_kernel, out_shape=jax.ShapeDtypeStruct(coarse_source...  0.82 us
  transfers between devices with their start and end apart: 7, of which 6 were waited for; matrix products, arithmetic and copies ran while one was open for 0% of the time, Pallas kernels for 5%

profile of v10, /device:TPU:128, one launch (start us, length us, event | category | flops | bytes accessed | tf_op | source)
XLA Modules:
  0.0 33.5 jit_solution(18325129590033960228)
XLA Ops:
  0.6 0.0 copy-start.2
  0.6 0.0 copy-start
  0.7 0.0 copy-start.3
  0.7 0.0 copy-start.4
  0.7 1.8 %pack.1 = (f32[808,128]{1,0:T(8,128)S(1)}, f32[808,128]{1,0:T(8,128)S(1)}) custom-call(s32[1,64]{1,0:T(1,128)} %counts.3, s32[1,2,6]{2,1,0:T(2,128)} %links.1, f32[3,1,4,32,1024]{4,3,2,1,0:T(8,128)} %fields.3), custom_call_target="tpu_custom_call" | custom-call | flops 1000000 | bytes 2097152 | tf_op jit(solution)/shard_map/pack/pallas_call | solution.py:571
  2.5 3.3 %collective-permute-start = (f32[808,128]{1,0:T(8,128)S(1)}, f32[808,128]{1,0:T(8,128)S(1)}, u32[]{:S(2)}, u32[]{:S(2)}) collective-permute-start(f32[808,128]{1,0:T(8,128)S(1)} %get-tuple-element.14), channel_id=1, source_target_pairs={{0,4},{8,12},{16,20},{24,28},{32,36},{40,44},{48,52},{56,60},{64,6... | collective-permute-start | bytes 1241096 | tf_op jit(solution)/shard_map/ppermute | solution.py:569
  5.8 4.0 %collective-permute-start.1 = (f32[808,128]{1,0:T(8,128)S(1)}, f32[808,128]{1,0:T(8,128)S(1)}, u32[]{:S(2)}, u32[]{:S(2)}) collective-permute-start(f32[808,128]{1,0:T(8,128)S(1)} %get-tuple-element.15._), channel_id=1, source_target_pairs={{4,8},{12,16},{20,24},{28,32},{36,40},{44,48},{52,56},{60,64},{68,... | collective-permute-start | bytes 1241096 | tf_op jit(solution)/shard_map/ppermute | solution.py:569
  9.8 0.0 copy-done.2
  9.8 0.0 copy-done
  9.8 0.7 %pack_far.1 = (f32[80,128]{1,0:T(8,128)S(1)}, f32[80,128]{1,0:T(8,128)S(1)}) custom-call(s32[1,64]{1,0:T(1,128)S(1)} %copy-done.2, f32[3,1,4,32,1024]{4,3,2,1,0:T(8,128)S(1)} %copy-done, f32[808,128]{1,0:T(8,128)S(1)} %get-tuple-element.15._), custom_call_target="tpu_custom_call" | custom-call | flops 1000000 | bytes 2097152 | tf_op jit(solution)/shard_map/pack_far/pallas_call | solution.py:586
  10.5 0.0 copy-start.1
  10.5 0.1 collective-permute-start.2
  10.6 3.2 %collective-permute-start.3 = (f32[80,128]{1,0:T(8,128)S(1)}, f32[80,128]{1,0:T(8,128)S(1)}, u32[]{:S(2)}, u32[]{:S(2)}) collective-permute-start(f32[80,128]{1,0:T(8,128)S(1)} %get-tuple-element.17), channel_id=1, source_target_pairs={{8,16},{12,20},{24,32},{28,36},{40,48},{44,52},{56,64},{60,68},{72... | collective-permute-start | bytes 122888 | tf_op jit(solution)/shard_map/ppermute | solution.py:569
  13.9 5.5 %collective-permute-done.2.far_a = f32[80,128]{1,0:T(8,128)S(1)} collective-permute-done((f32[80,128]{1,0:T(8,128)S(1)}, f32[80,128]{1,0:T(8,128)S(1)}, u32[]{:S(2)}, u32[]{:S(2)}) %collective-permute-start.2) | collective-permute-done | bytes 40992 | tf_op jit(solution)/shard_map/ppermute | solution.py:569
  19.4 0.5 %collective-permute-done.3.far_b = f32[80,128]{1,0:T(8,128)S(1)} collective-permute-done((f32[80,128]{1,0:T(8,128)S(1)}, f32[80,128]{1,0:T(8,128)S(1)}, u32[]{:S(2)}, u32[]{:S(2)}) %collective-permute-start.3) | collective-permute-done | bytes 40992 | tf_op jit(solution)/shard_map/ppermute | solution.py:569
  19.8 3.6 %collective-permute-done.near_a = f32[808,128]{1,0:T(8,128)S(1)} collective-permute-done((f32[808,128]{1,0:T(8,128)S(1)}, f32[808,128]{1,0:T(8,128)S(1)}, u32[]{:S(2)}, u32[]{:S(2)}) %collective-permute-start) | collective-permute-done | bytes 413728 | tf_op jit(solution)/shard_map/ppermute | solution.py:569
  23.5 1.4 %collective-permute-done.1.near_b = f32[808,128]{1,0:T(8,128)S(1)} collective-permute-done((f32[808,128]{1,0:T(8,128)S(1)}, f32[808,128]{1,0:T(8,128)S(1)}, u32[]{:S(2)}, u32[]{:S(2)}) %collective-permute-start.1) | collective-permute-done | bytes 413728 | tf_op jit(solution)/shard_map/ppermute | solution.py:569
  24.8 0.0 copy-done.3
  24.8 0.0 copy-done.4
  24.8 3.2 %smooth.1 = (f32[2,8,16,128]{3,2,1,0:T(8,128)S(1)}, f32[2,8,16,128]{3,2,1,0:T(8,128)S(1)}, f32[2,8,16,128]{3,2,1,0:T(8,128)S(1)}, f32[2,8,16,128]{3,2,1,0:T(8,128)S(1)}, f32[40,256]{1,0:T(8,128)S(1)}) custom-call(s32[1,64]{1,0:T(1,128)S(1)} %copy-done.2, s32[1,2,6]{2,1,0:T(2,128)S(1)} %copy-done.3, s32[1,2,3]{2,1,0:T(2,128)S(1)} %copy-done.4, ...), custom_call_target="tpu_custom_call" | custom-call | flops 10000000 | bytes 6291456 | tf_op jit(solution)/shard_map/smooth/pallas_call | solution.py:604
  28.1 0.1 collective-permute-start.6
  28.2 1.1 %collective-permute-start.5 = (f32[40,256]{1,0:T(8,128)S(1)}, f32[40,256]{1,0:T(8,128)S(1)}, u32[]{:S(2)}, u32[]{:S(2)}) collective-permute-start(f32[40,256]{1,0:T(8,128)S(1)} %get-tuple-element.24.refs_0_), channel_id=1, source_target_pairs={{0,2},{1,3},{2,0},{3,1},{4,6},{5,7},{6,4},{7,5},{8,10},{9,11},{10,... | collective-permute-start | bytes 122888 | tf_op jit(solution)/shard_map/ppermute | solution.py:616
  29.2 0.1 collective-permute-start.4
  29.4 0.8 %unpack.1 = (f32[1,2,32,1024]{3,2,1,0:T(8,128)}, f32[1,2,32,1024]{3,2,1,0:T(8,128)}) custom-call(f32[2,8,16,128]{3,2,1,0:T(8,128)S(1)} %get-tuple-element.18.red, f32[2,8,16,128]{3,2,1,0:T(8,128)S(1)} %get-tuple-element.19.black, f32[2,8,16,128]{3,2,1,0:T(8,128)S(1)} %get-tuple-element.20.red_left, f32[2,8,16,128]{3,2,1,0:T(8,128)S(1)} %get-tuple-element.21.black_left), custom_call_target="tpu_custom_call" | custom-call | flops 1000000 | bytes 3145728 | tf_op jit(solution)/shard_map/unpack/pallas_call | solution.py:619
  30.2 0.0 collective-permute-done.6.refs_3_
  30.2 2.1 %collective-permute-done.5.refs_2_ = f32[40,256]{1,0:T(8,128)S(1)} collective-permute-done((f32[40,256]{1,0:T(8,128)S(1)}, f32[40,256]{1,0:T(8,128)S(1)}, u32[]{:S(2)}, u32[]{:S(2)}) %collective-permute-start.5) | collective-permute-done | bytes 40992 | tf_op jit(solution)/shard_map/ppermute | solution.py:616
  32.4 0.3 %collective-permute-done.4.refs_1_ = f32[40,256]{1,0:T(8,128)S(1)} collective-permute-done((f32[40,256]{1,0:T(8,128)S(1)}, f32[40,256]{1,0:T(8,128)S(1)}, u32[]{:S(2)}, u32[]{:S(2)}) %collective-permute-start.4) | collective-permute-done | bytes 40992 | tf_op jit(solution)/shard_map/ppermute | solution.py:616
  32.7 0.0 copy-done.1
  32.7 0.8 %place.1 = f32[1,2,8,16,256]{4,3,2,1,0:T(8,128)} custom-call(f32[40,256]{1,0:T(8,128)S(1)} %get-tuple-element.24.refs_0_, f32[40,256]{1,0:T(8,128)S(1)} %collective-permute-done.4.refs_1_, f32[40,256]{1,0:T(8,128)S(1)} %collective-permute-done.5.refs_2_, f32[40,256]{1,0:T(8,128)S(1)} %collective-permute-done.6.refs_3_, f32[1,2,8,16,256]{4,3,2,1,0:T(8,128)S(1)} %copy-done.1), custom_call_target="tpu_custom_call" | custom-call | flops 1000000 | bytes 1048576 | tf_op jit(solution)/shard_map/place/pallas_call | solution.py:629
Async XLA Ops:
  0.6 9.1 %copy-start.2 = (s32[1,64]{1,0:T(1,128)S(1)}, s32[1,64]{1,0:T(1,128)}, u32[]{:S(2)}) copy-start(s32[1,64]{1,0:T(1,128)} %counts.3) | copy-start | bytes 772
  0.6 9.1 %copy-start = (f32[3,1,4,32,1024]{4,3,2,1,0:T(8,128)S(1)}, f32[3,1,4,32,1024]{4,3,2,1,0:T(8,128)}, u32[]{:S(2)}) copy-start(f32[3,1,4,32,1024]{4,3,2,1,0:T(8,128)} %fields.3) | copy-start | bytes 4718596
  0.7 24.2 %copy-start.3 = (s32[1,2,6]{2,1,0:T(2,128)S(1)}, s32[1,2,6]{2,1,0:T(2,128)}, u32[]{:S(2)}) copy-start(s32[1,2,6]{2,1,0:T(2,128)} %links.1) | copy-start | bytes 148
  0.7 24.2 %copy-start.4 = (s32[1,2,3]{2,1,0:T(2,128)S(1)}, s32[1,2,3]{2,1,0:T(2,128)}, u32[]{:S(2)}) copy-start(s32[1,2,3]{2,1,0:T(2,128)} %parents.1) | copy-start | bytes 76
  2.5 21.0 %collective-permute-start = (f32[808,128]{1,0:T(8,128)S(1)}, f32[808,128]{1,0:T(8,128)S(1)}, u32[]{:S(2)}, u32[]{:S(2)}) collective-permute-start(f32[808,128]{1,0:T(8,128)S(1)} %get-tuple-element.14), channel_id=1, source_target_pairs={{0,4},{8,12},{16,20},{24,28},{32,36},{40,44},{48,52},{56,60},{64,6... | collective-permute-start | bytes 1241096 | tf_op jit(solution)/shard_map/ppermute | solution.py:569
  5.8 19.1 %collective-permute-start.1 = (f32[808,128]{1,0:T(8,128)S(1)}, f32[808,128]{1,0:T(8,128)S(1)}, u32[]{:S(2)}, u32[]{:S(2)}) collective-permute-start(f32[808,128]{1,0:T(8,128)S(1)} %get-tuple-element.15._), channel_id=1, source_target_pairs={{4,8},{12,16},{20,24},{28,32},{36,40},{44,48},{52,56},{60,64},{68,... | collective-permute-start | bytes 1241096 | tf_op jit(solution)/shard_map/ppermute | solution.py:569
  10.5 22.2 %copy-start.1 = (f32[1,2,8,16,256]{4,3,2,1,0:T(8,128)S(1)}, f32[1,2,8,16,256]{4,3,2,1,0:T(8,128)}, u32[]{:S(2)}) copy-start(f32[1,2,8,16,256]{4,3,2,1,0:T(8,128)} %refs_4_.1) | copy-start | bytes 786436
  10.5 8.8 %collective-permute-start.2 = (f32[80,128]{1,0:T(8,128)S(1)}, f32[80,128]{1,0:T(8,128)S(1)}, u32[]{:S(2)}, u32[]{:S(2)}) collective-permute-start(f32[80,128]{1,0:T(8,128)S(1)} %get-tuple-element.16), channel_id=1, source_target_pairs={{0,8},{4,12},{16,24},{20,28},{32,40},{36,44},{48,56},{52,60},{64,7... | collective-permute-start | bytes 122888 | tf_op jit(solution)/shard_map/ppermute | solution.py:569
  10.6 9.2 %collective-permute-start.3 = (f32[80,128]{1,0:T(8,128)S(1)}, f32[80,128]{1,0:T(8,128)S(1)}, u32[]{:S(2)}, u32[]{:S(2)}) collective-permute-start(f32[80,128]{1,0:T(8,128)S(1)} %get-tuple-element.17), channel_id=1, source_target_pairs={{8,16},{12,20},{24,32},{28,36},{40,48},{44,52},{56,64},{60,68},{72... | collective-permute-start | bytes 122888 | tf_op jit(solution)/shard_map/ppermute | solution.py:569
  28.1 2.2 %collective-permute-start.6 = (f32[40,256]{1,0:T(8,128)S(1)}, f32[40,256]{1,0:T(8,128)S(1)}, u32[]{:S(2)}, u32[]{:S(2)}) collective-permute-start(f32[40,256]{1,0:T(8,128)S(1)} %get-tuple-element.24.refs_0_), channel_id=1, source_target_pairs={{0,3},{1,0},{2,1},{3,2},{4,7},{5,4},{6,5},{7,6},{8,11},{9,8},{10,9... | collective-permute-start | bytes 122888 | tf_op jit(solution)/shard_map/ppermute | solution.py:616
  28.2 4.2 %collective-permute-start.5 = (f32[40,256]{1,0:T(8,128)S(1)}, f32[40,256]{1,0:T(8,128)S(1)}, u32[]{:S(2)}, u32[]{:S(2)}) collective-permute-start(f32[40,256]{1,0:T(8,128)S(1)} %get-tuple-element.24.refs_0_), channel_id=1, source_target_pairs={{0,2},{1,3},{2,0},{3,1},{4,6},{5,7},{6,4},{7,5},{8,10},{9,11},{10,... | collective-permute-start | bytes 122888 | tf_op jit(solution)/shard_map/ppermute | solution.py:616
  29.2 3.4 %collective-permute-start.4 = (f32[40,256]{1,0:T(8,128)S(1)}, f32[40,256]{1,0:T(8,128)S(1)}, u32[]{:S(2)}, u32[]{:S(2)}) collective-permute-start(f32[40,256]{1,0:T(8,128)S(1)} %get-tuple-element.24.refs_0_), channel_id=1, source_target_pairs={{0,1},{1,2},{2,3},{3,0},{4,5},{5,6},{6,7},{7,4},{8,9},{9,10},{10,1... | collective-permute-start | bytes 122888 | tf_op jit(solution)/shard_map/ppermute | solution.py:616
